TPU v7x, 32 devices: a whole 2x2x4 slice. The times are simulated.
32 devices in a mesh: ctx: 8 (over y, x, core), wt: 4 (over z).
Axes of the slice: x: 2, y: 2, z: 4, core: 2. Of those that a mesh axis runs over, the one named last changes fastest.
Arguments:
- tokens: bfloat16 [4, 1024, 2048], P('wt', 'ctx'), may hold values from -6 to 6
- cotangent: bfloat16 [4, 1024, 2048], P('wt', 'ctx'), may hold values from -6 to 6
- segments: int32 [4, 1024], P('wt'), may hold values from 0 to 7, never falling along the last dimension, each value on 1 to 512 neighbouring positions
- routes: int32 [4, 1024, 8], P('wt', 'ctx'), may hold values from 0 to 31, all different within a row; in each aligned block of 64 rows (0 to 63, 64 to 127, ..., all dimensions but the last counted through in order) at most 20 rows name the same one
- pair_order: int32 [8], replicated, may hold values from 0 to 7, each once
- attn_gain: float32 [2048], replicated, may hold values from 0.25 to 1.75
- ffn_gain: float32 [2048], replicated, may hold values from 0.25 to 1.75
- query_gain: float32 [128], replicated, may hold values from 0.25 to 1.75
- key_gain: float32 [128], replicated, may hold values from 0.25 to 1.75
- w_query: bfloat16 [2048, 4096], P('wt'), may hold values from -0.125 to 0.125
- key_weight: bfloat16 [2048, 512], P('wt'), may hold values from -0.125 to 0.125
- value_weight: bfloat16 [2048, 512], P('wt'), may hold values from -0.125 to 0.125
- w_output: bfloat16 [4096, 2048], P('wt'), may hold values from -0.75 to 0.75
- w_router: bfloat16 [2048, 32], P('wt'), may hold values from -0.0625 to 0.0625
- w_gate: bfloat16 [32, 2048, 768], P(('ctx', 'wt')), may hold values from -0.125 to 0.125
- w_up: bfloat16 [32, 2048, 768], P(('ctx', 'wt')), may hold values from -0.125 to 0.125
- w_down: bfloat16 [32, 768, 2048], P(('ctx', 'wt')), may hold values from -1 to 1
Outputs:
- mixed: bfloat16 [4, 1024, 2048], P('wt', 'ctx')
- loss: float32 [], replicated
- balance: float32 [32], replicated
- tokens_grad: float32 [4, 1024, 2048], P('wt', 'ctx')
- attn_gain_grad: float32 [2048], P('wt')
- ffn_gain_grad: float32 [2048], P('wt')
- query_gain_grad: float32 [128], P('wt')
- key_gain_grad: float32 [128], P('wt')
- w_query_grad: float32 [2048, 4096], P('wt')
- w_key_grad: float32 [2048, 512], P('wt')
- w_value_grad: float32 [2048, 512], P('wt')
- w_output_grad: float32 [4096, 2048], P('wt')
- w_router_grad: float32 [2048, 32], P('wt')
- w_gate_grad: float32 [32, 2048, 768], P(('ctx', 'wt'))
- w_up_grad: float32 [32, 2048, 768], P(('ctx', 'wt'))
- w_down_grad: float32 [32, 768, 2048], P(('ctx', 'wt'))
Inputs may be any that keep to these rules, and one draw needn't show every extreme that they name: `segments`: positions of a sequence run through documents in order; every document has 1 to 512 positions, and one has exactly that many. `routes`: A token's 8 experts differ. In each aligned block of 64 rows (one device holds two) no expert is named by more than 20 rows, a bound that some block reaches. A permutation; index j of ctx holds blocks pair_order[j] and 15 - pair_order[j] of every sequence of its wt index.
All inputs are finite; a program needn't handle non-finite values.
Results may differ from a plain program's by a relative error of at most 0.024.
Values may be sent and summed in bfloat16 or wider, within the bound.
No kernel may reach another device: no remote copies, remote signals or barrier semaphores. Data moves between devices by JAX's collectives and lax.ppermute only.
A program may use at most 320 MiB of HBM per device.

v0:
```python
import jax
import jax.numpy as jnp
from jax import lax
from jax.sharding import PartitionSpec as P

EPSILON = 1e-06
ROPE_BASE = 1000000.0
MASKED = -1e30


def rms_norm(value_vectors, gain_vector):
    return (
        value_vectors
        * lax.rsqrt(jnp.mean(value_vectors * value_vectors, axis=-1, keepdims=True) + EPSILON)
        * gain_vector
    )


def rope_tables(positions, head_width):
    inv_freq = ROPE_BASE ** (-jnp.arange(0, head_width // 2, dtype=jnp.float32) * 2.0 / head_width)
    angle_table = positions.astype(jnp.float32)[:, None] * inv_freq[None, :]
    angle_table = jnp.concatenate([angle_table, angle_table], axis=-1)
    return (jnp.cos(angle_table), jnp.sin(angle_table))


def rotate(value_vectors, cosine_table, sine_lookup):
    half_width = value_vectors.shape[-1] // 2
    turned = jnp.concatenate(
        [-value_vectors[..., half_width:], value_vectors[..., :half_width]], axis=-1
    )
    return value_vectors * cosine_table[:, None, :] + turned * sine_lookup[:, None, :]


def prepare_heads(raw_values, gain_vector, cosine_table, sine_lookup, head_count):
    shaped = raw_values.reshape(raw_values.shape[0], head_count, -1)
    return rotate(rms_norm(shaped, gain_vector), cosine_table, sine_lookup)


def layout_positions(pair_order, half_rows):
    pair_count = pair_order.shape[0]
    offsets = jnp.arange(half_rows, dtype=jnp.int32)
    first_half = pair_order[:, None] * half_rows + offsets[None, :]
    second = (2 * pair_count - 1 - pair_order[:, None]) * half_rows + offsets[None, :]
    return jnp.concatenate([first_half, second], axis=1).reshape(-1)


def low_matmul(left, right):
    return jnp.dot(left, right, preferred_element_type=jnp.float32)


def swiglu(gate_pre, up_pre):
    return jax.nn.silu(gate_pre) * up_pre


def move_slots(slot_array):
    return lax.all_to_all(slot_array, ("ctx", "wt"), split_axis=0, concat_axis=0, tiled=True)


def local(
    tokens,
    cotangent,
    segments,
    routes,
    pair_order,
    attn_gain,
    ffn_gain,
    query_gain,
    key_gain,
    w_query,
    key_weight,
    value_weight,
    w_output,
    w_router,
    w_gate,
    w_up,
    w_down,
):
    ctx_count = lax.axis_size("ctx")
    wt_count = lax.axis_size("wt")
    ctx_place = lax.axis_index("ctx")
    inputs = tokens[0].astype(jnp.float32)
    tok_rows, model_width = inputs.shape
    half_rows = tok_rows // 2
    head_dim = query_gain.shape[0]
    experts = w_router.shape[1]
    top_count = routes.shape[2]
    capacity = max(2, half_rows * top_count * 5 // (4 * experts))
    slot_rows = 2 * capacity
    local_experts = w_gate.shape[0]
    total_tokens = tok_rows * ctx_count * wt_count
    score_scale = head_dim ** (-0.5)
    key_pos = layout_positions(pair_order, half_rows)
    own_pos = lax.dynamic_slice_in_dim(key_pos, ctx_place * tok_rows, tok_rows)
    seq_segments = segments[0]
    key_seg = seq_segments[key_pos]
    own_seg = seq_segments[own_pos]
    allowed = (own_seg[:, None] == key_seg[None, :]) & (key_pos[None, :] <= own_pos[:, None])
    w_query_all, w_key_all, w_value_all, w_output_all, w_router_all = (
        lax.all_gather(w_query, "wt", axis=0, tiled=True),
        lax.all_gather(key_weight, "wt", axis=0, tiled=True),
        lax.all_gather(value_weight, "wt", axis=0, tiled=True),
        lax.all_gather(w_output, "wt", axis=0, tiled=True),
        lax.all_gather(w_router, "wt", axis=0, tiled=True),
    )
    q_heads = w_query_all.shape[1] // head_dim
    kv_heads = w_key_all.shape[1] // head_dim
    group_size = q_heads // kv_heads
    cosine_table, sine_lookup = rope_tables(own_pos, head_dim)
    normed_one, attn_back = jax.vjp(rms_norm, inputs, attn_gain)
    normed_low = normed_one.astype(jnp.bfloat16)
    query_raw = low_matmul(normed_low, w_query_all)
    key_raw = low_matmul(normed_low, w_key_all)
    value_raw = low_matmul(normed_low, w_value_all)

    def prep_query(raw_values, gain_vector):
        return prepare_heads(raw_values, gain_vector, cosine_table, sine_lookup, q_heads)

    def prep_keys(raw_values, gain_vector):
        return prepare_heads(raw_values, gain_vector, cosine_table, sine_lookup, kv_heads)

    query_roped, query_back = jax.vjp(prep_query, query_raw, query_gain)
    key_roped, key_back = jax.vjp(prep_keys, key_raw, key_gain)
    query_reduced = query_roped.astype(jnp.bfloat16).reshape(
        tok_rows, kv_heads, group_size, head_dim
    )
    key_reduced = key_roped.astype(jnp.bfloat16).reshape(tok_rows, kv_heads * head_dim)
    value_low = value_raw.astype(jnp.bfloat16)
    keys_all, values_all = (
        lax.all_gather(key_reduced, "ctx", axis=0, tiled=True),
        lax.all_gather(value_low, "ctx", axis=0, tiled=True),
    )
    seq_len = keys_all.shape[0]
    keys_all = keys_all.reshape(seq_len, kv_heads, head_dim)
    values_all = values_all.reshape(seq_len, kv_heads, head_dim)

    def head_scores(head_index):
        query_part = lax.dynamic_index_in_dim(query_reduced, head_index, 1, keepdims=False)
        key_part = lax.dynamic_index_in_dim(keys_all, head_index, 1, keepdims=False)
        value_part = lax.dynamic_index_in_dim(values_all, head_index, 1, keepdims=False)
        raw_scores = jnp.einsum(
            "tgd,kd->gtk", query_part, key_part, preferred_element_type=jnp.float32
        )
        scores = jnp.where(allowed[None], raw_scores * score_scale, MASKED)
        return (query_part, key_part, value_part, scores)

    def head_forward(head_index):
        query_part, key_part, value_part, scores = head_scores(head_index)
        top_score = jnp.max(scores, axis=-1, keepdims=True)
        exp_scores = jnp.exp(scores - top_score)
        exp_total = jnp.sum(exp_scores, axis=-1, keepdims=True)
        attn_probs = (exp_scores / exp_total).astype(jnp.bfloat16)
        head_out = jnp.einsum(
            "gtk,kd->tgd", attn_probs, value_part, preferred_element_type=jnp.float32
        )
        return (head_out, (top_score + jnp.log(exp_total))[..., 0])

    head_out, head_lse = lax.map(head_forward, jnp.arange(kv_heads, dtype=jnp.int32))
    attn_low = (
        head_out.transpose(1, 0, 2, 3).reshape(tok_rows, q_heads * head_dim).astype(jnp.bfloat16)
    )
    residual = inputs + low_matmul(attn_low, w_output_all)
    normed_two, ffn_back = jax.vjp(rms_norm, residual, ffn_gain)
    normed_two_low = normed_two.astype(jnp.bfloat16)
    logits = low_matmul(normed_two_low, w_router_all)
    local_routes = routes[0]

    def router_fn(logit_values):
        router_probs = jax.nn.softmax(logit_values, axis=-1)
        chosen = jnp.take_along_axis(router_probs, local_routes, axis=1)
        return (chosen / jnp.sum(chosen, axis=1, keepdims=True), router_probs)

    (gate_values, router_probs), router_back = jax.vjp(router_fn, logits)
    route_flat = local_routes.reshape(-1)
    route_hits = (route_flat[:, None] == jnp.arange(experts, dtype=jnp.int32)[None, :]).astype(
        jnp.int32
    )
    counts, prob_sums = lax.psum(
        (jnp.sum(route_hits, axis=0).astype(jnp.float32), jnp.sum(router_probs, axis=0)),
        ("ctx", "wt"),
    )
    shares = counts / (total_tokens * top_count)
    balance = experts * experts * shares * (prob_sums / total_tokens)
    loss_value = jnp.mean(balance)
    halves = route_hits.reshape(2, half_rows * top_count, experts)
    ranks = jnp.sum((jnp.cumsum(halves, axis=1) - halves) * halves, axis=2).reshape(-1)
    half_index = jnp.arange(tok_rows * top_count, dtype=jnp.int32) // (half_rows * top_count)
    slot_index = route_flat * slot_rows + half_index * capacity + ranks
    slot_owner = (
        jnp.full((experts * slot_rows,), tok_rows * top_count, jnp.int32)
        .at[slot_index]
        .set(jnp.arange(tok_rows * top_count, dtype=jnp.int32))
    )
    slot_shape = (experts // local_experts, local_experts, slot_rows, model_width)
    padded = jnp.concatenate([normed_two_low, jnp.zeros((1, model_width), jnp.bfloat16)], axis=0)
    outgoing = padded[slot_owner // top_count].reshape(slot_shape)
    arrived = move_slots(outgoing)
    gate_pre = jnp.einsum("nesd,edf->nesf", arrived, w_gate, preferred_element_type=jnp.float32)
    up_pre = jnp.einsum("nesd,edf->nesf", arrived, w_up, preferred_element_type=jnp.float32)
    hidden_low, swiglu_back = jax.vjp(swiglu, gate_pre, up_pre)
    hidden_low = hidden_low.astype(jnp.bfloat16)
    expert_out = jnp.einsum(
        "nesf,efd->nesd", hidden_low, w_down, preferred_element_type=jnp.float32
    ).astype(jnp.bfloat16)
    returned = move_slots(expert_out).reshape(experts * slot_rows, model_width)
    picked = returned[slot_index].reshape(tok_rows, top_count, model_width)
    mixture = jnp.einsum("tk,tkd->td", gate_values, picked, preferred_element_type=jnp.float32)
    output = (residual + mixture).astype(jnp.bfloat16)
    grad_out = cotangent[0].astype(jnp.float32)
    grad_gates = jnp.einsum("td,tkd->tk", grad_out, picked, preferred_element_type=jnp.float32)
    grad_routed = (
        (gate_values[:, :, None] * grad_out[:, None, :])
        .astype(jnp.bfloat16)
        .reshape(-1, model_width)
    )
    grad_routed = jnp.concatenate([grad_routed, jnp.zeros((1, model_width), jnp.bfloat16)], axis=0)
    grad_arrived = move_slots(grad_routed[slot_owner].reshape(slot_shape))
    grad_hidden = jnp.einsum(
        "nesd,efd->nesf", grad_arrived, w_down, preferred_element_type=jnp.float32
    )
    grad_w_down = jnp.einsum(
        "nesf,nesd->efd", hidden_low, grad_arrived, preferred_element_type=jnp.float32
    )
    grad_gate_pre, grad_up_pre = swiglu_back(grad_hidden)
    gate_grad_low = grad_gate_pre.astype(jnp.bfloat16)
    up_grad_low = grad_up_pre.astype(jnp.bfloat16)
    grad_w_gate = jnp.einsum(
        "nesd,nesf->edf", arrived, gate_grad_low, preferred_element_type=jnp.float32
    )
    grad_w_up = jnp.einsum(
        "nesd,nesf->edf", arrived, up_grad_low, preferred_element_type=jnp.float32
    )
    grad_slots = (
        jnp.einsum("nesf,edf->nesd", gate_grad_low, w_gate, preferred_element_type=jnp.float32)
        + jnp.einsum("nesf,edf->nesd", up_grad_low, w_up, preferred_element_type=jnp.float32)
    ).astype(jnp.bfloat16)
    grad_back = move_slots(grad_slots).reshape(experts * slot_rows, model_width)
    grad_normed_two = jnp.sum(
        grad_back[slot_index].reshape(tok_rows, top_count, model_width).astype(jnp.float32), axis=1
    )
    prob_grad = jnp.broadcast_to(experts * shares / total_tokens, router_probs.shape)
    (grad_logits,) = router_back((grad_gates, prob_grad))
    logits_low = grad_logits.astype(jnp.bfloat16)
    grad_normed_two = grad_normed_two + jnp.einsum(
        "te,de->td", logits_low, w_router_all, preferred_element_type=jnp.float32
    )
    grad_residual_part, grad_ffn_gain = ffn_back(grad_normed_two)
    grad_residual = grad_out + grad_residual_part
    grad_attn_low = grad_residual.astype(jnp.bfloat16)
    grad_heads = jnp.einsum(
        "td,cd->tc", grad_attn_low, w_output_all, preferred_element_type=jnp.float32
    )
    grad_heads_low = grad_heads.astype(jnp.bfloat16).reshape(
        tok_rows, kv_heads, group_size, head_dim
    )

    def head_backward(head_index):
        query_part, key_part, value_part, scores = head_scores(head_index)
        attn_probs = jnp.exp(scores - head_lse[head_index][..., None])
        grad_part = lax.dynamic_index_in_dim(grad_heads_low, head_index, 1, keepdims=False)
        grad_probs = jnp.einsum(
            "tgd,kd->gtk", grad_part, value_part, preferred_element_type=jnp.float32
        )
        grad_values = jnp.einsum(
            "gtk,tgd->kd",
            attn_probs.astype(jnp.bfloat16),
            grad_part,
            preferred_element_type=jnp.float32,
        )
        inner = jnp.sum(attn_probs * grad_probs, axis=-1, keepdims=True)
        grad_scores = (attn_probs * (grad_probs - inner) * score_scale).astype(jnp.bfloat16)
        grad_query = jnp.einsum(
            "gtk,kd->tgd", grad_scores, key_part, preferred_element_type=jnp.float32
        )
        grad_keys = jnp.einsum(
            "gtk,tgd->kd", grad_scores, query_part, preferred_element_type=jnp.float32
        )
        return (grad_query, grad_keys, grad_values)

    grad_query, grad_keys, grad_values = lax.map(
        head_backward, jnp.arange(kv_heads, dtype=jnp.int32)
    )
    grad_query = grad_query.transpose(1, 0, 2, 3).reshape(tok_rows, q_heads, head_dim)
    grad_keys = grad_keys.transpose(1, 0, 2).reshape(seq_len, kv_heads * head_dim)
    grad_values = grad_values.transpose(1, 0, 2).reshape(seq_len, kv_heads * head_dim)
    key_grad_own, value_grad_own = (
        lax.psum_scatter(
            grad_keys.astype(jnp.bfloat16), "ctx", scatter_dimension=0, tiled=True
        ).astype(jnp.float32),
        lax.psum_scatter(
            grad_values.astype(jnp.bfloat16), "ctx", scatter_dimension=0, tiled=True
        ).astype(jnp.float32),
    )
    grad_query_raw, grad_query_gain = query_back(grad_query)
    grad_key_raw, grad_key_gain = key_back(key_grad_own.reshape(tok_rows, kv_heads, head_dim))
    query_grad_low = grad_query_raw.astype(jnp.bfloat16)
    key_grad_low = grad_key_raw.astype(jnp.bfloat16)
    value_grad_low = value_grad_own.astype(jnp.bfloat16)
    grad_normed_one = (
        jnp.einsum("te,ce->tc", query_grad_low, w_query_all, preferred_element_type=jnp.float32)
        + jnp.einsum("te,ce->tc", key_grad_low, w_key_all, preferred_element_type=jnp.float32)
        + jnp.einsum("te,ce->tc", value_grad_low, w_value_all, preferred_element_type=jnp.float32)
    )
    grad_inputs_part, grad_attn_gain = attn_back(grad_normed_one)
    grad_inputs = grad_residual + grad_inputs_part
    grad_w_query = jnp.einsum(
        "tc,te->ce", normed_low, query_grad_low, preferred_element_type=jnp.float32
    )
    grad_w_key = jnp.einsum(
        "tc,te->ce", normed_low, key_grad_low, preferred_element_type=jnp.float32
    )
    grad_w_value = jnp.einsum(
        "tc,te->ce", normed_low, value_grad_low, preferred_element_type=jnp.float32
    )
    grad_w_output = jnp.einsum(
        "tc,td->cd", attn_low, grad_attn_low, preferred_element_type=jnp.float32
    )
    grad_w_router = jnp.einsum(
        "td,te->de", normed_two_low, logits_low, preferred_element_type=jnp.float32
    )
    shard_grads = (
        lax.psum_scatter(
            grad_w_query.astype(jnp.bfloat16), "wt", scatter_dimension=0, tiled=True
        ).astype(jnp.float32),
        lax.psum_scatter(
            grad_w_key.astype(jnp.bfloat16), "wt", scatter_dimension=0, tiled=True
        ).astype(jnp.float32),
        lax.psum_scatter(
            grad_w_value.astype(jnp.bfloat16), "wt", scatter_dimension=0, tiled=True
        ).astype(jnp.float32),
        lax.psum_scatter(
            grad_w_output.astype(jnp.bfloat16), "wt", scatter_dimension=0, tiled=True
        ).astype(jnp.float32),
        lax.psum_scatter(
            grad_w_router.astype(jnp.bfloat16), "wt", scatter_dimension=0, tiled=True
        ).astype(jnp.float32),
        lax.psum_scatter(
            grad_attn_gain.astype(jnp.bfloat16), "wt", scatter_dimension=0, tiled=True
        ).astype(jnp.float32),
        lax.psum_scatter(
            grad_ffn_gain.astype(jnp.bfloat16), "wt", scatter_dimension=0, tiled=True
        ).astype(jnp.float32),
        lax.psum_scatter(
            grad_query_gain.astype(jnp.bfloat16), "wt", scatter_dimension=0, tiled=True
        ).astype(jnp.float32),
        lax.psum_scatter(
            grad_key_gain.astype(jnp.bfloat16), "wt", scatter_dimension=0, tiled=True
        ).astype(jnp.float32),
    )
    summed = (
        lax.psum(shard_grads[0].astype(jnp.bfloat16), "ctx").astype(jnp.float32),
        lax.psum(shard_grads[1].astype(jnp.bfloat16), "ctx").astype(jnp.float32),
        lax.psum(shard_grads[2].astype(jnp.bfloat16), "ctx").astype(jnp.float32),
        lax.psum(shard_grads[3].astype(jnp.bfloat16), "ctx").astype(jnp.float32),
        lax.psum(shard_grads[4].astype(jnp.bfloat16), "ctx").astype(jnp.float32),
        lax.psum(shard_grads[5].astype(jnp.bfloat16), "ctx").astype(jnp.float32),
        lax.psum(shard_grads[6].astype(jnp.bfloat16), "ctx").astype(jnp.float32),
        lax.psum(shard_grads[7].astype(jnp.bfloat16), "ctx").astype(jnp.float32),
        lax.psum(shard_grads[8].astype(jnp.bfloat16), "ctx").astype(jnp.float32),
    )
    return (
        output[None],
        loss_value,
        balance,
        grad_inputs[None],
        summed[5],
        summed[6],
        summed[7],
        summed[8],
        summed[0],
        summed[1],
        summed[2],
        summed[3],
        summed[4],
        grad_w_gate,
        grad_w_up,
        grad_w_down,
    )


def solution(mesh):
    in_specs = (
        P("wt", "ctx", None),
        P("wt", "ctx", None),
        P("wt", None),
        P("wt", "ctx", None),
        P(),
        P(),
        P(),
        P(),
        P(),
        P("wt", None),
        P("wt", None),
        P("wt", None),
        P("wt", None),
        P("wt", None),
        P(("ctx", "wt"), None, None),
        P(("ctx", "wt"), None, None),
        P(("ctx", "wt"), None, None),
    )
    out_specs = (
        P("wt", "ctx", None),
        P(),
        P(),
        P("wt", "ctx", None),
        P("wt"),
        P("wt"),
        P("wt"),
        P("wt"),
        P("wt", None),
        P("wt", None),
        P("wt", None),
        P("wt", None),
        P("wt", None),
        P(("ctx", "wt"), None, None),
        P(("ctx", "wt"), None, None),
        P(("ctx", "wt"), None, None),
    )
    return jax.shard_map(local, mesh=mesh, in_specs=in_specs, out_specs=out_specs, check_vma=False)
```

profile of v0, /device:TPU:0, one launch (start us, length us, event | category | flops | bytes accessed | tf_op | source)
XLA Modules:
  0.0 2421.4 jit_solution(16462376311945884841)
XLA Ops:
  11.3 47.0 %all-gather.11.cloned.1.call-done = bf16[2048,512]{1,0:T(8,128)(2,1)} async-done(((bf16[512,512]{1,0:T(8,128)(2,1)}), bf16[2048,512]{1,0:T(8,128)(2,1)}) %all-gather.11.cloned.1.call-update) | async-done | bytes 2097168 | tf_op jit(solution)/shard_map/all_gather | solution.py:100
  66.3 38.2 %all-gather.7.cloned.1.call-done = bf16[2048,512]{1,0:T(8,128)(2,1)} async-done(((bf16[512,512]{1,0:T(8,128)(2,1)}), bf16[2048,512]{1,0:T(8,128)(2,1)}) %all-gather.7.cloned.1.call-update) | async-done | bytes 2097168 | tf_op jit(solution)/shard_map/all_gather | solution.py:101
  126.8 13.8 all_gather.27
  157.5 286.0 %all-gather.15.cloned.1.call-done = bf16[2048,4096]{1,0:T(8,128)(2,1)} async-done(((bf16[512,4096]{1,0:T(8,128)(2,1)}), bf16[2048,4096]{1,0:T(8,128)(2,1)}) %all-gather.15.cloned.1.call-update) | async-done | bytes 16777232 | tf_op jit(solution)/shard_map/all_gather | solution.py:99
  443.4 23.1 copy.94
  480.2 35.6 %while.30 = (s32[]{:T(128)}, bf16[4,128,8,128]{1,3,2,0:T(8,128)(2,1)}, f32[4,8,128]{2,1,0:T(8,128)}, s32[4]{0:T(128)S(1)}, bf16[1024,4,128]{0,2,1:T(8,128)(2,1)}...) while((s32[]{:T(128)}, ...), condition=%wide.region_6.7_spmd.clone.clone, body=%wide.region_3.6_spmd.clone.sunk.clone | while | flops 549846016 | bytes 22849768 | solution.py:157
  515.8 214.1 %all-gather.17.cloned.1.call-done = bf16[4096,2048]{1,0:T(8,128)(2,1)} async-done(((bf16[1024,2048]{1,0:T(8,128)(2,1)}), bf16[4096,2048]{1,0:T(8,128)(2,1)}) %all-gather.17.cloned.1.call-update) | async-done | bytes 16777232 | tf_op jit(solution)/shard_map/all_gather | solution.py:102
  752.4 13.6 gather_fusion.4
  771.4 11.9 gather_fusion.2
  783.4 100.7 %all-to-all-done.2 = bf16[32,1,40,2048]{3,2,1,0:T(8,128)(2,1)} async-done(((bf16[32,1,40,2048]{3,2,1,0:T(8,128)(2,1)}), bf16[32,1,40,2048]{3,2,1,0:T(8,128)(2,1)}, u32[]{:S(2)}, u32[]{:S(2)}) %all-to-all-start.2) | async-done | bytes 5242912 | tf_op jit(solution)/shard_map/all_to_all | solution.py:56
  900.2 104.8 %all-to-all-done = bf16[32,1,40,2048]{3,2,1,0:T(8,128)(2,1)} async-done(((bf16[32,1,40,2048]{3,2,1,0:T(8,128)(2,1)}), bf16[32,1,40,2048]{3,2,1,0:T(8,128)(2,1)}, u32[]{:S(2)}, u32[]{:S(2)}) %all-to-all-start) | async-done | bytes 5242912 | tf_op jit(solution)/shard_map/all_to_all | solution.py:56
  1048.8 107.0 %all-to-all-done.3 = bf16[32,1,40,2048]{3,2,1,0:T(8,128)(2,1)} async-done(((bf16[32,1,40,2048]{3,2,1,0:T(8,128)(2,1)}), bf16[32,1,40,2048]{3,2,1,0:T(8,128)(2,1)}, u32[]{:S(2)}, u32[]{:S(2)}) %all-to-all-start.3) | async-done | bytes 5242912 | tf_op jit(solution)/shard_map/all_to_all | solution.py:56
  1163.9 135.9 %all-reduce.10 = (f32[32]{0:T(128)S(1)}, f32[32]{0:T(128)S(1)}) all-reduce(f32[32]{0:T(128)S(1)} %get-tuple-element.361, f32[32]{0:T(128)S(1)} %convert_element_type.261), channel_id=1, replica_groups=mesh['ctx'=8,'wt'=4] {'ctx','wt'}, use_global_device_ids=true, to_apply=%region_18.19 | all-reduce | flops 64 | bytes 512 | tf_op jit(solution)/shard_map/psum | solution.py:177
  1301.1 12.0 gather_fusion.5
  1318.2 12.0 gather_fusion.3
  1361.0 136.2 %while.31 = (s32[]{:T(128)}, f32[4,128,8,128]{1,3,2,0:T(8,128)}, bf16[4,1024,128]{1,2,0:T(8,128)(2,1)}, bf16[4,1024,128]{1,2,0:T(8,128)(2,1)}, s32[4]{0:T(128)S(...) while((s32[]{:T(128)}, f32[4,128,8,128]{1,3,2,0:T(8,128)}, ...), condition=%wide.region_27.28_spmd.clone.clone, body=%wide.region_25.27_spmd.clone.sunk.clone | while | flops 1369837568 | bytes 67672392 | solution.py:279
  1502.1 34.5 %reduce-scatter.22.cloned.1.call-done = bf16[128,512]{1,0:T(8,128)(2,1)} async-done(((bf16[1024,512]{1,0:T(8,128)(2,1)}), bf16[128,512]{1,0:T(8,128)(2,1)}) %reduce-scatter.22.cloned.1.call-update) | async-done | bytes 131088
  1540.3 36.1 %reduce-scatter.24.cloned.1.call-done = bf16[128,512]{1,0:T(8,128)(2,1)} async-done(((bf16[1024,512]{1,0:T(8,128)(2,1)}), bf16[128,512]{1,0:T(8,128)(2,1)}) %reduce-scatter.24.cloned.1.call-update) | async-done | bytes 131088
  1629.5 39.7 %reduce-scatter.16.cloned.1.call-done = bf16[512,512]{1,0:T(8,128)(2,1)} async-done(((bf16[2048,512]{1,0:T(8,128)(2,1)}), bf16[512,512]{1,0:T(8,128)(2,1)}) %reduce-scatter.16.cloned.1.call-update) | async-done | bytes 524304 | tf_op jit(solution)/shard_map/reduce_scatter | solution.py:327
  1669.2 282.0 %reduce-scatter.12.cloned.1.call-done = bf16[512,4096]{1,0:T(8,128)(2,1)} async-done(((bf16[2048,4096]{1,0:T(8,128)(2,1)}), bf16[512,4096]{1,0:T(8,128)(2,1)}) %reduce-scatter.12.cloned.1.call-update) | async-done | bytes 4194320 | tf_op jit(solution)/shard_map/reduce_scatter | solution.py:321
  1951.2 283.4 %reduce-scatter.18.cloned.1.call-done = bf16[1024,2048]{1,0:T(8,128)(2,1)} async-done(((bf16[4096,2048]{1,0:T(8,128)(2,1)}), bf16[1024,2048]{1,0:T(8,128)(2,1)}) %reduce-scatter.18.cloned.1.call-update) | async-done | bytes 4194320 | tf_op jit(solution)/shard_map/reduce_scatter | solution.py:330
  2244.8 12.7 fusion.206
  2273.3 25.5 %all-reduce.11 = (bf16[512]{0:T(512)(128)(2,1)S(1)}, bf16[512]{0:T(512)(128)(2,1)S(1)}, bf16[32]{0:T(256)(128)(2,1)S(1)}, bf16[32]{0:T(256)(128)(2,1)S(1)}, bf16[512,32]{0,1:T(8,128)(2,1)S(1)}) all-reduce(bf16[512]{0:T(512)(128)(2,1)S(1)} %dynamic-slice.1, ...), channel_id=1, replica_groups=mesh['ctx'=8,'wt'=4] {'ctx'}, use_global_device_ids=true, to_apply=%region_35.36 | all-reduce | flops 17472 | bytes 69888 | tf_op jit(solution)/shard_map/psum | solution.py:355
  2302.9 97.1 %all-reduce.16.cloned.1.call-done = (bf16[512,4096]{1,0:T(8,128)(2,1)}, bf16[512,512]{1,0:T(8,128)(2,1)}, bf16[512,512]{1,0:T(8,128)(2,1)}, bf16[1024,2048]{1,0:T(8,128)(2,1)}) async-done(((bf16[512,4096]{1,0:T(8,128)(2,1)}, bf16[512,512]{1,0:T(8,128)(2,1)}, bf16[512,512]{1,0:T(8,128)(2,1)}, bf16[1024,2048]{1,0:T(8,128)(2,1)}), (bf16[512,4096]{1,0:T(8,128)(2,1)}, bf16[512,512]{1,0:T(8,128)(2,1)}, ...) | async-done | bytes 9437200 | tf_op jit(solution)/shard_map/psum | solution.py:350
  (457 shorter events, 455.3 us)
Async XLA Ops:
  7.2 1005.1 %copy-start = (bf16[1,2048,768]{2,1,0:T(8,128)(2,1)S(1)}, bf16[1,2048,768]{2,1,0:T(8,128)(2,1)}, u32[]{:S(2)}) copy-start(bf16[1,2048,768]{2,1,0:T(8,128)(2,1)} %param.35) | copy-start | bytes 9437188
  7.2 51.1 %all-gather.11.cloned.1.call-start = ((), (), s32[]{:S(2)}) async-start(), calls=%async_computation.13 | async-start | bytes 2621440 | tf_op jit(solution)/shard_map/all_gather | solution.py:100
  8.0 96.6 %all-gather.7.cloned.1.call-start = ((), (), s32[]{:S(2)}) async-start(), calls=%async_computation.11 | async-start | bytes 2621440 | tf_op jit(solution)/shard_map/all_gather | solution.py:101
  8.7 135.3 %all-gather.13.cloned.1.call-start = ((), (), s32[]{:S(2)}) async-start(), calls=%async_computation.14 | async-start | bytes 1179648 | tf_op jit(solution)/shard_map/all_gather | solution.py:129
  10.0 465.6 %copy-start.23 = (f32[128,128]{0,1:T(8,128)}, f32[128,128]{0,1:T(8,128)S(1)}, u32[]{:S(2)}) copy-start(f32[128,128]{0,1:T(8,128)S(1)} %get-tuple-element.382) | copy-start | bytes 196612
  10.0 465.6 %copy-start.27 = (f32[128,128]{0,1:T(8,128)}, f32[128,128]{0,1:T(8,128)S(1)}, u32[]{:S(2)}) copy-start(f32[128,128]{0,1:T(8,128)S(1)} %get-tuple-element.383) | copy-start | bytes 196612
  66.3 89.0 %all-gather.9.cloned.1.call-start = ((), (), s32[]{:S(2)}) async-start(), calls=%async_computation.12 | async-start | bytes 1179648 | tf_op jit(solution)/shard_map/all_gather | solution.py:130
  107.5 335.9 %all-gather.15.cloned.1.call-start = ((), (), s32[]{:S(2)}) async-start(), calls=%async_computation.15 | async-start | bytes 20971520 | tf_op jit(solution)/shard_map/all_gather | solution.py:99
  108.1 621.7 %all-gather.17.cloned.1.call-start = ((), (), s32[]{:S(2)}) async-start(), calls=%async_computation.16 | async-start | bytes 20971520 | tf_op jit(solution)/shard_map/all_gather | solution.py:102
  122.5 344.0 %copy-start.63 = (s32[1024,1]{0,1:T(1,128)}, s32[1024,1]{0,1:T(1,128)S(1)}, u32[]{:S(2)}) copy-start(s32[1024,1]{0,1:T(1,128)S(1)} %compare_select_fusion.1) | copy-start | bytes 12292
  140.6 598.6 %copy-start.29 = (bf16[2048,32]{0,1:T(8,128)(2,1)}, bf16[2048,32]{0,1:T(8,128)(2,1)S(1)}, u32[]{:S(2)}) copy-start(bf16[2048,32]{0,1:T(8,128)(2,1)S(1)} %all_gather.27) | copy-start | bytes 393220
  515.8 222.7 %copy-start.52 = (s32[128]{0:T(128)}, s32[128]{0:T(128)S(1)}, u32[]{:S(2)}) copy-start(s32[128]{0:T(128)S(1)} %get-tuple-element.778) | copy-start | bytes 1540
  765.9 118.1 %all-to-all-start.2 = ((bf16[32,1,40,2048]{3,2,1,0:T(8,128)(2,1)}), bf16[32,1,40,2048]{3,2,1,0:T(8,128)(2,1)}, u32[]{:S(2)}, u32[]{:S(2)}) async-start(bf16[32,1,40,2048]{3,2,1,0:T(8,128)(2,1)} %bitcast.602), calls=%async_computation.2 | async-start | bytes 10485760 | tf_op jit(solution)/shard_map/all_to_all | solution.py:56
  884.1 120.9 %all-to-all-start = ((bf16[32,1,40,2048]{3,2,1,0:T(8,128)(2,1)}), bf16[32,1,40,2048]{3,2,1,0:T(8,128)(2,1)}, u32[]{:S(2)}, u32[]{:S(2)}) async-start(bf16[32,1,40,2048]{3,2,1,0:T(8,128)(2,1)} %bitcast.603), calls=%async_computation | async-start | bytes 10485760 | tf_op jit(solution)/shard_map/all_to_all | solution.py:56
  1034.8 120.9 %all-to-all-start.3 = ((bf16[32,1,40,2048]{3,2,1,0:T(8,128)(2,1)}), bf16[32,1,40,2048]{3,2,1,0:T(8,128)(2,1)}, u32[]{:S(2)}, u32[]{:S(2)}) async-start(bf16[32,1,40,2048]{3,2,1,0:T(8,128)(2,1)} %fusion.84), calls=%async_computation.3 | async-start | bytes 10485760 | tf_op jit(solution)/shard_map/all_to_all | solution.py:56
  1155.8 162.4 %all-to-all-start.1 = ((bf16[32,1,40,2048]{3,2,1,0:T(8,128)(2,1)}), bf16[32,1,40,2048]{3,2,1,0:T(8,128)(2,1)}, u32[]{:S(2)}, u32[]{:S(2)}) async-start(bf16[32,1,40,2048]{3,2,1,0:T(8,128)(2,1)} %convert_bitcast_fusion), calls=%async_computation.1 | async-start | bytes 10485760 | tf_op jit(solution)/shard_map/all_to_all | solution.py:56
  1162.2 374.4 %reduce-scatter.22.cloned.1.call-start = ((), (), s32[]{:S(2)}) async-start(), calls=%async_computation.22 | async-start | bytes 1179648
  1499.6 76.7 %reduce-scatter.24.cloned.1.call-start = ((), (), s32[]{:S(2)}) async-start(), calls=%async_computation.23 | async-start | bytes 1179648
  1502.0 127.5 %reduce-scatter.14.cloned.1.call-start = ((), (), s32[]{:S(2)}) async-start(), calls=%async_computation.18 | async-start | bytes 2621440 | tf_op jit(solution)/shard_map/reduce_scatter | solution.py:324
  1540.2 129.0 %reduce-scatter.16.cloned.1.call-start = ((), (), s32[]{:S(2)}) async-start(), calls=%async_computation.19 | async-start | bytes 2621440 | tf_op jit(solution)/shard_map/reduce_scatter | solution.py:327
  1579.4 371.8 %reduce-scatter.12.cloned.1.call-start = ((), (), s32[]{:S(2)}) async-start(), calls=%async_computation.17 | async-start | bytes 20971520 | tf_op jit(solution)/shard_map/reduce_scatter | solution.py:321
  1594.9 639.6 %reduce-scatter.18.cloned.1.call-start = ((), (), s32[]{:S(2)}) async-start(), calls=%async_computation.20 | async-start | bytes 20971520 | tf_op jit(solution)/shard_map/reduce_scatter | solution.py:330
  1604.7 668.6 %reduce-scatter.20.cloned.1.call-start = ((), (), s32[]{:S(2)}) async-start(), calls=%async_computation.21 | async-start | bytes 163840 | tf_op jit(solution)/shard_map/reduce_scatter | solution.py:333
  1619.0 781.0 %all-reduce.16.cloned.1.call-start = ((), (), s32[]{:S(2)}) async-start(), calls=%async_computation.24 | async-start | bytes 18874368 | tf_op jit(solution)/shard_map/psum | solution.py:350
  (98 other events, 2410.4 us)
Sparse Core Ops, SparseCore 0:
  9.6 48.6 all-gather.10
  59.8 44.6 all-gather.6
  107.0 22.3 all-gather.12
  131.7 23.4 all-gather.8
  156.6 286.7 all-gather.14
  444.9 284.9 all-gather.16
  1499.8 36.7 reduce-scatter.21
  1540.3 35.9 reduce-scatter.23
  1579.2 43.8 reduce-scatter.13
  1625.9 43.1 reduce-scatter.15
  1671.5 279.5 reduce-scatter.11
  1953.5 281.0 reduce-scatter.17
  2237.4 19.9 reduce-scatter.19
  2261.7 138.2 all-reduce.15
where the time goes:
time: 2430 us; the launch traced here: 2420 us
  waiting for transfers between devices  1680 us (69%)
  matrix products  292 us (12%)
  blocking collectives  187 us (8%)
  local copies, waits for them, and re-layouts  137 us (6%)
  other arithmetic  64.5 us (3%)
    all_to_all x4, waiting for transfers between devices, move_slots(): lax.all_to_all(slot_array, ('ctx', 'wt'), split_axis=0, concat_axis=0, ti...  312 us
    all_gather x1, waiting for transfers between devices, local(): lax.all_gather(w_query, 'wt', axis=0, tiled=True)  286 us
    reduce_scatter x1, waiting for transfers between devices, local(): lax.psum_scatter(grad_w_output.astype(jnp.bfloat16), 'wt', scatter_dimens...  283 us
    reduce_scatter x1, waiting for transfers between devices, local(): lax.psum_scatter(grad_w_query.astype(jnp.bfloat16), 'wt', scatter_dimensi...  282 us
    all_gather x1, waiting for transfers between devices, local(): lax.all_gather(w_output, 'wt', axis=0, tiled=True)  214 us
    psum x1, blocking collectives, local(): lax.psum((jnp.sum(route_hits, axis=0).astype(jnp.float32), jnp.sum(router...  136 us
    psum x1, waiting for transfers between devices, local(): lax.psum(shard_grads[0].astype(jnp.bfloat16), 'ctx').astype(jnp.float32)  97.1 us
    unnamed x16, waiting for transfers between devices  73.2 us
  transfers between devices with their start and end apart: 18, of which 14 were waited for; matrix products, arithmetic and copies ran while one was open for 10% of the time, Pallas kernels for 0%

commit v1 on v0

v1 whole, which is shorter than its diff:
```python
import functools

import jax
import jax.numpy as jnp
from jax import lax
from jax.experimental import pallas as pl
from jax.experimental.pallas import tpu as pltpu
from jax.sharding import PartitionSpec as P

EPSILON = 1e-06
ROPE_BASE = 1000000.0
MASKED = -1e30
BF = jnp.bfloat16
F32 = jnp.float32
VMEM_SPEC = pl.BlockSpec(memory_space=pltpu.VMEM)
SMEM_SPEC = pl.BlockSpec(memory_space=pltpu.SMEM)
QUERY_ROWS = 128
KEY_ROWS = 256


def rms_norm(value_vectors, gain_vector):
    return (
        value_vectors
        * lax.rsqrt(jnp.mean(value_vectors * value_vectors, axis=-1, keepdims=True) + EPSILON)
        * gain_vector
    )


def low_matmul(left, right):
    return jnp.dot(left, right, preferred_element_type=F32)


def swiglu(gate_pre, up_pre):
    return jax.nn.silu(gate_pre) * up_pre


def rope_tables(length, head_width):
    inv_freq = ROPE_BASE ** (-jnp.arange(0, head_width // 2, dtype=F32) * 2.0 / head_width)
    angle_table = jnp.arange(length, dtype=F32)[:, None] * inv_freq[None, :]
    cosine, sine = jnp.cos(angle_table), jnp.sin(angle_table)
    return jnp.concatenate([cosine, cosine], 1), jnp.concatenate([-sine, sine], 1)


RELATIVE = (0, 2, 4, 6, 1, 3, 5, 7)


def swap(value, bit):
    count = lax.axis_size("ctx")
    return lax.ppermute(value, "ctx", [(i, i ^ bit) for i in range(count)])


def block_owner(count, me):
    if count == 8:
        return jnp.asarray(RELATIVE, jnp.int32) ^ me
    return jnp.arange(count, dtype=jnp.int32)


def plane_gather(block):
    count = lax.axis_size("ctx")
    if count != 8:
        return lax.all_gather(block, "ctx", axis=0, tiled=False)
    half = block.shape[0] // 2
    via_x = swap(block, 2)
    via_y = swap(block, 4)
    diag_a = swap(via_x[:half], 4)
    diag_b = swap(via_y[half:], 2)
    mine = jnp.concatenate([block, via_x, via_y, diag_a, diag_b], axis=0)
    return jnp.concatenate([mine, swap(mine, 1)], axis=0).reshape((count,) + block.shape)


def plane_scatter(parts):
    count = parts.shape[0]
    if count != 8:
        return lax.psum_scatter(parts, "ctx", scatter_dimension=0, tiled=False).astype(F32)
    half = parts.shape[1] // 2
    kept = parts[:4].astype(F32) + swap(parts[4:], 1).astype(F32)
    diag = kept[3].astype(BF)
    from_y = swap(diag[:half], 4)
    from_x = swap(diag[half:], 2)
    part_x = kept[1].at[:half].add(from_y.astype(F32)).astype(BF)
    part_y = kept[2].at[half:].add(from_x.astype(F32)).astype(BF)
    return kept[0] + swap(part_x, 2).astype(F32) + swap(part_y, 4).astype(F32)


def head_norm(raw, gain):
    scale = lax.rsqrt(jnp.mean(raw * raw, axis=-1, keepdims=True) + EPSILON)
    return raw * scale * gain


def turn(value):
    return pltpu.roll(value, value.shape[-1] // 2, 1)


def tile_mask(seg_col, seg_row, row_start, col_start):
    shape = (seg_col.shape[0], seg_row.shape[1])
    rows = lax.broadcasted_iota(jnp.int32, shape, 0) + row_start
    cols = lax.broadcasted_iota(jnp.int32, shape, 1) + col_start
    return (seg_col == seg_row) & (cols <= rows)


def attend_kernel(
    heads,
    block_ref,
    place_ref,
    first_ref,
    hidden_ref,
    weight_ref,
    query_gain_ref,
    key_gain_ref,
    cosine_ref,
    sine_ref,
    seg_row_ref,
    seg_col_ref,
    query_ref,
    key_ref,
    value_ref,
    raw_ref,
    out_ref,
    score_ref,
):
    count, rows, width = hidden_ref.shape
    half = rows // 2
    dim = query_gain_ref.shape[1]
    scale = dim ** (-0.5)

    def project(pair, carry):
        lhs = hidden_ref[pl.ds(pair * 2, 2)].reshape(2 * rows, width)
        raw = jnp.dot(lhs, weight_ref[...], preferred_element_type=F32)
        for piece in range(4):
            start = pl.multiple_of(block_ref[pair * 4 + piece] * half, half)
            spot = pl.ds(start, half)
            cosine, sine = cosine_ref[spot, :], sine_ref[spot, :]
            part = raw[piece * half : (piece + 1) * half]
            for head in range(heads + 1):
                cols = slice(head * dim, (head + 1) * dim)
                gain = query_gain_ref[...] if head < heads else key_gain_ref[...]
                normed = head_norm(part[:, cols], gain)
                roped = (normed * cosine + turn(normed) * sine).astype(BF)
                if head < heads:
                    query_ref[spot, cols] = roped
                else:
                    key_ref[spot, :] = roped
            raw_ref[spot, :] = part[:, : (heads + 1) * dim]
            value_ref[spot, :] = part[:, (heads + 1) * dim :].astype(BF)
        return carry

    lax.fori_loop(0, count // 2, project, 0)
    seq = key_ref.shape[0]
    stacked = heads * QUERY_ROWS

    def attend(index, carry):
        row_start = pl.multiple_of(index * QUERY_ROWS, QUERY_ROWS)
        row_spot = pl.ds(row_start, QUERY_ROWS)
        query = jnp.concatenate(
            [query_ref[row_spot, h * dim : (h + 1) * dim] for h in range(heads)], axis=0
        )
        seg_col = seg_col_ref[row_spot, :]
        low = first_ref[index] // KEY_ROWS
        high = (row_start + QUERY_ROWS + KEY_ROWS - 1) // KEY_ROWS

        def scores(tile, top):
            start = pl.multiple_of(tile * KEY_ROWS, KEY_ROWS)
            spot = pl.ds(start, KEY_ROWS)
            raw = lax.dot_general(
                query, key_ref[spot, :], (((1,), (1,)), ((), ())), preferred_element_type=F32
            )
            allowed = tile_mask(seg_col, seg_row_ref[:, spot], row_start, start)
            raw = raw.reshape(heads, QUERY_ROWS, KEY_ROWS) * scale
            masked = jnp.where(allowed[None], raw, MASKED).reshape(stacked, KEY_ROWS)
            score_ref[:, spot] = masked
            return jnp.maximum(top, jnp.max(masked, axis=1, keepdims=True))

        top = lax.fori_loop(low, high, scores, jnp.full((stacked, 1), MASKED, F32))

        def gather(tile, state):
            total, acc = state
            start = pl.multiple_of(tile * KEY_ROWS, KEY_ROWS)
            spot = pl.ds(start, KEY_ROWS)
            probs = jnp.exp(score_ref[:, spot] - top)
            total = total + jnp.sum(probs, axis=1, keepdims=True)
            acc = acc + jnp.dot(
                probs.astype(BF), value_ref[spot, :], preferred_element_type=F32
            )
            return total, acc

        total, acc = lax.fori_loop(
            low, high, gather, (jnp.zeros((stacked, 1), F32), jnp.zeros((stacked, dim), F32))
        )
        result = (acc / total).astype(BF)
        for head in range(heads):
            for piece in range(QUERY_ROWS // half):
                spot = place_ref[index * (QUERY_ROWS // half) + piece]
                begin = head * QUERY_ROWS + piece * half
                out_ref[spot, :, head * dim : (head + 1) * dim] = result[begin : begin + half]
        return carry

    lax.fori_loop(0, seq // QUERY_ROWS, attend, 0)


def attend_back_kernel(
    heads,
    place_ref,
    first_ref,
    grad_ref,
    query_ref,
    key_ref,
    value_ref,
    raw_ref,
    query_gain_ref,
    key_gain_ref,
    cosine_ref,
    sine_ref,
    seg_row_ref,
    seg_col_ref,
    out_ref,
    query_gain_grad_ref,
    key_gain_grad_ref,
    score_ref,
    prob_grad_ref,
    key_grad_ref,
    value_grad_ref,
):
    half = grad_ref.shape[1]
    dim = query_gain_ref.shape[1]
    scale = dim ** (-0.5)
    seq = key_ref.shape[0]
    stacked = heads * QUERY_ROWS
    pieces = QUERY_ROWS // half
    key_grad_ref[...] = jnp.zeros_like(key_grad_ref)
    value_grad_ref[...] = jnp.zeros_like(value_grad_ref)
    query_gain_grad_ref[...] = jnp.zeros_like(query_gain_grad_ref)
    key_gain_grad_ref[...] = jnp.zeros_like(key_gain_grad_ref)

    def unrope(grad, raw, gain, cosine, sine):
        norm_scale = lax.rsqrt(jnp.mean(raw * raw, axis=-1, keepdims=True) + EPSILON)
        unit = raw * norm_scale
        grad = grad * cosine + turn(grad * sine)
        gain_grad = jnp.sum(grad * unit, axis=0, keepdims=True)
        grad = grad * gain
        grad = norm_scale * (grad - unit * jnp.mean(grad * unit, axis=-1, keepdims=True))
        return grad, gain_grad

    def back(index, carry):
        row_start = pl.multiple_of(index * QUERY_ROWS, QUERY_ROWS)
        row_spot = pl.ds(row_start, QUERY_ROWS)
        places = [place_ref[index * pieces + piece] for piece in range(pieces)]
        query = jnp.concatenate(
            [query_ref[row_spot, h * dim : (h + 1) * dim] for h in range(heads)], axis=0
        )
        grad = jnp.concatenate(
            [
                grad_ref[place, :, h * dim : (h + 1) * dim]
                for h in range(heads)
                for place in places
            ],
            axis=0,
        )
        seg_col = seg_col_ref[row_spot, :]
        low = first_ref[index] // KEY_ROWS
        high = (row_start + QUERY_ROWS + KEY_ROWS - 1) // KEY_ROWS

        def scores(tile, top):
            start = pl.multiple_of(tile * KEY_ROWS, KEY_ROWS)
            spot = pl.ds(start, KEY_ROWS)
            raw = lax.dot_general(
                query, key_ref[spot, :], (((1,), (1,)), ((), ())), preferred_element_type=F32
            )
            allowed = tile_mask(seg_col, seg_row_ref[:, spot], row_start, start)
            raw = raw.reshape(heads, QUERY_ROWS, KEY_ROWS) * scale
            masked = jnp.where(allowed[None], raw, MASKED).reshape(stacked, KEY_ROWS)
            score_ref[:, spot] = masked
            return jnp.maximum(top, jnp.max(masked, axis=1, keepdims=True))

        top = lax.fori_loop(low, high, scores, jnp.full((stacked, 1), MASKED, F32))

        def probabilities(tile, state):
            total, inner = state
            start = pl.multiple_of(tile * KEY_ROWS, KEY_ROWS)
            spot = pl.ds(start, KEY_ROWS)
            probs = jnp.exp(score_ref[:, spot] - top)
            prob_grad = lax.dot_general(
                grad, value_ref[spot, :], (((1,), (1,)), ((), ())), preferred_element_type=F32
            )
            score_ref[:, spot] = probs
            prob_grad_ref[:, spot] = prob_grad
            total = total + jnp.sum(probs, axis=1, keepdims=True)
            inner = inner + jnp.sum(probs * prob_grad, axis=1, keepdims=True)
            return total, inner

        zero = jnp.zeros((stacked, 1), F32)
        total, inner = lax.fori_loop(low, high, probabilities, (zero, zero))
        share = 1.0 / total
        inner = inner * share

        def gradients(tile, acc):
            start = pl.multiple_of(tile * KEY_ROWS, KEY_ROWS)
            spot = pl.ds(start, KEY_ROWS)
            probs = score_ref[:, spot] * share
            score_grad = (probs * (prob_grad_ref[:, spot] - inner) * scale).astype(BF)
            acc = acc + jnp.dot(score_grad, key_ref[spot, :], preferred_element_type=F32)
            key_grad_ref[spot, :] += lax.dot_general(
                score_grad, query, (((0,), (0,)), ((), ())), preferred_element_type=F32
            )
            value_grad_ref[spot, :] += lax.dot_general(
                probs.astype(BF), grad, (((0,), (0,)), ((), ())), preferred_element_type=F32
            )
            return acc

        acc = lax.fori_loop(low, high, gradients, jnp.zeros((stacked, dim), F32))
        cosine, sine = cosine_ref[row_spot, :], sine_ref[row_spot, :]
        for head in range(heads):
            cols = slice(head * dim, (head + 1) * dim)
            part = acc[head * QUERY_ROWS : (head + 1) * QUERY_ROWS]
            part, gain_grad = unrope(
                part, raw_ref[row_spot, cols], query_gain_ref[...], cosine, sine
            )
            query_gain_grad_ref[...] += gain_grad
            part = part.astype(BF)
            for piece in range(pieces):
                out_ref[places[piece], :, cols] = part[piece * half : (piece + 1) * half]
        return carry

    lax.fori_loop(0, seq // QUERY_ROWS, back, 0)

    def finish(index, carry):
        row_start = pl.multiple_of(index * QUERY_ROWS, QUERY_ROWS)
        row_spot = pl.ds(row_start, QUERY_ROWS)
        key_cols = slice(heads * dim, (heads + 1) * dim)
        value_cols = slice((heads + 1) * dim, (heads + 2) * dim)
        part, gain_grad = unrope(
            key_grad_ref[row_spot, :],
            raw_ref[row_spot, key_cols],
            key_gain_ref[...],
            cosine_ref[row_spot, :],
            sine_ref[row_spot, :],
        )
        key_gain_grad_ref[...] += gain_grad
        part = part.astype(BF)
        value = value_grad_ref[row_spot, :].astype(BF)
        for piece in range(pieces):
            place = place_ref[index * pieces + piece]
            out_ref[place, :, key_cols] = part[piece * half : (piece + 1) * half]
            out_ref[place, :, value_cols] = value[piece * half : (piece + 1) * half]
        return carry

    lax.fori_loop(0, seq // QUERY_ROWS, finish, 0)


def move_slots(slot_array):
    return lax.all_to_all(slot_array, ("ctx", "wt"), split_axis=0, concat_axis=0, tiled=True)


def local(
    tokens,
    cotangent,
    segments,
    routes,
    pair_order,
    attn_gain,
    ffn_gain,
    query_gain,
    key_gain,
    w_query,
    key_weight,
    value_weight,
    w_output,
    w_router,
    w_gate,
    w_up,
    w_down,
):
    ctx_count = lax.axis_size("ctx")
    wt_count = lax.axis_size("wt")
    me = lax.axis_index("ctx")
    plane = lax.axis_index("wt")
    inputs = tokens[0].astype(F32)
    tok_rows, model_width = inputs.shape
    half_rows = tok_rows // 2
    head_dim = query_gain.shape[0]
    experts = w_router.shape[1]
    top_count = routes.shape[2]
    seq_len = segments.shape[1]
    total_tokens = tok_rows * ctx_count * wt_count
    heads = w_query.shape[1] // head_dim // ctx_count
    kv_heads = key_weight.shape[1] // head_dim
    share = ctx_count // kv_heads
    head_cols = heads * head_dim
    group = me // share

    kv_start = group * head_dim
    own_weight = jnp.concatenate(
        [
            lax.dynamic_slice_in_dim(w_query, me * head_cols, head_cols, 1),
            lax.dynamic_slice_in_dim(key_weight, kv_start, head_dim, 1),
            lax.dynamic_slice_in_dim(value_weight, kv_start, head_dim, 1),
        ],
        axis=1,
    )
    weight = lax.all_gather(own_weight, "wt", axis=0, tiled=True)
    own_chunks = ctx_count // wt_count
    piece_rows = head_cols // ctx_count
    out_piece = lax.dynamic_index_in_dim(
        w_output.reshape(own_chunks, ctx_count, piece_rows, model_width), me, 1, keepdims=False
    )
    out_pieces = lax.all_gather(out_piece, "wt", axis=0, tiled=True)
    out_weight = lax.all_to_all(out_pieces, "ctx", 0, 0, tiled=True).reshape(
        head_cols, model_width
    )
    w_router_all = lax.all_gather(w_router, "wt", axis=0, tiled=True)

    owner_pair = pair_order[block_owner(ctx_count, me)]
    blocks = jnp.stack([owner_pair, 2 * ctx_count - 1 - owner_pair], 1).reshape(-1)
    order = jnp.arange(2 * ctx_count, dtype=jnp.int32)
    places = jnp.sum(jnp.where(blocks[:, None] == order[None, :], order[:, None], 0), axis=0)
    places = places.astype(jnp.int32)
    seg = segments[0]
    first = jnp.sum(
        (seg[None, :] < seg[::QUERY_ROWS][:, None]).astype(jnp.int32), axis=1
    ).astype(jnp.int32)
    seg_row, seg_col = seg.reshape(1, seq_len), seg.reshape(seq_len, 1)
    cosine, sine = rope_tables(seq_len, head_dim)
    query_gain_row, key_gain_row = query_gain.reshape(1, -1), key_gain.reshape(1, -1)

    normed_one, attn_back = jax.vjp(rms_norm, inputs, attn_gain)
    hidden_all = plane_gather(normed_one.astype(BF))
    width = head_cols + 2 * head_dim
    stacked = heads * QUERY_ROWS
    query, key, value, raw, attn_low = pl.pallas_call(
        functools.partial(attend_kernel, heads),
        out_shape=(
            jax.ShapeDtypeStruct((seq_len, head_cols), BF),
            jax.ShapeDtypeStruct((seq_len, head_dim), BF),
            jax.ShapeDtypeStruct((seq_len, head_dim), BF),
            jax.ShapeDtypeStruct((seq_len, head_cols + head_dim), F32),
            jax.ShapeDtypeStruct((2 * ctx_count, half_rows, head_cols), BF),
        ),
        in_specs=[SMEM_SPEC] * 3 + [VMEM_SPEC] * 8,
        out_specs=[VMEM_SPEC] * 5,
        scratch_shapes=[pltpu.VMEM((stacked, seq_len), F32)],
        cost_estimate=pl.CostEstimate(
            flops=2 * seq_len * model_width * width + 2 * seq_len * seq_len * head_cols,
            bytes_accessed=16 << 20,
            transcendentals=heads * seq_len * seq_len // 2,
        ),
    )(
        blocks,
        places,
        first,
        hidden_all,
        weight,
        query_gain_row,
        key_gain_row,
        cosine,
        sine,
        seg_row,
        seg_col,
    )
    attn_rows = attn_low.reshape(seq_len, head_cols)
    attn_part = low_matmul(attn_rows, out_weight).astype(BF)
    residual = inputs + plane_scatter(attn_part.reshape(ctx_count, tok_rows, model_width))
    normed_two, ffn_back = jax.vjp(rms_norm, residual, ffn_gain)
    normed_two_low = normed_two.astype(BF)
    grad_out = cotangent[0].astype(F32)
    capacity = max(2, half_rows * top_count * 5 // (4 * experts))
    slot_rows = 2 * capacity
    local_experts = w_gate.shape[0]
    logits = low_matmul(normed_two_low, w_router_all)
    local_routes = routes[0]

    def router_fn(logit_values):
        router_probs = jax.nn.softmax(logit_values, axis=-1)
        chosen = jnp.take_along_axis(router_probs, local_routes, axis=1)
        return (chosen / jnp.sum(chosen, axis=1, keepdims=True), router_probs)

    (gate_values, router_probs), router_back = jax.vjp(router_fn, logits)
    route_flat = local_routes.reshape(-1)
    route_hits = (route_flat[:, None] == jnp.arange(experts, dtype=jnp.int32)[None, :]).astype(
        jnp.int32
    )
    counts, prob_sums = lax.psum(
        (jnp.sum(route_hits, axis=0).astype(jnp.float32), jnp.sum(router_probs, axis=0)),
        ("ctx", "wt"),
    )
    shares = counts / (total_tokens * top_count)
    balance = experts * experts * shares * (prob_sums / total_tokens)
    loss_value = jnp.mean(balance)
    halves = route_hits.reshape(2, half_rows * top_count, experts)
    ranks = jnp.sum((jnp.cumsum(halves, axis=1) - halves) * halves, axis=2).reshape(-1)
    half_index = jnp.arange(tok_rows * top_count, dtype=jnp.int32) // (half_rows * top_count)
    slot_index = route_flat * slot_rows + half_index * capacity + ranks
    slot_owner = (
        jnp.full((experts * slot_rows,), tok_rows * top_count, jnp.int32)
        .at[slot_index]
        .set(jnp.arange(tok_rows * top_count, dtype=jnp.int32))
    )
    slot_shape = (experts // local_experts, local_experts, slot_rows, model_width)
    padded = jnp.concatenate([normed_two_low, jnp.zeros((1, model_width), jnp.bfloat16)], axis=0)
    outgoing = padded[slot_owner // top_count].reshape(slot_shape)
    arrived = move_slots(outgoing)
    gate_pre = jnp.einsum("nesd,edf->nesf", arrived, w_gate, preferred_element_type=jnp.float32)
    up_pre = jnp.einsum("nesd,edf->nesf", arrived, w_up, preferred_element_type=jnp.float32)
    hidden_low, swiglu_back = jax.vjp(swiglu, gate_pre, up_pre)
    hidden_low = hidden_low.astype(jnp.bfloat16)
    expert_out = jnp.einsum(
        "nesf,efd->nesd", hidden_low, w_down, preferred_element_type=jnp.float32
    ).astype(jnp.bfloat16)
    returned = move_slots(expert_out).reshape(experts * slot_rows, model_width)
    picked = returned[slot_index].reshape(tok_rows, top_count, model_width)
    mixture = jnp.einsum("tk,tkd->td", gate_values, picked, preferred_element_type=jnp.float32)
    output = (residual + mixture).astype(jnp.bfloat16)
    grad_gates = jnp.einsum("td,tkd->tk", grad_out, picked, preferred_element_type=jnp.float32)
    grad_routed = (
        (gate_values[:, :, None] * grad_out[:, None, :])
        .astype(jnp.bfloat16)
        .reshape(-1, model_width)
    )
    grad_routed = jnp.concatenate([grad_routed, jnp.zeros((1, model_width), jnp.bfloat16)], axis=0)
    grad_arrived = move_slots(grad_routed[slot_owner].reshape(slot_shape))
    grad_hidden = jnp.einsum(
        "nesd,efd->nesf", grad_arrived, w_down, preferred_element_type=jnp.float32
    )
    grad_w_down = jnp.einsum(
        "nesf,nesd->efd", hidden_low, grad_arrived, preferred_element_type=jnp.float32
    )
    grad_gate_pre, grad_up_pre = swiglu_back(grad_hidden)
    gate_grad_low = grad_gate_pre.astype(jnp.bfloat16)
    up_grad_low = grad_up_pre.astype(jnp.bfloat16)
    grad_w_gate = jnp.einsum(
        "nesd,nesf->edf", arrived, gate_grad_low, preferred_element_type=jnp.float32
    )
    grad_w_up = jnp.einsum(
        "nesd,nesf->edf", arrived, up_grad_low, preferred_element_type=jnp.float32
    )
    grad_slots = (
        jnp.einsum("nesf,edf->nesd", gate_grad_low, w_gate, preferred_element_type=jnp.float32)
        + jnp.einsum("nesf,edf->nesd", up_grad_low, w_up, preferred_element_type=jnp.float32)
    ).astype(jnp.bfloat16)
    grad_back = move_slots(grad_slots).reshape(experts * slot_rows, model_width)
    grad_normed_two = jnp.sum(
        grad_back[slot_index].reshape(tok_rows, top_count, model_width).astype(jnp.float32), axis=1
    )
    prob_grad = jnp.broadcast_to(experts * shares / total_tokens, router_probs.shape)
    (grad_logits,) = router_back((grad_gates, prob_grad))
    logits_low = grad_logits.astype(jnp.bfloat16)
    grad_normed_two = grad_normed_two + jnp.einsum(
        "te,de->td", logits_low, w_router_all, preferred_element_type=jnp.float32
    )
    grad_w_router = jnp.einsum(
        "td,te->de", normed_two_low, logits_low, preferred_element_type=jnp.float32
    )
    grad_residual_part, grad_ffn_gain = ffn_back(grad_normed_two)
    grad_residual = grad_out + grad_residual_part
    grad_attn_all = plane_gather(grad_residual.astype(BF)).reshape(seq_len, model_width)
    grad_heads = lax.dot_general(
        grad_attn_all, out_weight, (((1,), (1,)), ((), ())), preferred_element_type=F32
    ).astype(BF)
    head_grads, grad_query_gain, grad_key_gain = pl.pallas_call(
        functools.partial(attend_back_kernel, heads),
        out_shape=(
            jax.ShapeDtypeStruct((2 * ctx_count, half_rows, width), BF),
            jax.ShapeDtypeStruct((1, head_dim), F32),
            jax.ShapeDtypeStruct((1, head_dim), F32),
        ),
        in_specs=[SMEM_SPEC] * 2 + [VMEM_SPEC] * 11,
        out_specs=[VMEM_SPEC] * 3,
        scratch_shapes=[
            pltpu.VMEM((stacked, seq_len), F32),
            pltpu.VMEM((stacked, seq_len), F32),
            pltpu.VMEM((seq_len, head_dim), F32),
            pltpu.VMEM((seq_len, head_dim), F32),
        ],
        cost_estimate=pl.CostEstimate(
            flops=5 * seq_len * seq_len * head_cols,
            bytes_accessed=12 << 20,
            transcendentals=heads * seq_len * seq_len // 2,
        ),
    )(
        places,
        first,
        grad_heads.reshape(2 * ctx_count, half_rows, head_cols),
        query,
        key,
        value,
        raw,
        query_gain_row,
        key_gain_row,
        cosine,
        sine,
        seg_row,
        seg_col,
    )
    head_grads = head_grads.reshape(seq_len, width)
    hidden_rows = hidden_all.reshape(seq_len, model_width)
    weight_grad = lax.dot_general(
        hidden_rows, head_grads, (((0,), (0,)), ((), ())), preferred_element_type=F32
    ).astype(BF)
    weight_grad = lax.psum_scatter(weight_grad, "wt", scatter_dimension=0, tiled=True)
    weight_grads = lax.all_gather(weight_grad, "ctx", axis=0, tiled=False)
    shard_rows = w_query.shape[0]
    grad_w_query = (
        weight_grads[:, :, :head_cols].transpose(1, 0, 2).reshape(shard_rows, -1).astype(F32)
    )

    def pair_sum(cols):
        cols = cols.astype(F32).reshape(kv_heads, share, shard_rows, head_dim)
        return jnp.sum(cols, axis=1).transpose(1, 0, 2).reshape(shard_rows, -1)

    grad_w_key = pair_sum(weight_grads[:, :, head_cols : head_cols + head_dim])
    grad_w_value = pair_sum(weight_grads[:, :, head_cols + head_dim :])
    out_grad = lax.dot_general(
        attn_rows, grad_attn_all, (((0,), (0,)), ((), ())), preferred_element_type=F32
    ).astype(BF)
    out_grad = lax.all_to_all(
        out_grad.reshape(ctx_count, piece_rows, model_width), "ctx", 0, 0, tiled=True
    )
    out_grad = lax.psum_scatter(out_grad, "wt", scatter_dimension=0, tiled=True)
    out_grads = lax.all_gather(out_grad, "ctx", axis=1, tiled=False)
    grad_w_output = out_grads.reshape(w_output.shape).astype(F32)
    grad_hidden_part = lax.dot_general(
        head_grads, weight, (((1,), (1,)), ((), ())), preferred_element_type=F32
    ).astype(BF)
    grad_normed_one = plane_scatter(grad_hidden_part.reshape(ctx_count, tok_rows, model_width))
    grad_inputs_part, grad_attn_gain = attn_back(grad_normed_one)
    grad_inputs = grad_residual + grad_inputs_part
    small = lax.psum(
        (
            grad_w_router,
            grad_attn_gain,
            grad_ffn_gain,
            grad_query_gain[0],
            grad_key_gain[0],
        ),
        ("ctx", "wt"),
    )
    small = [
        lax.dynamic_slice_in_dim(s, plane * (s.shape[0] // wt_count), s.shape[0] // wt_count, 0)
        for s in small
    ]
    return (
        output[None],
        loss_value,
        balance,
        grad_inputs[None],
        small[1],
        small[2],
        small[3],
        small[4],
        grad_w_query,
        grad_w_key,
        grad_w_value,
        grad_w_output,
        small[0],
        grad_w_gate,
        grad_w_up,
        grad_w_down,
    )


def solution(mesh):
    in_specs = (
        P("wt", "ctx", None),
        P("wt", "ctx", None),
        P("wt", None),
        P("wt", "ctx", None),
        P(),
        P(),
        P(),
        P(),
        P(),
        P("wt", None),
        P("wt", None),
        P("wt", None),
        P("wt", None),
        P("wt", None),
        P(("ctx", "wt"), None, None),
        P(("ctx", "wt"), None, None),
        P(("ctx", "wt"), None, None),
    )
    out_specs = (
        P("wt", "ctx", None),
        P(),
        P(),
        P("wt", "ctx", None),
        P("wt"),
        P("wt"),
        P("wt"),
        P("wt"),
        P("wt", None),
        P("wt", None),
        P("wt", None),
        P("wt", None),
        P("wt", None),
        P(("ctx", "wt"), None, None),
        P(("ctx", "wt"), None, None),
        P(("ctx", "wt"), None, None),
    )
    return jax.shard_map(local, mesh=mesh, in_specs=in_specs, out_specs=out_specs, check_vma=False)
```

time: 2430 us -> 1220 us (0.50)
  waiting for transfers between devices: 1680 us -> 591 us
  matrix products: 292 us -> 111 us
  Pallas kernels: 0 us -> 52.4 us
  blocking collectives: 187 us -> 221 us
  local copies, waits for them, and re-layouts: 137 us -> 107 us
  starting transfers between devices: 23.6 us -> 52.5 us
    reduce_scatter x5 -> x2, waiting for transfers between devices: 605 us -> 47.9 us  [the longest x1 47.9 us: local(): lax.psum_scatter(weight_grad, 'wt', scatter_dimension=0, tiled=True)]
    all_gather x6 -> x4, waiting for transfers between devices: 594 us -> 95.2 us  [the longest x1 50.3 us: local(): weight = lax.all_gather(own_weight, 'wt', axis=0, tiled=True)]
    dot_general x41 -> x6, matrix products: 204 us -> 26.9 us  [the longest x1 7.93 us: local(): lax.dot_general(hidden_rows, head_grads, (((0,), (0,)), ((), ())), prefer...]
    unnamed x16 -> x7, waiting for transfers between devices: 73.2 us -> 0.6 us
    pallas_call x0 -> x2, Pallas kernels: none -> 52.4 us  [the longest x1 30.3 us: local(): pl.pallas_call(functools.partial(attend_back_kernel, heads), out_shape=(j...]
    ppermute x0 -> x20, waiting for transfers between devices: none -> 43.5 us  [swap(): return lax.ppermute(value, 'ctx', [(i, i ^ bit) for i in range(count)])]
    psum x1 -> x2, blocking collectives: 136 us -> 177 us  [local(): lax.psum((jnp.sum(route_hits, axis=0).astype(jnp.float32), jnp.sum(router...]
    all_to_all x0 -> x1, blocking collectives: none -> 29.8 us  [local(): lax.all_to_all(out_grad.reshape(ctx_count, piece_rows, model_width), 'ctx...]
  transfers between devices with their start and end apart: 18 -> 32, of which waited for: 14 -> 19; matrix products, arithmetic and copies ran while one was open for 10% -> 13% of each run, Pallas kernels for 0% -> 4%
where the time goes in v1:
time: 1220 us; the launch traced here: 1210 us
  waiting for transfers between devices  591 us (48%)
  blocking collectives  221 us (18%)
  matrix products  111 us (9%)
  local copies, waits for them, and re-layouts  107 us (9%)
  other arithmetic  55.3 us (5%)
  starting transfers between devices  52.5 us (4%)
  Pallas kernels  52.4 us (4%)
  between operations  17.1 us (1%)
    all_to_all x4, waiting for transfers between devices, move_slots(): lax.all_to_all(slot_array, ('ctx', 'wt'), split_axis=0, concat_axis=0, ti...  312 us
    psum x2, blocking collectives, local(): lax.psum((jnp.sum(route_hits, axis=0).astype(jnp.float32), jnp.sum(router...  177 us
    psum x1, waiting for transfers between devices, local(): lax.psum((grad_w_router, grad_attn_gain, grad_ffn_gain, grad_query_gain[0...  91.4 us
    all_gather x1, waiting for transfers between devices, local(): weight = lax.all_gather(own_weight, 'wt', axis=0, tiled=True)  50.3 us
    reduce_scatter x1, waiting for transfers between devices, local(): lax.psum_scatter(weight_grad, 'wt', scatter_dimension=0, tiled=True)  47.9 us
    ppermute x20, waiting for transfers between devices, swap(): return lax.ppermute(value, 'ctx', [(i, i ^ bit) for i in range(count)])  43.5 us
    pallas_call x1, Pallas kernels, local(): pl.pallas_call(functools.partial(attend_back_kernel, heads), out_shape=(j...  30.3 us
    all_to_all x1, blocking collectives, local(): lax.all_to_all(out_grad.reshape(ctx_count, piece_rows, model_width), 'ctx...  29.8 us
  transfers between devices with their start and end apart: 32, of which 19 were waited for; matrix products, arithmetic and copies ran while one was open for 13% of the time, Pallas kernels for 4%

profile of v1, /device:TPU:0, one launch (start us, length us, event | category | flops | bytes accessed | tf_op | source)
XLA Modules:
  0.0 1207.0 jit_solution(7586665347121557550)
XLA Ops:
  21.5 9.6 collective-permute-done
  40.9 18.0 %all-gather.10.cloned.1.call-done = bf16[8,1,64,2048]{3,2,1,0:T(8,128)(2,1)} async-done(((bf16[2,1,64,2048]{3,2,1,0:T(8,128)(2,1)}), bf16[8,1,64,2048]{3,2,1,0:T(8,128)(2,1)}) %all-gather.10.cloned.1.call-update) | async-done | bytes 2097168 | tf_op jit(solution)/shard_map/all_gather | solution.py:405
  72.9 50.3 %all-gather.8.cloned.1.call-done.weight_ref = bf16[2048,768]{1,0:T(8,128)(2,1)} async-done(((bf16[512,768]{1,0:T(8,128)(2,1)}), bf16[2048,768]{1,0:T(8,128)(2,1)}) %all-gather.8.cloned.1.call-update) | async-done | bytes 3145744 | tf_op jit(solution)/shard_map/all_gather | solution.py:399
  123.3 22.1 %shard_map.297 = (bf16[1024,512]{1,0:T(8,128)(2,1)}, bf16[1024,128]{1,0:T(8,128)(2,1)}, bf16[1024,128]{1,0:T(8,128)(2,1)}, f32[1024,640]{1,0:T(8,128)}, bf16[16,64,512]{2,1,0:T(8,128)(2,1)}) custom-call(s32[16]{0:T(128)} %copy-done.38, s32[16]{0:T(128)} %select_reduce_fusion.place_ref, s32[8]{0:T(128)} %convert_reduce_fusion.4.first_ref, ...), custom_call_target="tpu_custom_call" | custom-call | flops 4294967296 | bytes 16777216 | tf_op jit(solution)/shard_map/pallas_call | solution.py:428
  175.7 13.6 %all_gather.23 = bf16[2048,32]{0,1:T(8,128)(2,1)S(1)} all-gather(bf16[512,32]{0,1:T(8,128)(2,1)S(1)} %copy-done.23), channel_id=1, replica_groups=mesh['ctx'=8,'wt'=4] {'wt'}, dimensions={0}, use_global_device_ids=true | all-gather | bytes 163840 | tf_op jit(solution)/shard_map/all_gather | solution.py:409
  204.3 13.6 %gather_fusion.3 = bf16[1280,2048]{1,0:T(8,128)(2,1)} fusion(bf16[1025,2048]{1,0:T(8,128)(2,1)} %concatenate.43, s32[2048]{0:T(1024)S(1)} %get-tuple-element.186), kind=kCustom, calls=%fused_computation.3 | custom fusion | bytes 10490880 | tf_op jit(solution)/shard_map/gather | solution.py:518
  223.3 11.9 gather_fusion.1
  235.3 100.7 %all-to-all-done.3 = bf16[32,1,40,2048]{3,2,1,0:T(8,128)(2,1)} async-done(((bf16[32,1,40,2048]{3,2,1,0:T(8,128)(2,1)}), bf16[32,1,40,2048]{3,2,1,0:T(8,128)(2,1)}, u32[]{:S(2)}, u32[]{:S(2)}) %all-to-all-start.3) | async-done | bytes 5242912 | tf_op jit(solution)/shard_map/all_to_all | solution.py:350
  342.8 9.7 fusion.4
  352.5 104.8 %all-to-all-done.1 = bf16[32,1,40,2048]{3,2,1,0:T(8,128)(2,1)} async-done(((bf16[32,1,40,2048]{3,2,1,0:T(8,128)(2,1)}), bf16[32,1,40,2048]{3,2,1,0:T(8,128)(2,1)}, u32[]{:S(2)}, u32[]{:S(2)}) %all-to-all-start.1) | async-done | bytes 5242912 | tf_op jit(solution)/shard_map/all_to_all | solution.py:350
  464.6 10.1 fusion.43
  501.0 107.0 %all-to-all-done.4 = bf16[32,1,40,2048]{3,2,1,0:T(8,128)(2,1)} async-done(((bf16[32,1,40,2048]{3,2,1,0:T(8,128)(2,1)}), bf16[32,1,40,2048]{3,2,1,0:T(8,128)(2,1)}, u32[]{:S(2)}, u32[]{:S(2)}) %all-to-all-start.4) | async-done | bytes 5242912 | tf_op jit(solution)/shard_map/all_to_all | solution.py:350
  614.6 137.5 %psum.49 = f32[32]{0:T(128)S(1)} all-reduce(f32[32]{0:T(128)S(1)} %convert_element_type.201), channel_id=1, replica_groups=mesh['ctx'=8,'wt'=4] {'ctx','wt'}, use_global_device_ids=true, to_apply=%region_12.13 | all-reduce | flops 32 | bytes 256 | tf_op jit(solution)/shard_map/psum | solution.py:480
  752.6 12.0 gather_fusion.4
  770.6 12.0 gather_fusion.2
  800.4 9.6 collective-permute-done.10
  825.2 29.8 %all_to_all.30 = bf16[8,64,2048]{2,1,0:T(8,128)(2,1)} all-to-all(bf16[8,64,2048]{2,1,0:T(8,128)(2,1)S(1)} %bitcast.375), channel_id=1, replica_groups=mesh['ctx'=8,'wt'=4] {'ctx'}, dimensions={0} | all-to-all | bytes 4194304 | tf_op jit(solution)/shard_map/all_to_all | solution.py:613
  861.3 30.3 %shard_map.298 = (bf16[16,64,768]{2,1,0:T(8,128)(2,1)}, f32[1,128]{1,0:T(1,128)}, f32[1,128]{1,0:T(1,128)}) custom-call(s32[16]{0:T(128)} %select_reduce_fusion.place_ref, s32[8]{0:T(128)} %convert_reduce_fusion.4.first_ref, bf16[16,64,512]{2,1,0:T(8,128)(2,1)} %bitcast.399, bf16[1024,512]{1,0:T(8,128)(2,1)} %get-tuple-element.73.query_ref, ...), custom_call_target="tpu_custom_call" | custom-call | flops 2684354560 | bytes 12582912 | tf_op jit(solution)/shard_map/pallas_call | solution.py:557
  901.5 10.2 fusion.26
  911.7 47.9 %reduce-scatter.3.cloned.1.call-done = bf16[512,768]{1,0:T(8,128)(2,1)} async-done(((bf16[2048,768]{1,0:T(8,128)(2,1)}), bf16[512,768]{1,0:T(8,128)(2,1)}) %reduce-scatter.3.cloned.1.call-update) | async-done | bytes 786448 | tf_op jit(solution)/shard_map/reduce_scatter | solution.py:597
  966.9 8.8 fusion.29
  1000.1 91.4 %all-reduce.5.cloned.1.call-done = f32[2048,32]{0,1:T(8,128)} async-done(((f32[2048,32]{0,1:T(8,128)}), f32[2048,32]{0,1:T(8,128)}) %all-reduce.5.cloned.1.call-update) | async-done | bytes 262160 | tf_op jit(solution)/shard_map/psum | solution.py:625
  1095.2 39.9 %all-reduce.2 = (f32[32]{0:T(128)S(1)}, f32[2048]{0:T(1024)S(1)}, f32[2048]{0:T(1024)S(1)}, f32[128]{0:T(128)S(1)}, f32[128]{0:T(128)S(1)}) all-reduce(f32[32]{0:T(128)S(1)} %copy-done.31, f32[2048]{0:T(1024)S(1)} %get-tuple-element.114, f32[2048]{0:T(1024)S(1)} %get-tuple-element.116, ...), channel_id=1, replica_groups=mesh['ctx'=8,'wt'=4] {'ctx','wt'}, use_global_device_ids=true, to_apply=%region_14.15 | all-reduce | flops 4384 | bytes 35072 | tf_op jit(solution)/shard_map/psum | solution.py:480
  1150.3 26.9 %all-gather.12.cloned.1.call-done = bf16[4096,768]{1,0:T(8,128)(2,1)} async-done(((bf16[512,768]{1,0:T(8,128)(2,1)}), bf16[4096,768]{1,0:T(8,128)(2,1)}) %all-gather.12.cloned.1.call-update) | async-done | bytes 6291472 | tf_op jit(solution)/shard_map/all_gather | solution.py:598
  (303 shorter events, 262.4 us)
Async XLA Ops:
  7.2 51.6 %all-gather.10.cloned.1.call-start = ((), (), s32[]{:S(2)}) async-start(), calls=%async_computation.12 | async-start | bytes 2621440 | tf_op jit(solution)/shard_map/all_gather | solution.py:405
  9.3 113.9 %all-gather.8.cloned.1.call-start = ((), (), s32[]{:S(2)}) async-start(), calls=%async_computation.8 | async-start | bytes 3932160 | tf_op jit(solution)/shard_map/all_gather | solution.py:399
  16.2 14.9 %collective-permute-start = (bf16[128,2048]{1,0:T(8,128)(2,1)S(1)}, bf16[128,2048]{1,0:T(8,128)(2,1)S(1)}, u32[]{:S(2)}, u32[]{:S(2)}) collective-permute-start(bf16[128,2048]{1,0:T(8,128)(2,1)S(1)} %get-tuple-element.132), channel_id=1, source_target_pairs={{0,8},{4,12},{8,0},{12,4},{16,24},{20,28},{24,16},{28,20},{1,9},{5... | collective-permute-start | bytes 1572872 | tf_op jit(solution)/shard_map/ppermute | solution.py:49
  19.2 13.8 %collective-permute-start.1 = (bf16[128,2048]{1,0:T(8,128)(2,1)S(1)}, bf16[128,2048]{1,0:T(8,128)(2,1)S(1)}, u32[]{:S(2)}, u32[]{:S(2)}) collective-permute-start(bf16[128,2048]{1,0:T(8,128)(2,1)S(1)} %get-tuple-element.132), channel_id=1, source_target_pairs={{0,16},{4,20},{8,24},{12,28},{16,0},{20,4},{24,8},{28,12},{1,17},{... | collective-permute-start | bytes 1572872 | tf_op jit(solution)/shard_map/ppermute | solution.py:49
  40.9 28.9 %collective-permute-start.4 = (bf16[512,2048]{1,0:T(8,128)(2,1)}, bf16[512,2048]{1,0:T(8,128)(2,1)}, u32[]{:S(2)}, u32[]{:S(2)}) collective-permute-start(bf16[512,2048]{1,0:T(8,128)(2,1)} %get-tuple-element.170), channel_id=1, source_target_pairs={{0,4},{4,0},{8,12},{12,8},{16,20},{20,16},{24,28},{28,24},{1,5},{5... | collective-permute-start | bytes 6291464 | tf_op jit(solution)/shard_map/ppermute | solution.py:49
  58.9 86.5 %all-to-all-start = ((bf16[8,64,2048]{2,1,0:T(8,128)(2,1)}), bf16[8,64,2048]{2,1,0:T(8,128)(2,1)}, u32[]{:S(2)}, u32[]{:S(2)}) async-start(bf16[8,64,2048]{2,1,0:T(8,128)(2,1)} %bitcast.374), calls=%async_computation | async-start | bytes 4194304 | tf_op jit(solution)/shard_map/all_to_all | solution.py:406
  163.5 8.8 collective-permute-start.6
  165.0 8.4 collective-permute-start.8
  173.6 16.7 %collective-permute-start.9 = (bf16[128,2048]{1,0:T(8,128)(2,1)S(1)}, bf16[128,2048]{1,0:T(8,128)(2,1)S(1)}, u32[]{:S(2)}, u32[]{:S(2)}) collective-permute-start(bf16[128,2048]{1,0:T(8,128)(2,1)S(1)} %get-tuple-element.145), channel_id=1, source_target_pairs={{0,16},{4,20},{8,24},{12,28},{16,0},{20,4},{24,8},{28,12},{1,17},{... | collective-permute-start | bytes 1572872 | tf_op jit(solution)/shard_map/ppermute | solution.py:49
  174.2 16.1 %collective-permute-start.7 = (bf16[128,2048]{1,0:T(8,128)(2,1)S(1)}, bf16[128,2048]{1,0:T(8,128)(2,1)S(1)}, u32[]{:S(2)}, u32[]{:S(2)}) collective-permute-start(bf16[128,2048]{1,0:T(8,128)(2,1)S(1)} %get-tuple-element.144), channel_id=1, source_target_pairs={{0,8},{4,12},{8,0},{12,4},{16,24},{20,28},{24,16},{28,20},{1,9},{5... | collective-permute-start | bytes 1572872 | tf_op jit(solution)/shard_map/ppermute | solution.py:49
  217.8 118.1 %all-to-all-start.3 = ((bf16[32,1,40,2048]{3,2,1,0:T(8,128)(2,1)}), bf16[32,1,40,2048]{3,2,1,0:T(8,128)(2,1)}, u32[]{:S(2)}, u32[]{:S(2)}) async-start(bf16[32,1,40,2048]{3,2,1,0:T(8,128)(2,1)} %bitcast.362), calls=%async_computation.3 | async-start | bytes 10485760 | tf_op jit(solution)/shard_map/all_to_all | solution.py:350
  336.0 121.3 %all-to-all-start.1 = ((bf16[32,1,40,2048]{3,2,1,0:T(8,128)(2,1)}), bf16[32,1,40,2048]{3,2,1,0:T(8,128)(2,1)}, u32[]{:S(2)}, u32[]{:S(2)}) async-start(bf16[32,1,40,2048]{3,2,1,0:T(8,128)(2,1)} %bitcast.363), calls=%async_computation.1 | async-start | bytes 10485760 | tf_op jit(solution)/shard_map/all_to_all | solution.py:350
  487.1 120.9 %all-to-all-start.4 = ((bf16[32,1,40,2048]{3,2,1,0:T(8,128)(2,1)}), bf16[32,1,40,2048]{3,2,1,0:T(8,128)(2,1)}, u32[]{:S(2)}, u32[]{:S(2)}) async-start(bf16[32,1,40,2048]{3,2,1,0:T(8,128)(2,1)} %fusion.1), calls=%async_computation.4 | async-start | bytes 10485760 | tf_op jit(solution)/shard_map/all_to_all | solution.py:350
  608.0 162.6 %all-to-all-start.2 = ((bf16[32,1,40,2048]{3,2,1,0:T(8,128)(2,1)}), bf16[32,1,40,2048]{3,2,1,0:T(8,128)(2,1)}, u32[]{:S(2)}, u32[]{:S(2)}) async-start(bf16[32,1,40,2048]{3,2,1,0:T(8,128)(2,1)} %convert_bitcast_fusion.1), calls=%async_computation.2 | async-start | bytes 10485760 | tf_op jit(solution)/shard_map/all_to_all | solution.py:350
  614.4 286.1 %reduce-scatter.5.cloned.1.call-start = ((), (), s32[]{:S(2)}) async-start(), calls=%async_computation.10 | async-start | bytes 2621440 | tf_op jit(solution)/shard_map/reduce_scatter | solution.py:616
  796.5 13.5 %collective-permute-start.10 = (bf16[128,2048]{1,0:T(8,128)(2,1)S(1)}, bf16[128,2048]{1,0:T(8,128)(2,1)S(1)}, u32[]{:S(2)}, u32[]{:S(2)}) collective-permute-start(bf16[128,2048]{1,0:T(8,128)(2,1)S(1)} %get-tuple-element.126), channel_id=1, source_target_pairs={{0,8},{4,12},{8,0},{12,4},{16,24},{20,28},{24,16},{28,20},{1,9},{5... | collective-permute-start | bytes 1572872 | tf_op jit(solution)/shard_map/ppermute | solution.py:49
  798.8 13.0 %collective-permute-start.11 = (bf16[128,2048]{1,0:T(8,128)(2,1)S(1)}, bf16[128,2048]{1,0:T(8,128)(2,1)S(1)}, u32[]{:S(2)}, u32[]{:S(2)}) collective-permute-start(bf16[128,2048]{1,0:T(8,128)(2,1)S(1)} %get-tuple-element.126), channel_id=1, source_target_pairs={{0,16},{4,20},{8,24},{12,28},{16,0},{20,4},{24,8},{28,12},{1,17},{... | collective-permute-start | bytes 1572872 | tf_op jit(solution)/shard_map/ppermute | solution.py:49
  855.0 104.6 %reduce-scatter.3.cloned.1.call-start = ((), (), s32[]{:S(2)}) async-start(), calls=%async_computation.9 | async-start | bytes 3932160 | tf_op jit(solution)/shard_map/reduce_scatter | solution.py:597
  899.5 192.0 %all-reduce.5.cloned.1.call-start = ((), (), s32[]{:S(2)}) async-start(), calls=%async_computation.11 | async-start | bytes 524288 | tf_op jit(solution)/shard_map/psum | solution.py:625
  900.5 243.2 %all-gather.14.cloned.1.call-start = ((), (), s32[]{:S(2)}) async-start(), calls=%async_computation.14 | async-start | bytes 4718592 | tf_op jit(solution)/shard_map/all_gather | solution.py:617
  901.1 276.1 %all-gather.12.cloned.1.call-start = ((), (), s32[]{:S(2)}) async-start(), calls=%async_computation.13 | async-start | bytes 7077888 | tf_op jit(solution)/shard_map/all_gather | solution.py:598
  966.0 9.7 collective-permute-start.15
  987.1 105.9 %collective-permute-start.19 = (bf16[128,2048]{1,0:T(8,128)(2,1)}, bf16[128,2048]{1,0:T(8,128)(2,1)}, u32[]{:S(2)}, u32[]{:S(2)}) collective-permute-start(bf16[128,2048]{1,0:T(8,128)(2,1)} %get-tuple-element.137), channel_id=1, source_target_pairs={{0,16},{4,20},{8,24},{12,28},{16,0},{20,4},{24,8},{28,12},{1,17},{... | collective-permute-start | bytes 1572872 | tf_op jit(solution)/shard_map/ppermute | solution.py:49
  987.6 105.4 %collective-permute-start.17 = (bf16[128,2048]{1,0:T(8,128)(2,1)}, bf16[128,2048]{1,0:T(8,128)(2,1)}, u32[]{:S(2)}, u32[]{:S(2)}) collective-permute-start(bf16[128,2048]{1,0:T(8,128)(2,1)} %get-tuple-element.136), channel_id=1, source_target_pairs={{0,8},{4,12},{8,0},{12,4},{16,24},{20,28},{24,16},{28,20},{1,9},{5... | collective-permute-start | bytes 1572872 | tf_op jit(solution)/shard_map/ppermute | solution.py:49
  (59 other events, 2244.6 us)
Sparse Core Ops, SparseCore 0:
  10.2 48.6 all-gather.9
  61.0 62.2 all-gather.7
  855.1 41.9 reduce-scatter.4
  899.9 59.5 reduce-scatter.2
  966.4 125.0 all-reduce.4
  1093.4 36.0 all-gather.13
  1131.5 45.5 all-gather.11

commit v2 on v1

--- a/solution.py
+++ b/solution.py
@@ -16,6 +16,8 @@
 SMEM_SPEC = pl.BlockSpec(memory_space=pltpu.SMEM)
 QUERY_ROWS = 128
 KEY_ROWS = 256
+ATTEND_LIMIT = 40 << 20
+COST = pl.CostEstimate(flops=1, bytes_accessed=1, transcendentals=0)
 
 
 def rms_norm(value_vectors, gain_vector):
@@ -55,31 +57,100 @@
     return jnp.arange(count, dtype=jnp.int32)
 
 
+def after(value, *others):
+    return lax.optimization_barrier((value,) + others)[0]
+
+
+def plane_pieces(block):
+    half = block.shape[0] // 2
+    via_x = swap(block, 2)
+    via_y = swap(block, 4)
+    return [block, via_x, via_y, swap(via_x[:half], 4), swap(via_y[half:], 2)]
+
+
+def plane_sends(block):
+    half = block.shape[0] // 2
+    via_x = swap(block, 2)
+    via_y = swap(block, 4)
+    from_x, from_y = via_x[:half], via_y[half:]
+    return [block, via_x, via_y, swap(from_x, 4), swap(from_y, 2)], (from_x, from_y)
+
+
 def plane_gather(block):
     count = lax.axis_size("ctx")
     if count != 8:
-        return lax.all_gather(block, "ctx", axis=0, tiled=False)
-    half = block.shape[0] // 2
-    via_x = swap(block, 2)
-    via_y = swap(block, 4)
-    diag_a = swap(via_x[:half], 4)
-    diag_b = swap(via_y[half:], 2)
-    mine = jnp.concatenate([block, via_x, via_y, diag_a, diag_b], axis=0)
-    return jnp.concatenate([mine, swap(mine, 1)], axis=0).reshape((count,) + block.shape)
-
-
-def plane_scatter(parts):
-    count = parts.shape[0]
+        return [lax.all_gather(block, "ctx", axis=0, tiled=True)]
+    mine = plane_pieces(block)
+    return mine + [swap(piece, 1) for piece in mine]
+
+
+def diag_sends(diag):
+    half = diag.shape[0] // 2
+    return swap(diag[:half], 4), swap(diag[half:], 2)
+
+
+def add_diag(part_x, part_y, from_y, from_x):
+    half = from_y.shape[0]
+    part_x, part_y = part_x.astype(F32), part_y.astype(F32)
+    part_x = jnp.concatenate([part_x[:half] + from_y.astype(F32), part_x[half:]], 0).astype(BF)
+    part_y = jnp.concatenate([part_y[:half], part_y[half:] + from_x.astype(F32)], 0).astype(BF)
+    return part_x, part_y
+
+
+def plane_sum(own, part_x, part_y, diag):
+    part_x, part_y = add_diag(part_x, part_y, *diag_sends(diag))
+    return own.astype(F32) + swap(part_x, 2).astype(F32) + swap(part_y, 4).astype(F32)
+
+
+def plane_scatter(multiply, left, fill=None, *others):
+    count = lax.axis_size("ctx")
     if count != 8:
-        return lax.psum_scatter(parts, "ctx", scatter_dimension=0, tiled=False).astype(F32)
-    half = parts.shape[1] // 2
-    kept = parts[:4].astype(F32) + swap(parts[4:], 1).astype(F32)
-    diag = kept[3].astype(BF)
-    from_y = swap(diag[:half], 4)
-    from_x = swap(diag[half:], 2)
-    part_x = kept[1].at[:half].add(from_y.astype(F32)).astype(BF)
-    part_y = kept[2].at[half:].add(from_x.astype(F32)).astype(BF)
-    return kept[0] + swap(part_x, 2).astype(F32) + swap(part_y, 4).astype(F32)
+        parts = multiply(left).astype(BF)
+        return lax.psum_scatter(parts, "ctx", scatter_dimension=0, tiled=True).astype(F32)
+    side = left.shape[0] // 2
+    rows = side // 4
+    give = multiply(left[side:]).astype(BF)
+    got = swap(give, 1)
+    keep = multiply(after(left[:side], give))
+    kept = keep + after(got, keep).astype(F32)
+    if others:
+        kept = after(kept, *others)
+    diag = kept[3 * rows :].astype(BF)
+    half = rows // 2
+    sends = diag[:half], diag[half:]
+    from_y, from_x = swap(sends[0], 4), swap(sends[1], 2)
+    if fill is not None:
+        from_y, from_x = after((from_y, from_x), fill(sends))
+    part_x, part_y = add_diag(kept[rows : 2 * rows], kept[2 * rows : 3 * rows], from_y, from_x)
+    return kept[:rows] + swap(part_x, 2).astype(F32) + swap(part_y, 4).astype(F32)
+
+
+def ring(value):
+    count = lax.axis_size("wt")
+    return lax.ppermute(value, "wt", [(i, (i + 1) % count) for i in range(count)])
+
+
+def ring_chunks(block):
+    chunks = [block]
+    for _ in range(lax.axis_size("wt") - 1):
+        chunks.append(ring(chunks[-1]))
+    return chunks
+
+
+def ring_sum(parts, kind):
+    total = parts[1]
+    for part in parts[2:] + parts[:1]:
+        total = ring(total.astype(kind)).astype(F32) + part
+    return total
+
+
+def axis_sum(value, name):
+    count = lax.axis_size(name)
+    bit = 1
+    while bit < count:
+        value = value + lax.ppermute(value, name, [(i, i ^ bit) for i in range(count)])
+        bit *= 2
+    return value
 
 
 def head_norm(raw, gain):
@@ -100,10 +171,33 @@
 
 def attend_kernel(
     heads,
+    pieces,
     block_ref,
     place_ref,
     first_ref,
-    hidden_ref,
+    *refs,
+):
+    attend_body(heads, block_ref, place_ref, first_ref, refs[:pieces], *refs[pieces:])
+
+
+def joined(refs, rows):
+    group, have = [], 0
+    for ref in refs:
+        for start in range(0, ref.shape[0], rows):
+            stop = min(start + rows, ref.shape[0])
+            group.append(ref[start:stop])
+            have += stop - start
+            if have == rows:
+                yield group[0] if len(group) == 1 else jnp.concatenate(group, axis=0)
+                group, have = [], 0
+
+
+def attend_body(
+    heads,
+    block_ref,
+    place_ref,
+    first_ref,
+    hidden_refs,
     weight_ref,
     query_gain_ref,
     key_gain_ref,
@@ -118,13 +212,11 @@
     out_ref,
     score_ref,
 ):
-    count, rows, width = hidden_ref.shape
-    half = rows // 2
+    half = out_ref.shape[1]
     dim = query_gain_ref.shape[1]
     scale = dim ** (-0.5)
 
-    def project(pair, carry):
-        lhs = hidden_ref[pl.ds(pair * 2, 2)].reshape(2 * rows, width)
+    for pair, lhs in enumerate(joined(hidden_refs, 4 * half)):
         raw = jnp.dot(lhs, weight_ref[...], preferred_element_type=F32)
         for piece in range(4):
             start = pl.multiple_of(block_ref[pair * 4 + piece] * half, half)
@@ -142,9 +234,7 @@
                     key_ref[spot, :] = roped
             raw_ref[spot, :] = part[:, : (heads + 1) * dim]
             value_ref[spot, :] = part[:, (heads + 1) * dim :].astype(BF)
-        return carry
-
-    lax.fori_loop(0, count // 2, project, 0)
+
     seq = key_ref.shape[0]
     stacked = heads * QUERY_ROWS
 
@@ -197,11 +287,16 @@
     lax.fori_loop(0, seq // QUERY_ROWS, attend, 0)
 
 
-def attend_back_kernel(
+def attend_back_kernel(heads, pieces, place_ref, first_ref, *refs):
+    attend_back_body(heads, place_ref, first_ref, refs[:pieces], *refs[pieces:])
+
+
+def attend_back_body(
     heads,
     place_ref,
     first_ref,
-    grad_ref,
+    piece_refs,
+    out_weight_ref,
     query_ref,
     key_ref,
     value_ref,
@@ -219,8 +314,17 @@
     prob_grad_ref,
     key_grad_ref,
     value_grad_ref,
+    grad_ref,
 ):
     half = grad_ref.shape[1]
+    spot = 0
+    for part in joined(piece_refs, 4 * half):
+        part = lax.dot_general(
+            part, out_weight_ref[...], (((1,), (1,)), ((), ())), preferred_element_type=F32
+        ).astype(BF)
+        for piece in range(4):
+            grad_ref[spot] = part[piece * half : (piece + 1) * half]
+            spot += 1
     dim = query_gain_ref.shape[1]
     scale = dim ** (-0.5)
     seq = key_ref.shape[0]
@@ -344,6 +448,258 @@
         return carry
 
     lax.fori_loop(0, seq // QUERY_ROWS, finish, 0)
+
+
+def one_hot(hit):
+    return hit.astype(F32).astype(BF)
+
+
+def select_kernel(groups, joint, *refs):
+    target_ref, mine_ref, other_ref = refs[sum(groups) :]
+    slots = mine_ref.shape[0] // 2
+    target = target_ref[...]
+    half = target.shape[1] // 8
+    index = lax.broadcasted_iota(jnp.int32, (2 * slots, target.shape[1]), 0)
+    pick = one_hot((index == target[0:1]) | (index == target[1:2]))
+    for k in range(2):
+        rows = []
+        if joint:
+            for ref in refs[: groups[0]]:
+                for start in range(k * half, ref.shape[0], 2 * half):
+                    rows.append(ref[start : start + half])
+        else:
+            first = k * groups[0]
+            rows = [ref[...] for ref in refs[first : first + groups[k]]]
+        picked = jnp.dot(pick, jnp.concatenate(rows, axis=0), preferred_element_type=F32)
+        picked = picked.astype(BF)
+        mine_ref[k * slots : (k + 1) * slots] = picked[:slots]
+        other_ref[k * slots : (k + 1) * slots] = picked[slots:]
+
+
+def select_rows(pieces, others, target, slots):
+    width = pieces[0].shape[1]
+    return pl.pallas_call(
+        functools.partial(select_kernel, (len(pieces), len(others)), not others),
+        out_shape=(jax.ShapeDtypeStruct((2 * slots, width), BF),) * 2,
+        in_specs=[VMEM_SPEC] * (len(pieces) + len(others) + 1),
+        out_specs=[VMEM_SPEC] * 2,
+        compiler_params=pltpu.CompilerParams(vmem_limit_bytes=24 << 20),
+        cost_estimate=COST,
+    )(*pieces, *others, target)
+
+
+def spread_kernel(chunks, part, *refs):
+    mine_refs, other_refs = refs[:chunks], refs[chunks : 2 * chunks]
+    target_ref, own_ref, x_ref, y_ref, diag_ref = refs[2 * chunks :]
+    slots = mine_refs[0].shape[0] // 2
+    rows = own_ref.shape[0] // chunks
+    spot = slice(part * slots, (part + 1) * slots)
+    for j in range(chunks):
+        values = jnp.concatenate([mine_refs[j][spot], other_refs[j][spot]], axis=0)
+        target = target_ref[j]
+        index = lax.broadcasted_iota(jnp.int32, (4 * rows, 2 * slots), 1)
+        pick = one_hot((index == target[:, 0:1]) | (index == target[:, 1:2]))
+        spread = jnp.dot(pick, values, preferred_element_type=F32).astype(BF)
+        for k, ref in enumerate((own_ref, x_ref, y_ref, diag_ref)):
+            ref[j * rows : (j + 1) * rows] = spread[k * rows : (k + 1) * rows]
+
+
+def spread_rows(mine, other, target, rows, part):
+    chunks = len(mine)
+    slots, width = mine[0].shape
+    return pl.pallas_call(
+        functools.partial(spread_kernel, chunks, part),
+        out_shape=(jax.ShapeDtypeStruct((chunks * rows, width), BF),) * 4,
+        in_specs=[VMEM_SPEC] * (2 * chunks + 1),
+        out_specs=[VMEM_SPEC] * 4,
+        compiler_params=pltpu.CompilerParams(
+            vmem_limit_bytes=(16 << 20) if chunks == 1 else (36 << 20)
+        ),
+        cost_estimate=COST,
+    )(*mine, *other, target)
+
+
+def expert_kernel(expert_ref, mine_ref, other_ref, *refs):
+    slots = mine_ref.shape[0] // 2
+    rows, grads = slice(0, slots), slice(slots, 2 * slots)
+    expert_body(
+        expert_ref, mine_ref.at[rows], other_ref.at[rows], mine_ref.at[grads], other_ref.at[grads], *refs
+    )
+
+
+def expert_body(
+    expert_ref,
+    mine_ref,
+    other_ref,
+    grad_mine_ref,
+    grad_other_ref,
+    target_ref,
+    route_ref,
+    gate_ref,
+    up_ref,
+    down_ref,
+    router_ref,
+    back_mine_ref,
+    back_other_ref,
+    hidden_ref,
+    gate_grad_ref,
+    up_grad_ref,
+    routed_ref,
+    router_grad_ref,
+):
+    slots = mine_ref.shape[0]
+    experts = router_ref.shape[0]
+    tokens = target_ref.shape[1]
+    rows = jnp.concatenate([mine_ref[...], other_ref[...]], axis=0)
+    nt = (((1,), (1,)), ((), ()))
+    tn = (((0,), (0,)), ((), ()))
+    gate_pre = jnp.dot(rows, gate_ref[...], preferred_element_type=F32)
+    up_pre = jnp.dot(rows, up_ref[...], preferred_element_type=F32)
+    sigmoid = 1.0 / (1.0 + jnp.exp(-gate_pre))
+    silu = gate_pre * sigmoid
+    hidden = (silu * up_pre).astype(BF)
+    hidden_ref[...] = hidden
+    result = jnp.dot(hidden, down_ref[...], preferred_element_type=F32).astype(BF).astype(F32)
+    slot_iota = lax.broadcasted_iota(jnp.int32, (slots, tokens), 0)
+    expert_iota = lax.broadcasted_iota(jnp.int32, (experts, tokens), 0)
+    masks = []
+    for side in range(2):
+        pick = one_hot(slot_iota == target_ref[side : side + 1, :])
+        chosen = expert_iota == route_ref[side, 0:1, :]
+        for k in range(1, route_ref.shape[1]):
+            chosen = chosen | (expert_iota == route_ref[side, k : k + 1, :])
+        masks.append(lax.dot_general(pick, one_hot(chosen), nt, preferred_element_type=F32))
+    chosen = jnp.concatenate(masks, axis=0) > 0.5
+    logits = lax.dot_general(rows, router_ref[...], nt, preferred_element_type=F32)
+    top = jnp.max(jnp.where(chosen, logits, MASKED), axis=1, keepdims=True)
+    weights = jnp.where(chosen, jnp.exp(logits - top), 0.0)
+    total = jnp.sum(weights, axis=1, keepdims=True)
+    gates = weights / jnp.where(total > 0.0, total, 1.0)
+    mine = lax.broadcasted_iota(jnp.int32, gates.shape, 1) == expert_ref[0]
+    gate = jnp.sum(jnp.where(mine, gates, 0.0), axis=1, keepdims=True)
+    gated = (result * gate).astype(BF)
+    back_mine_ref[slots:] = gated[:slots]
+    back_other_ref[slots:] = gated[slots:]
+    grad = jnp.concatenate([grad_mine_ref[...], grad_other_ref[...]], axis=0).astype(F32)
+    gate_value_grad = jnp.sum(grad * result, axis=1, keepdims=True)
+    routed = (grad * gate).astype(BF)
+    routed_ref[...] = routed
+    hidden_grad = lax.dot_general(routed, down_ref[...], nt, preferred_element_type=F32)
+    gate_low = (hidden_grad * up_pre * sigmoid * (1.0 + gate_pre * (1.0 - sigmoid))).astype(BF)
+    up_low = (hidden_grad * silu).astype(BF)
+    gate_grad_ref[...] = gate_low
+    up_grad_ref[...] = up_low
+    logit_grad = (gate_value_grad * gate) * (jnp.where(mine, 1.0, 0.0) - gates)
+    high = logit_grad.astype(BF)
+    low = (logit_grad - high.astype(F32)).astype(BF)
+    both = jnp.concatenate([high, low], axis=1)
+    router = router_ref[...]
+    slot_grad = lax.dot_general(gate_low, gate_ref[...], nt, preferred_element_type=F32)
+    slot_grad = slot_grad + lax.dot_general(up_low, up_ref[...], nt, preferred_element_type=F32)
+    slot_grad = slot_grad + jnp.dot(
+        both, jnp.concatenate([router, router], axis=0), preferred_element_type=F32
+    )
+    slot_grad = slot_grad.astype(BF)
+    back_mine_ref[:slots] = slot_grad[:slots]
+    back_other_ref[:slots] = slot_grad[slots:]
+    router_grad = lax.dot_general(both, rows, tn, preferred_element_type=F32)
+    router_grad_ref[...] = router_grad[:experts] + router_grad[experts:]
+
+
+def expert_rows(expert, mine, other, target, route, *weights):
+    count, width = mine.shape
+    ff = weights[0].shape[1]
+    experts = weights[3].shape[0]
+    low = lambda cols: jax.ShapeDtypeStruct((count, cols), BF)
+    return pl.pallas_call(
+        expert_kernel,
+        out_shape=(
+            low(width),
+            low(width),
+            low(ff),
+            low(ff),
+            low(ff),
+            low(width),
+            jax.ShapeDtypeStruct((experts, width), F32),
+        ),
+        in_specs=[SMEM_SPEC] + [VMEM_SPEC] * 8,
+        out_specs=[VMEM_SPEC] * 7,
+        compiler_params=pltpu.CompilerParams(vmem_limit_bytes=40 << 20),
+        cost_estimate=COST,
+    )(expert, mine, other, target, route, *weights)
+
+
+def place_kernel(share, order_ref, owner_ref, part_ref, query_ref, key_ref, value_ref):
+    cols = query_ref.shape[1]
+    dim = key_ref.shape[1]
+    part = part_ref[0]
+    query_ref[...] = part[:, :cols].astype(F32)
+    key = part[:, cols : cols + dim].astype(F32)
+    value = part[:, cols + dim :].astype(F32)
+    first = pl.program_id(0) % share == 0
+
+    @pl.when(first)
+    def _():
+        key_ref[...] = key
+        value_ref[...] = value
+
+    @pl.when(jnp.logical_not(first))
+    def _():
+        key_ref[...] += key
+        value_ref[...] += value
+
+
+def place_weight_grads(parts, owner, share, dim):
+    count, rows, width = parts.shape
+    cols = width - 2 * dim
+    if count == 8 and share == 2:
+        order = jnp.asarray([0, 4, 1, 5, 2, 6, 3, 7], jnp.int32)
+    else:
+        order = jnp.arange(count, dtype=jnp.int32)
+    owner = owner[order]
+    group = lambda g, order, owner: (0, owner[g] // share)
+    return pl.pallas_call(
+        functools.partial(place_kernel, share),
+        grid_spec=pltpu.PrefetchScalarGridSpec(
+            num_scalar_prefetch=2,
+            grid=(count,),
+            in_specs=[pl.BlockSpec((1, rows, width), lambda g, order, owner: (order[g], 0, 0))],
+            out_specs=[
+                pl.BlockSpec((rows, cols), lambda g, order, owner: (0, owner[g])),
+                pl.BlockSpec((rows, dim), group),
+                pl.BlockSpec((rows, dim), group),
+            ],
+        ),
+        out_shape=(
+            jax.ShapeDtypeStruct((rows, cols * count), F32),
+            jax.ShapeDtypeStruct((rows, dim * count // share), F32),
+            jax.ShapeDtypeStruct((rows, dim * count // share), F32),
+        ),
+        compiler_params=pltpu.CompilerParams(vmem_limit_bytes=20 << 20),
+        cost_estimate=COST,
+    )(order, owner, parts)
+
+
+def rows_kernel(owner_ref, part_ref, out_ref):
+    out_ref[:, 0] = part_ref[0].astype(F32)
+
+
+def place_rows(parts, owner):
+    count, chunks, rows, width = parts.shape
+    return pl.pallas_call(
+        rows_kernel,
+        grid_spec=pltpu.PrefetchScalarGridSpec(
+            num_scalar_prefetch=1,
+            grid=(count,),
+            in_specs=[pl.BlockSpec((1, chunks, rows, width), lambda g, owner: (g, 0, 0, 0))],
+            out_specs=pl.BlockSpec(
+                (chunks, 1, rows, width), lambda g, owner: (0, owner[g], 0, 0)
+            ),
+        ),
+        out_shape=jax.ShapeDtypeStruct((chunks, count, rows, width), F32),
+        compiler_params=pltpu.CompilerParams(vmem_limit_bytes=20 << 20),
+        cost_estimate=COST,
+    )(owner, parts)
 
 
 def move_slots(slot_array):
@@ -386,7 +742,16 @@
     share = ctx_count // kv_heads
     head_cols = heads * head_dim
     group = me // share
-
+    shard_width = model_width // wt_count
+    capacity = max(2, half_rows * top_count * 5 // (4 * experts))
+    dense = ctx_count == 8 and w_gate.shape[0] == 1
+    nt = (((1,), (1,)), ((), ()))
+    tn = (((0,), (0,)), ((), ()))
+    owners = block_owner(ctx_count, me)
+    planes = (plane - jnp.arange(wt_count, dtype=jnp.int32)) % wt_count
+
+    normed_one, attn_back = jax.vjp(rms_norm, inputs, attn_gain)
+    normed_low = normed_one.astype(BF)
     kv_start = group * head_dim
     own_weight = jnp.concatenate(
         [
@@ -396,19 +761,97 @@
         ],
         axis=1,
     )
-    weight = lax.all_gather(own_weight, "wt", axis=0, tiled=True)
     own_chunks = ctx_count // wt_count
     piece_rows = head_cols // ctx_count
     out_piece = lax.dynamic_index_in_dim(
         w_output.reshape(own_chunks, ctx_count, piece_rows, model_width), me, 1, keepdims=False
     )
-    out_pieces = lax.all_gather(out_piece, "wt", axis=0, tiled=True)
-    out_weight = lax.all_to_all(out_pieces, "ctx", 0, 0, tiled=True).reshape(
-        head_cols, model_width
-    )
-    w_router_all = lax.all_gather(w_router, "wt", axis=0, tiled=True)
-
-    owner_pair = pair_order[block_owner(ctx_count, me)]
+    cot = cotangent[0]
+    if dense:
+        cap_rows = 2 * capacity
+        slots = 4 * cap_rows
+        expert = me * wt_count + plane
+        triangle = jnp.triu(jnp.ones((tok_rows, tok_rows), F32)).astype(BF)
+        offsets = (jnp.arange(ctx_count, dtype=jnp.int32) % 4) * cap_rows
+
+        def tables(near):
+            near = near.astype(jnp.int32).reshape(-1, ctx_count, top_count, tok_rows)
+
+            def slot_of(routed_to):
+                hits = jnp.any(near == routed_to, axis=2)
+                ranks = jnp.dot(hits.astype(BF), triangle, preferred_element_type=F32)
+                place = ranks.astype(jnp.int32) - 1 + offsets[None, :, None]
+                return jnp.where(hits, place, -1).reshape(-1, 2, 4 * tok_rows)
+
+            own_slot = slot_of(expert)
+            other_slot = slot_of((me ^ 1) * wt_count + plane)[:, 0]
+            target = jnp.stack(
+                [own_slot[:, 0], jnp.where(other_slot < 0, -1, other_slot + slots)], axis=1
+            )
+            near_routes = (
+                near.reshape(-1, 2, 4, top_count, tok_rows)
+                .transpose(0, 1, 3, 2, 4)
+                .reshape(-1, 2, top_count, 4 * tok_rows)
+            )
+            indices = jnp.arange(experts, dtype=jnp.int32)[:, None, None, None, None]
+            counts = jnp.sum((near[None] == indices).astype(F32), axis=(1, 2, 3, 4))
+            return own_slot, target, target.transpose(0, 2, 1), near_routes, counts
+
+        near = routes[0].T.astype(BF)
+        near_x, near_y = swap(near, 2), swap(near, 4)
+        near = jnp.concatenate([near, near_x, near_y, swap(near_x, 4)], axis=0)
+        near = jnp.concatenate([near, swap(near, 1)], axis=0)
+        via_x, via_y = swap(normed_low, 2), swap(normed_low, 4)
+        router_rows = w_router.T.reshape(-1, model_width)
+        block_rows = own_chunks * piece_rows
+        shard = jnp.concatenate([out_piece.reshape(block_rows, model_width), router_rows], axis=0)
+        out_pieces = jnp.zeros((ctx_count * piece_rows, model_width), BF)
+        router = jnp.zeros((wt_count,) + router_rows.shape, BF)
+        weight = jnp.zeros((model_width, own_weight.shape[1]), BF)
+
+        def keep(j, out_pieces, router, weight, shard, own_weight):
+            put = lax.dynamic_update_slice_in_dim
+            return (
+                put(out_pieces, shard[:block_rows], planes[j] * block_rows, 0),
+                put(router, shard[None, block_rows:], planes[j], 0),
+                put(weight, own_weight, planes[j] * shard_width, 0),
+            )
+
+        ticks = [(shard, own_weight), (ring(shard), ring(own_weight))]
+        diag_a, diag_b = swap(via_x[:half_rows], 4), swap(via_y[half_rows:], 2)
+        hidden_pieces = [normed_low, via_x, via_y, diag_a, diag_b]
+        hidden_pieces = hidden_pieces + [swap(piece, 1) for piece in hidden_pieces]
+        ticks[1], near, cot_block = after((ticks[1], near, cot), ticks[1], hidden_pieces, near)
+        nears = [near, ring(near)]
+        cot_x, cot_y = swap(cot_block, 2), swap(cot_block, 4)
+        ticks.append((ring(ticks[1][0]), ring(ticks[1][1])))
+        first_tables = tables(near)
+        ticks[2], cot_x, cot_y, nears[1] = after(
+            (ticks[2], cot_x, cot_y, nears[1]), ticks[2], cot_x, cot_y, nears[1], first_tables
+        )
+        nears.append(ring(nears[1]))
+        cot_sent = cot_x[:half_rows], cot_y[half_rows:]
+        diag_a, diag_b = swap(cot_sent[0], 4), swap(cot_sent[1], 2)
+        ticks.append((ring(ticks[2][0]), ring(ticks[2][1])))
+        for j in range(wt_count - 1):
+            out_pieces, router, weight = keep(j, out_pieces, router, weight, *ticks[j])
+        cot_all = jnp.concatenate([cot, cot_x, cot_y, diag_a, diag_b], axis=0)
+        ticks[3] = after(ticks[3], cot_all, nears[2], weight, out_pieces)
+        out_pieces, router, weight = keep(3, out_pieces, router, weight, *ticks[3])
+        router = router.reshape(wt_count, experts, shard_width).transpose(1, 0, 2)
+        router = router.reshape(experts, model_width)
+        nears.append(ring(after(nears[2], weight)))
+        cots = [cot_all, ring(after(cot_all, weight))]
+    else:
+        hidden_pieces = plane_gather(normed_low)
+        out_pieces = lax.all_gather(out_piece, "wt", axis=0, tiled=True)
+        weight = lax.all_gather(own_weight, "wt", axis=0, tiled=True)
+        router = lax.all_gather(w_router, "wt", axis=0, tiled=True).T
+    out_weight = lax.all_to_all(
+        out_pieces.reshape(ctx_count, piece_rows, model_width), "ctx", 0, 0, tiled=True
+    ).reshape(head_cols, model_width)
+
+    owner_pair = pair_order[owners]
     blocks = jnp.stack([owner_pair, 2 * ctx_count - 1 - owner_pair], 1).reshape(-1)
     order = jnp.arange(2 * ctx_count, dtype=jnp.int32)
     places = jnp.sum(jnp.where(blocks[:, None] == order[None, :], order[:, None], 0), axis=0)
@@ -421,12 +864,11 @@
     cosine, sine = rope_tables(seq_len, head_dim)
     query_gain_row, key_gain_row = query_gain.reshape(1, -1), key_gain.reshape(1, -1)
 
-    normed_one, attn_back = jax.vjp(rms_norm, inputs, attn_gain)
-    hidden_all = plane_gather(normed_one.astype(BF))
     width = head_cols + 2 * head_dim
     stacked = heads * QUERY_ROWS
+    piece_count = len(hidden_pieces)
     query, key, value, raw, attn_low = pl.pallas_call(
-        functools.partial(attend_kernel, heads),
+        functools.partial(attend_kernel, heads, piece_count),
         out_shape=(
             jax.ShapeDtypeStruct((seq_len, head_cols), BF),
             jax.ShapeDtypeStruct((seq_len, head_dim), BF),
@@ -434,19 +876,16 @@
             jax.ShapeDtypeStruct((seq_len, head_cols + head_dim), F32),
             jax.ShapeDtypeStruct((2 * ctx_count, half_rows, head_cols), BF),
         ),
-        in_specs=[SMEM_SPEC] * 3 + [VMEM_SPEC] * 8,
+        in_specs=[SMEM_SPEC] * 3 + [VMEM_SPEC] * (7 + piece_count),
         out_specs=[VMEM_SPEC] * 5,
         scratch_shapes=[pltpu.VMEM((stacked, seq_len), F32)],
-        cost_estimate=pl.CostEstimate(
-            flops=2 * seq_len * model_width * width + 2 * seq_len * seq_len * head_cols,
-            bytes_accessed=16 << 20,
-            transcendentals=heads * seq_len * seq_len // 2,
-        ),
+        compiler_params=pltpu.CompilerParams(vmem_limit_bytes=ATTEND_LIMIT),
+        cost_estimate=COST,
     )(
         blocks,
         places,
         first,
-        hidden_all,
+        *hidden_pieces,
         weight,
         query_gain_row,
         key_gain_row,
@@ -456,128 +895,240 @@
         seg_col,
     )
     attn_rows = attn_low.reshape(seq_len, head_cols)
-    attn_part = low_matmul(attn_rows, out_weight).astype(BF)
-    residual = inputs + plane_scatter(attn_part.reshape(ctx_count, tok_rows, model_width))
+    later_tables = []
+
+    def fill(sends):
+        if dense:
+            later_tables.extend(tables(after(jnp.concatenate(nears[1:], axis=0), sends)))
+        return tuple(later_tables)
+
+    residual = inputs + plane_scatter(
+        lambda rows: low_matmul(rows, out_weight), attn_rows, fill
+    )
     normed_two, ffn_back = jax.vjp(rms_norm, residual, ffn_gain)
     normed_two_low = normed_two.astype(BF)
     grad_out = cotangent[0].astype(F32)
-    capacity = max(2, half_rows * top_count * 5 // (4 * experts))
-    slot_rows = 2 * capacity
-    local_experts = w_gate.shape[0]
-    logits = low_matmul(normed_two_low, w_router_all)
-    local_routes = routes[0]
-
-    def router_fn(logit_values):
-        router_probs = jax.nn.softmax(logit_values, axis=-1)
-        chosen = jnp.take_along_axis(router_probs, local_routes, axis=1)
-        return (chosen / jnp.sum(chosen, axis=1, keepdims=True), router_probs)
-
-    (gate_values, router_probs), router_back = jax.vjp(router_fn, logits)
-    route_flat = local_routes.reshape(-1)
-    route_hits = (route_flat[:, None] == jnp.arange(experts, dtype=jnp.int32)[None, :]).astype(
-        jnp.int32
-    )
-    counts, prob_sums = lax.psum(
-        (jnp.sum(route_hits, axis=0).astype(jnp.float32), jnp.sum(router_probs, axis=0)),
-        ("ctx", "wt"),
-    )
-    shares = counts / (total_tokens * top_count)
-    balance = experts * experts * shares * (prob_sums / total_tokens)
-    loss_value = jnp.mean(balance)
-    halves = route_hits.reshape(2, half_rows * top_count, experts)
-    ranks = jnp.sum((jnp.cumsum(halves, axis=1) - halves) * halves, axis=2).reshape(-1)
-    half_index = jnp.arange(tok_rows * top_count, dtype=jnp.int32) // (half_rows * top_count)
-    slot_index = route_flat * slot_rows + half_index * capacity + ranks
-    slot_owner = (
-        jnp.full((experts * slot_rows,), tok_rows * top_count, jnp.int32)
-        .at[slot_index]
-        .set(jnp.arange(tok_rows * top_count, dtype=jnp.int32))
-    )
-    slot_shape = (experts // local_experts, local_experts, slot_rows, model_width)
-    padded = jnp.concatenate([normed_two_low, jnp.zeros((1, model_width), jnp.bfloat16)], axis=0)
-    outgoing = padded[slot_owner // top_count].reshape(slot_shape)
-    arrived = move_slots(outgoing)
-    gate_pre = jnp.einsum("nesd,edf->nesf", arrived, w_gate, preferred_element_type=jnp.float32)
-    up_pre = jnp.einsum("nesd,edf->nesf", arrived, w_up, preferred_element_type=jnp.float32)
-    hidden_low, swiglu_back = jax.vjp(swiglu, gate_pre, up_pre)
-    hidden_low = hidden_low.astype(jnp.bfloat16)
-    expert_out = jnp.einsum(
-        "nesf,efd->nesd", hidden_low, w_down, preferred_element_type=jnp.float32
-    ).astype(jnp.bfloat16)
-    returned = move_slots(expert_out).reshape(experts * slot_rows, model_width)
-    picked = returned[slot_index].reshape(tok_rows, top_count, model_width)
-    mixture = jnp.einsum("tk,tkd->td", gate_values, picked, preferred_element_type=jnp.float32)
-    output = (residual + mixture).astype(jnp.bfloat16)
-    grad_gates = jnp.einsum("td,tkd->tk", grad_out, picked, preferred_element_type=jnp.float32)
-    grad_routed = (
-        (gate_values[:, :, None] * grad_out[:, None, :])
-        .astype(jnp.bfloat16)
-        .reshape(-1, model_width)
-    )
-    grad_routed = jnp.concatenate([grad_routed, jnp.zeros((1, model_width), jnp.bfloat16)], axis=0)
-    grad_arrived = move_slots(grad_routed[slot_owner].reshape(slot_shape))
-    grad_hidden = jnp.einsum(
-        "nesd,efd->nesf", grad_arrived, w_down, preferred_element_type=jnp.float32
-    )
-    grad_w_down = jnp.einsum(
-        "nesf,nesd->efd", hidden_low, grad_arrived, preferred_element_type=jnp.float32
-    )
-    grad_gate_pre, grad_up_pre = swiglu_back(grad_hidden)
-    gate_grad_low = grad_gate_pre.astype(jnp.bfloat16)
-    up_grad_low = grad_up_pre.astype(jnp.bfloat16)
-    grad_w_gate = jnp.einsum(
-        "nesd,nesf->edf", arrived, gate_grad_low, preferred_element_type=jnp.float32
-    )
-    grad_w_up = jnp.einsum(
-        "nesd,nesf->edf", arrived, up_grad_low, preferred_element_type=jnp.float32
-    )
-    grad_slots = (
-        jnp.einsum("nesf,edf->nesd", gate_grad_low, w_gate, preferred_element_type=jnp.float32)
-        + jnp.einsum("nesf,edf->nesd", up_grad_low, w_up, preferred_element_type=jnp.float32)
-    ).astype(jnp.bfloat16)
-    grad_back = move_slots(grad_slots).reshape(experts * slot_rows, model_width)
-    grad_normed_two = jnp.sum(
-        grad_back[slot_index].reshape(tok_rows, top_count, model_width).astype(jnp.float32), axis=1
-    )
-    prob_grad = jnp.broadcast_to(experts * shares / total_tokens, router_probs.shape)
-    (grad_logits,) = router_back((grad_gates, prob_grad))
-    logits_low = grad_logits.astype(jnp.bfloat16)
-    grad_normed_two = grad_normed_two + jnp.einsum(
-        "te,de->td", logits_low, w_router_all, preferred_element_type=jnp.float32
-    )
-    grad_w_router = jnp.einsum(
-        "td,te->de", normed_two_low, logits_low, preferred_element_type=jnp.float32
-    )
+    if dense:
+        own_slot, target_rows, target_cols, near_routes = (
+            jnp.concatenate([f, r], axis=0) for f, r in zip(first_tables[:4], later_tables[:4])
+        )
+        counts = first_tables[4] + later_tables[4]
+        logits = lax.dot_general(normed_two_low, router, nt, preferred_element_type=F32)
+        router_probs = jax.nn.softmax(logits, axis=-1)
+        shares = counts / (total_tokens * top_count)
+        prob_grad = (experts * shares / total_tokens)[None, :]
+        logits_grad = router_probs * (
+            prob_grad - jnp.sum(router_probs * prob_grad, axis=1, keepdims=True)
+        )
+        logits_grad_low = logits_grad.astype(BF)
+        last = wt_count - 1
+        mine_backs, other_backs, results = [], [], []
+
+        def compute(j, pieces, others, gates):
+            pieces = after(pieces, *gates)
+            mine, other = select_rows(pieces, others, target_rows[j], slots)
+            received = swap(other, 1)
+            result = expert_rows(
+                expert.reshape(1),
+                mine,
+                received,
+                own_slot[j],
+                near_routes[j],
+                w_gate[0],
+                w_up[0],
+                w_down[0],
+                router,
+            )
+            mine_backs.append(result[0])
+            other_backs.append(swap(result[1], 1))
+            results.append((mine[:slots], received[:slots]) + tuple(result[2:]))
+            return result[0]
+
+        chunk, pieces, done = normed_two_low, None, None
+        for j in range(wt_count):
+            if j > 0:
+                chunk = ring(chunk)
+            payload = chunk
+            if j == last:
+                cot_last = ring(cots[j - 1][:tok_rows])
+                halves = chunk[:half_rows], cot_last[:half_rows], chunk[half_rows:], cot_last[half_rows:]
+                payload = jnp.concatenate(halves, axis=0)
+            elif j > 1:
+                cots.append(ring(cots[-1]))
+            if j > 0:
+                payload = after(payload, sent)
+            via_x, via_y = swap(payload, 2), swap(payload, 4)
+            if done is not None:
+                via_x, via_y = after((via_x, via_y), done)
+            middle = via_x.shape[0] // 2
+            sent = via_x[:middle], via_y[middle:]
+            before, pieces = pieces, [payload, via_x, via_y, swap(sent[0], 4), swap(sent[1], 2)]
+            if before is not None:
+                done = compute(j - 1, before, [cots[j - 1]], (sent,))
+        parts = spread_rows(mine_backs, other_backs, target_cols[:last], tok_rows, 0)
+        half = parts[3].shape[0] // 2
+        group_sent = parts[3][:half], parts[3][half:]
+        group_diag = swap(group_sent[0], 4), swap(group_sent[1], 2)
+        done = compute(last, pieces, [], (group_sent,))
+        group_x, group_y = add_diag(*after((parts[1], parts[2]), done), *after(group_diag, done))
+        got_x, got_y = swap(group_x, 2), swap(group_y, 4)
+        tail = spread_rows(
+            mine_backs[last:], other_backs[last:], after(target_cols[last:], group_x, group_y), tok_rows, 0
+        )
+        tail_sent = tail[3][:half_rows], tail[3][half_rows:]
+        tail_diag = swap(tail_sent[0], 4), swap(tail_sent[1], 2)
+        rows_all = jnp.concatenate([r for res in results for r in res[:2]], axis=0)
+        hidden_low, gate_low, up_low, routed = (
+            jnp.concatenate([res[k] for res in results], axis=0) for k in range(2, 6)
+        )
+        rows_all = after(rows_all, tail_sent)
+        grad_w_gate = lax.dot_general(rows_all, gate_low, tn, preferred_element_type=F32)[None]
+        tail_x, tail_y = add_diag(
+            *after((tail[1], tail[2]), grad_w_gate), *after(tail_diag, grad_w_gate)
+        )
+        tail_got = swap(tail_x, 2), swap(tail_y, 4)
+        rows_all = after(rows_all, tail_x, tail_y)
+        grad_w_up = lax.dot_general(rows_all, up_low, tn, preferred_element_type=F32)[None]
+        hidden_low = after(hidden_low, grad_w_up)
+        grad_w_down = lax.dot_general(hidden_low, routed, tn, preferred_element_type=F32)[None]
+        got_x, got_y = after((got_x, got_y), grad_w_down)
+        sums = parts[0].astype(F32) + got_x.astype(F32) + got_y.astype(F32)
+        sums = sums.reshape(last, tok_rows, model_width)
+        total = sums[1].astype(BF)
+        backs = after(mine_backs[0], total)
+        total = ring(total)
+        parts = spread_rows([backs] + mine_backs[1:], other_backs, target_cols, tok_rows, 1)
+        total = after(total, parts)
+        tail_got = after(tail_got, parts)
+        for j in range(2, last):
+            total = ring((total.astype(F32) + sums[j]).astype(BF)).astype(F32)
+        tail_sum = tail[0].astype(F32) + tail_got[0].astype(F32) + tail_got[1].astype(F32)
+        total = ring((total.astype(F32) + tail_sum).astype(BF)).astype(F32) + sums[0]
+        grad_normed_two = total + jnp.dot(logits_grad_low, router, preferred_element_type=F32)
+        router_grad = sum(res[6] for res in results) + lax.dot_general(
+            logits_grad_low, normed_two_low, tn, preferred_element_type=F32
+        )
+    else:
+        w_router_all = router.T
+        slot_rows = 2 * capacity
+        local_experts = w_gate.shape[0]
+        logits = low_matmul(normed_two_low, w_router_all)
+        local_routes = routes[0]
+
+        def router_fn(logit_values):
+            router_probs = jax.nn.softmax(logit_values, axis=-1)
+            chosen = jnp.take_along_axis(router_probs, local_routes, axis=1)
+            return (chosen / jnp.sum(chosen, axis=1, keepdims=True), router_probs)
+
+        (gate_values, router_probs), router_back = jax.vjp(router_fn, logits)
+        route_flat = local_routes.reshape(-1)
+        route_hits = (route_flat[:, None] == jnp.arange(experts, dtype=jnp.int32)[None, :]).astype(
+            jnp.int32
+        )
+        counts = lax.psum(jnp.sum(route_hits, axis=0).astype(jnp.float32), ("ctx", "wt"))
+        shares = counts / (total_tokens * top_count)
+        halves = route_hits.reshape(2, half_rows * top_count, experts)
+        ranks = jnp.sum((jnp.cumsum(halves, axis=1) - halves) * halves, axis=2).reshape(-1)
+        half_index = jnp.arange(tok_rows * top_count, dtype=jnp.int32) // (half_rows * top_count)
+        slot_index = route_flat * slot_rows + half_index * capacity + ranks
+        slot_owner = (
+            jnp.full((experts * slot_rows,), tok_rows * top_count, jnp.int32)
+            .at[slot_index]
+            .set(jnp.arange(tok_rows * top_count, dtype=jnp.int32))
+        )
+        slot_shape = (experts // local_experts, local_experts, slot_rows, model_width)
+        padded = jnp.concatenate([normed_two_low, jnp.zeros((1, model_width), jnp.bfloat16)], axis=0)
+        outgoing = padded[slot_owner // top_count].reshape(slot_shape)
+        arrived = move_slots(outgoing)
+        gate_pre = jnp.einsum("nesd,edf->nesf", arrived, w_gate, preferred_element_type=jnp.float32)
+        up_pre = jnp.einsum("nesd,edf->nesf", arrived, w_up, preferred_element_type=jnp.float32)
+        hidden_low, swiglu_back = jax.vjp(swiglu, gate_pre, up_pre)
+        hidden_low = hidden_low.astype(jnp.bfloat16)
+        expert_out = jnp.einsum(
+            "nesf,efd->nesd", hidden_low, w_down, preferred_element_type=jnp.float32
+        ).astype(jnp.bfloat16)
+        returned = move_slots(expert_out).reshape(experts * slot_rows, model_width)
+        picked = returned[slot_index].reshape(tok_rows, top_count, model_width)
+        mixture = jnp.einsum("tk,tkd->td", gate_values, picked, preferred_element_type=jnp.float32)
+        output = (residual + mixture).astype(jnp.bfloat16)
+        grad_gates = jnp.einsum("td,tkd->tk", grad_out, picked, preferred_element_type=jnp.float32)
+        grad_routed = (
+            (gate_values[:, :, None] * grad_out[:, None, :])
+            .astype(jnp.bfloat16)
+            .reshape(-1, model_width)
+        )
+        grad_routed = jnp.concatenate([grad_routed, jnp.zeros((1, model_width), jnp.bfloat16)], axis=0)
+        grad_arrived = move_slots(grad_routed[slot_owner].reshape(slot_shape))
+        grad_hidden = jnp.einsum(
+            "nesd,efd->nesf", grad_arrived, w_down, preferred_element_type=jnp.float32
+        )
+        grad_w_down = jnp.einsum(
+            "nesf,nesd->efd", hidden_low, grad_arrived, preferred_element_type=jnp.float32
+        )
+        grad_gate_pre, grad_up_pre = swiglu_back(grad_hidden)
+        gate_grad_low = grad_gate_pre.astype(jnp.bfloat16)
+        up_grad_low = grad_up_pre.astype(jnp.bfloat16)
+        grad_w_gate = jnp.einsum(
+            "nesd,nesf->edf", arrived, gate_grad_low, preferred_element_type=jnp.float32
+        )
+        grad_w_up = jnp.einsum(
+            "nesd,nesf->edf", arrived, up_grad_low, preferred_element_type=jnp.float32
+        )
+        grad_slots = (
+            jnp.einsum("nesf,edf->nesd", gate_grad_low, w_gate, preferred_element_type=jnp.float32)
+            + jnp.einsum("nesf,edf->nesd", up_grad_low, w_up, preferred_element_type=jnp.float32)
+        ).astype(jnp.bfloat16)
+        grad_back = move_slots(grad_slots).reshape(experts * slot_rows, model_width)
+        grad_normed_two = jnp.sum(
+            grad_back[slot_index].reshape(tok_rows, top_count, model_width).astype(jnp.float32), axis=1
+        )
+        prob_grad = jnp.broadcast_to(experts * shares / total_tokens, router_probs.shape)
+        (grad_logits,) = router_back((grad_gates, prob_grad))
+        logits_low = grad_logits.astype(jnp.bfloat16)
+        grad_normed_two = grad_normed_two + jnp.einsum(
+            "te,de->td", logits_low, w_router_all, preferred_element_type=jnp.float32
+        )
+        grad_w_router = jnp.einsum(
+            "td,te->de", normed_two_low, logits_low, preferred_element_type=jnp.float32
+        )
+        router_grad = grad_w_router.T
     grad_residual_part, grad_ffn_gain = ffn_back(grad_normed_two)
     grad_residual = grad_out + grad_residual_part
-    grad_attn_all = plane_gather(grad_residual.astype(BF)).reshape(seq_len, model_width)
-    grad_heads = lax.dot_general(
-        grad_attn_all, out_weight, (((1,), (1,)), ((), ())), preferred_element_type=F32
+    grad_pieces = plane_gather(grad_residual.astype(BF))
+    out_grad = lax.dot_general(
+        attn_rows, jnp.concatenate(grad_pieces, axis=0), tn, preferred_element_type=F32
     ).astype(BF)
+    if dense:
+        half = parts[3].shape[0] // 2
+        out_sent = after((parts[3][:half], parts[3][half:]), grad_pieces)
+        out_diag = swap(out_sent[0], 4), swap(out_sent[1], 2)
+        query = after(query, out_sent, out_grad)
+    out_grad = lax.all_to_all(
+        out_grad.reshape(ctx_count, piece_rows, model_width), "ctx", 0, 0, tiled=True
+    )
     head_grads, grad_query_gain, grad_key_gain = pl.pallas_call(
-        functools.partial(attend_back_kernel, heads),
+        functools.partial(attend_back_kernel, heads, piece_count),
         out_shape=(
             jax.ShapeDtypeStruct((2 * ctx_count, half_rows, width), BF),
             jax.ShapeDtypeStruct((1, head_dim), F32),
             jax.ShapeDtypeStruct((1, head_dim), F32),
         ),
-        in_specs=[SMEM_SPEC] * 2 + [VMEM_SPEC] * 11,
+        in_specs=[SMEM_SPEC] * 2 + [VMEM_SPEC] * (11 + piece_count),
         out_specs=[VMEM_SPEC] * 3,
         scratch_shapes=[
             pltpu.VMEM((stacked, seq_len), F32),
             pltpu.VMEM((stacked, seq_len), F32),
             pltpu.VMEM((seq_len, head_dim), F32),
             pltpu.VMEM((seq_len, head_dim), F32),
+            pltpu.VMEM((2 * ctx_count, half_rows, head_cols), BF),
         ],
-        cost_estimate=pl.CostEstimate(
-            flops=5 * seq_len * seq_len * head_cols,
-            bytes_accessed=12 << 20,
-            transcendentals=heads * seq_len * seq_len // 2,
-        ),
+        compiler_params=pltpu.CompilerParams(vmem_limit_bytes=ATTEND_LIMIT),
+        cost_estimate=COST,
     )(
         places,
         first,
-        grad_heads.reshape(2 * ctx_count, half_rows, head_cols),
+        *grad_pieces,
+        out_weight,
         query,
         key,
         value,
@@ -590,66 +1141,101 @@
         seg_col,
     )
     head_grads = head_grads.reshape(seq_len, width)
-    hidden_rows = hidden_all.reshape(seq_len, model_width)
-    weight_grad = lax.dot_general(
-        hidden_rows, head_grads, (((0,), (0,)), ((), ())), preferred_element_type=F32
-    ).astype(BF)
-    weight_grad = lax.psum_scatter(weight_grad, "wt", scatter_dimension=0, tiled=True)
-    weight_grads = lax.all_gather(weight_grad, "ctx", axis=0, tiled=False)
-    shard_rows = w_query.shape[0]
-    grad_w_query = (
-        weight_grads[:, :, :head_cols].transpose(1, 0, 2).reshape(shard_rows, -1).astype(F32)
-    )
-
-    def pair_sum(cols):
-        cols = cols.astype(F32).reshape(kv_heads, share, shard_rows, head_dim)
-        return jnp.sum(cols, axis=1).transpose(1, 0, 2).reshape(shard_rows, -1)
-
-    grad_w_key = pair_sum(weight_grads[:, :, head_cols : head_cols + head_dim])
-    grad_w_value = pair_sum(weight_grads[:, :, head_cols + head_dim :])
-    out_grad = lax.dot_general(
-        attn_rows, grad_attn_all, (((0,), (0,)), ((), ())), preferred_element_type=F32
-    ).astype(BF)
-    out_grad = lax.all_to_all(
-        out_grad.reshape(ctx_count, piece_rows, model_width), "ctx", 0, 0, tiled=True
-    )
-    out_grad = lax.psum_scatter(out_grad, "wt", scatter_dimension=0, tiled=True)
-    out_grads = lax.all_gather(out_grad, "ctx", axis=1, tiled=False)
-    grad_w_output = out_grads.reshape(w_output.shape).astype(F32)
-    grad_hidden_part = lax.dot_general(
-        head_grads, weight, (((1,), (1,)), ((), ())), preferred_element_type=F32
-    ).astype(BF)
-    grad_normed_one = plane_scatter(grad_hidden_part.reshape(ctx_count, tok_rows, model_width))
+    hidden_rows = jnp.concatenate(hidden_pieces, axis=0)
+    last_gates = ()
+    if dense:
+        def weight_part(j, grads):
+            cols = lax.dynamic_slice_in_dim(hidden_rows, planes[j] * shard_width, shard_width, 1)
+            return lax.dot_general(cols, grads, tn, preferred_element_type=F32)
+
+        part = weight_part(1, head_grads).astype(BF)
+        total = ring(part)
+        out_x, out_y = add_diag(*after((parts[1], parts[2]), part), *after(out_diag, part))
+        got_x, got_y = swap(out_x, 2), swap(out_y, 4)
+        head_grads = after(head_grads, out_x, out_y)
+        part = weight_part(2, head_grads)
+        more = [weight_part(j, after(head_grads, part)) for j in (3, 0)]
+        total = after(total, more).astype(F32) + part
+        total_low = total.astype(BF)
+        total = ring(total_low)
+        head_grads = after(head_grads, total_low, out_grad)
+        total = total.astype(F32) + more[0]
+        total_low = total.astype(BF)
+        total = ring(total_low)
+        got_x, got_y = after((got_x, got_y), total_low)
+        out_parts = parts[0].astype(F32) + got_x.astype(F32) + got_y.astype(F32)
+        out_parts = out_parts.reshape(wt_count, tok_rows, model_width)
+        weight_grad = (total.astype(F32) + more[1]).astype(BF)
+        out_parts = after([out_parts[j] for j in range(wt_count)], weight_grad)
+        output = (residual + ring_sum(out_parts, BF)).astype(BF)
+        out_grad = after(out_grad, weight_grad)
+        last_gates = (got_x, got_y)
+    else:
+        weight_grad = lax.dot_general(hidden_rows, head_grads, tn, preferred_element_type=F32)
+        weight_grad = lax.psum_scatter(
+            weight_grad.astype(BF), "wt", scatter_dimension=0, tiled=True
+        )
+    weight_grads = jnp.concatenate(plane_gather(weight_grad), axis=0)
+    grad_w_query, grad_w_key, grad_w_value = place_weight_grads(
+        weight_grads.reshape(ctx_count, -1, width), owners, share, head_dim
+    )
+    if dense:
+        parts = out_grad.reshape(wt_count, own_chunks * piece_rows, model_width)[planes]
+        out_grad = ring_sum([parts[j] for j in range(wt_count)], BF).astype(BF)
+    else:
+        out_grad = lax.psum_scatter(out_grad, "wt", scatter_dimension=0, tiled=True)
+    out_grads = jnp.concatenate(plane_gather(out_grad.reshape(-1, model_width)), axis=0)
+    grad_w_output = place_rows(
+        out_grads.reshape(ctx_count, own_chunks, piece_rows, model_width), owners
+    ).reshape(w_output.shape)
+    grad_normed_one = plane_scatter(
+        lambda rows: lax.dot_general(rows, weight, nt, preferred_element_type=F32),
+        head_grads,
+        None,
+        *last_gates,
+    )
     grad_inputs_part, grad_attn_gain = attn_back(grad_normed_one)
     grad_inputs = grad_residual + grad_inputs_part
-    small = lax.psum(
-        (
-            grad_w_router,
-            grad_attn_gain,
-            grad_ffn_gain,
-            grad_query_gain[0],
-            grad_key_gain[0],
-        ),
-        ("ctx", "wt"),
-    )
-    small = [
-        lax.dynamic_slice_in_dim(s, plane * (s.shape[0] // wt_count), s.shape[0] // wt_count, 0)
-        for s in small
-    ]
+
+    part = head_dim // wt_count
+    prob_sums = jnp.sum(router_probs, axis=0)
+    prob_row = jnp.zeros((shard_width - 2 * part,), F32)
+    if dense:
+        prob_row = lax.dynamic_update_slice_in_dim(prob_row, prob_sums, plane * experts, 0)
+    gains = jnp.concatenate(
+        [
+            grad_query_gain.reshape(wt_count, part),
+            grad_key_gain.reshape(wt_count, part),
+            jnp.broadcast_to(prob_row[None], (wt_count, shard_width - 2 * part)),
+        ],
+        axis=1,
+    )
+    small = jnp.concatenate([router_grad, grad_ffn_gain[None], grad_attn_gain[None]], axis=0)
+    small = small.reshape(experts + 2, wt_count, shard_width).transpose(1, 0, 2)
+    small = jnp.concatenate([small, gains[:, None]], axis=1)[planes]
+    small = ring_sum([small[j] for j in range(wt_count)], F32)
+    small = axis_sum(small, "ctx")
+    if dense:
+        prob_sums = small[experts + 2, 2 * part : 2 * part + wt_count * experts]
+        prob_sums = jnp.sum(prob_sums.reshape(wt_count, experts), axis=0)
+    else:
+        prob_sums = axis_sum(axis_sum(prob_sums[None], "ctx"), "wt")[0]
+    balance = experts * experts * shares * (prob_sums / total_tokens)
+    loss_value = jnp.mean(balance)
     return (
         output[None],
         loss_value,
         balance,
         grad_inputs[None],
-        small[1],
-        small[2],
-        small[3],
-        small[4],
+        small[experts + 1],
+        small[experts],
+        small[experts + 2, :part],
+        small[experts + 2, part : 2 * part],
         grad_w_query,
         grad_w_key,
         grad_w_value,
         grad_w_output,
-        small[0],
+        small[:experts].T,
         grad_w_gate,
         grad_w_up,
         grad_w_down,

time: 1220 us -> 859 us (0.70)
  waiting for transfers between devices: 591 us -> 358 us
  blocking collectives: 221 us -> 0 us
  Pallas kernels: 52.4 us -> 128 us
  matrix products: 111 us -> 46.8 us
  starting transfers between devices: 52.5 us -> 103 us
  local copies, waits for them, and re-layouts: 107 us -> 137 us
    all_to_all x5 -> x2, waiting for transfers between devices: 312 us -> 0.27 us  [the longest x1 0.27 us: local(): lax.all_to_all(out_pieces.reshape(ctx_count, piece_rows, model_width), 'c...]
    ppermute x0 -> x33, waiting for transfers between devices: none -> 255 us  [the longest x30 250 us: ring(): lax.ppermute(value, 'wt', [(i, (i + 1) % count) for i in range(count)])]
    psum x2 -> x0, blocking collectives: 177 us -> none  [local(): lax.psum((jnp.sum(route_hits, axis=0).astype(jnp.float32), jnp.sum(router...]
    all_gather x4 -> x0, waiting for transfers between devices: 95.2 us -> none  [the longest x1 50.3 us: local(): weight = lax.all_gather(own_weight, 'wt', axis=0, tiled=True)]
    psum x1 -> x0, waiting for transfers between devices: 91.4 us -> none  [local(): lax.psum((grad_w_router, grad_attn_gain, grad_ffn_gain, grad_query_gain[0...]
    pallas_call x2 -> x15, Pallas kernels: 52.4 us -> 128 us  [the longest x4 48.5 us: expert_rows(): pl.pallas_call(expert_kernel, out_shape=(low(width), low(width), low(ff),...]
    dot_general x17, matrix products: 107 us -> 44.3 us  [the longest x1 8.77 us: local(): lax.dot_general(rows_all, up_low, tn, preferred_element_type=F32)[None]]
    ppermute x20 -> x90, waiting for transfers between devices: 43.5 us -> 102 us  [swap(): return lax.ppermute(value, 'ctx', [(i, i ^ bit) for i in range(count)])]
  transfers between devices with their start and end apart: 32 -> 125, of which waited for: 19 -> 59; matrix products, arithmetic and copies ran while one was open for 13% -> 24% of each run, Pallas kernels for 4% -> 13%
where the time goes in v2:
time: 859 us; the launch traced here: 851 us
  waiting for transfers between devices  358 us (42%)
  local copies, waits for them, and re-layouts  137 us (16%)
  Pallas kernels  128 us (15%)
  starting transfers between devices  103 us (12%)
  other arithmetic  60.5 us (7%)
  matrix products  46.8 us (5%)
  between operations  18.7 us (2%)
    ppermute x30, waiting for transfers between devices, ring(): lax.ppermute(value, 'wt', [(i, (i + 1) % count) for i in range(count)])  250 us
    ppermute x90, waiting for transfers between devices, swap(): return lax.ppermute(value, 'ctx', [(i, i ^ bit) for i in range(count)])  102 us
    ppermute x90, starting transfers between devices, swap(): return lax.ppermute(value, 'ctx', [(i, i ^ bit) for i in range(count)])  71 us
    unnamed x408, local copies, waits for them, and re-layouts  69.4 us
    pallas_call x4, Pallas kernels, expert_rows(): pl.pallas_call(expert_kernel, out_shape=(low(width), low(width), low(ff),...  48.5 us
    pallas_call x1, Pallas kernels, local(): pl.pallas_call(functools.partial(attend_back_kernel, heads, piece_count),...  23.1 us
    ppermute x30, starting transfers between devices, ring(): lax.ppermute(value, 'wt', [(i, (i + 1) % count) for i in range(count)])  20.4 us
  transfers between devices with their start and end apart: 125, of which 59 were waited for; matrix products, arithmetic and copies ran while one was open for 24% of the time, Pallas kernels for 13%

profile of v2, /device:TPU:0, one launch (start us, length us, event | category | flops | bytes accessed | tf_op | source)
XLA Modules:
  0.0 851.2 jit_solution(5891577075064242826)
XLA Ops:
  41.2 12.8 %collective-permute-done.10 = bf16[512,768]{1,0:T(8,128)(2,1)} collective-permute-done((bf16[512,768]{1,0:T(8,128)(2,1)}, bf16[512,768]{1,0:T(8,128)(2,1)}, u32[]{:S(2)}, u32[]{:S(2)}) %collective-permute-start.10) | collective-permute-done | bytes 786464 | tf_op jit(solution)/shard_map/ppermute | solution.py:130
  79.0 14.4 %collective-permute-done.16 = bf16[512,768]{1,0:T(8,128)(2,1)} collective-permute-done((bf16[512,768]{1,0:T(8,128)(2,1)}, bf16[512,768]{1,0:T(8,128)(2,1)}, u32[]{:S(2)}, u32[]{:S(2)}) %collective-permute-start.16) | collective-permute-done | bytes 786464 | tf_op jit(solution)/shard_map/ppermute | solution.py:130
  108.2 8.0 collective-permute-done.20
  116.2 13.5 %collective-permute-done.21 = bf16[512,768]{1,0:T(8,128)(2,1)} collective-permute-done((bf16[512,768]{1,0:T(8,128)(2,1)}, bf16[512,768]{1,0:T(8,128)(2,1)}, u32[]{:S(2)}, u32[]{:S(2)}) %collective-permute-start.21) | collective-permute-done | bytes 786464 | tf_op jit(solution)/shard_map/ppermute | solution.py:130
  140.5 15.1 %shard_map.306 = (bf16[1024,512]{1,0:T(8,128)(2,1)S(1)}, bf16[1024,128]{1,0:T(8,128)(2,1)S(1)}, bf16[1024,128]{1,0:T(8,128)(2,1)S(1)}, f32[1024,640]{1,0:T(8,128)S(1)}, bf16[16,64,512]{2,1,0:T(8,128)(2,1)S(1)}) custom-call(s32[16]{0:T(128)S(1)} %reshape.357.block_ref, s32[16]{0:T(128)S(1)} %select_reduce_fusion.place_ref, ...), custom_call_target="tpu_custom_call" | custom-call | flops 1 | bytes 1 | tf_op jit(solution)/shard_map/pallas_call | solution.py:870
  185.3 27.3 %collective-permute-done.44.refs_5_ = bf16[512,2048]{1,0:T(8,128)(2,1)} collective-permute-done((bf16[512,2048]{1,0:T(8,128)(2,1)}, bf16[512,2048]{1,0:T(8,128)(2,1)}, u32[]{:S(2)}, u32[]{:S(2)}) %collective-permute-start.44) | collective-permute-done | bytes 2097184 | tf_op jit(solution)/shard_map/ppermute | solution.py:130
  220.2 8.3 collective-permute-done.32.refs_2_
  230.0 43.1 %collective-permute-done.35.refs_0_ = bf16[128,2048]{1,0:T(8,128)(2,1)} collective-permute-done((bf16[128,2048]{1,0:T(8,128)(2,1)S(1)}, bf16[128,2048]{1,0:T(8,128)(2,1)}, u32[]{:S(2)}, u32[]{:S(2)}) %collective-permute-start.35) | collective-permute-done | bytes 524320 | tf_op jit(solution)/shard_map/ppermute | solution.py:130
  310.7 11.8 %collective-permute-done.41.refs_0_ = bf16[128,2048]{1,0:T(8,128)(2,1)} collective-permute-done((bf16[128,2048]{1,0:T(8,128)(2,1)}, bf16[128,2048]{1,0:T(8,128)(2,1)}, u32[]{:S(2)}, u32[]{:S(2)}) %collective-permute-start.41) | collective-permute-done | bytes 524320 | tf_op jit(solution)/shard_map/ppermute | solution.py:130
  338.9 12.0 %shard_map.308 = (bf16[320,2048]{1,0:T(8,128)(2,1)S(1)}, bf16[320,2048]{1,0:T(8,128)(2,1)S(1)}, bf16[320,768]{1,0:T(8,128)(2,1)S(1)}, bf16[320,768]{1,0:T(8,128)...) custom-call(s32[1]{0:T(128)} %bitcast.29.expert_ref, ...), custom_call_target="tpu_custom_call" | custom-call | flops 1 | bytes 1 | tf_op jit(solution)/shard_map/pallas_call | solution.py:614
  374.0 12.2 %shard_map.310 = (bf16[320,2048]{1,0:T(8,128)(2,1)S(1)}, bf16[320,2048]{1,0:T(8,128)(2,1)S(1)}, bf16[320,768]{1,0:T(8,128)(2,1)S(1)}, bf16[320,768]{1,0:T(8,128)...) custom-call(s32[1]{0:T(128)} %bitcast.29.expert_ref, ...), custom_call_target="tpu_custom_call" | custom-call | flops 1 | bytes 1 | tf_op jit(solution)/shard_map/pallas_call | solution.py:614
  411.4 12.3 %shard_map.312 = (bf16[320,2048]{1,0:T(8,128)(2,1)S(1)}, bf16[320,2048]{1,0:T(8,128)(2,1)S(1)}, bf16[320,768]{1,0:T(8,128)(2,1)S(1)}, bf16[320,768]{1,0:T(8,128)...) custom-call(s32[1]{0:T(128)} %bitcast.29.expert_ref, ...), custom_call_target="tpu_custom_call" | custom-call | flops 1 | bytes 1 | tf_op jit(solution)/shard_map/pallas_call | solution.py:614
  452.2 12.0 %shard_map.315 = (bf16[320,2048]{1,0:T(8,128)(2,1)S(1)}, bf16[320,2048]{1,0:T(8,128)(2,1)S(1)}, bf16[320,768]{1,0:T(8,128)(2,1)S(1)}, bf16[320,768]{1,0:T(8,128)...) custom-call(s32[1]{0:T(128)} %bitcast.29.expert_ref, ...), custom_call_target="tpu_custom_call" | custom-call | flops 1 | bytes 1 | tf_op jit(solution)/shard_map/pallas_call | solution.py:614
  487.0 30.7 %collective-permute-done.66 = bf16[64,2048]{1,0:T(8,128)(2,1)S(1)} collective-permute-done((bf16[64,2048]{1,0:T(8,128)(2,1)S(1)}, bf16[64,2048]{1,0:T(8,128)(2,1)S(1)}, u32[]{:S(2)}, u32[]{:S(2)}) %collective-permute-start.66) | collective-permute-done | bytes 262176 | tf_op jit(solution)/shard_map/ppermute | solution.py:51
  517.9 8.8 %convolution_bitcast_fusion = f32[1,2048,768]{2,1,0:T(8,128)} fusion(bf16[1280,2048]{1,0:T(8,128)(2,1)} %copy-done.147, bf16[320,768]{1,0:T(8,128)(2,1)S(1)} %get-tuple-element.250, bf16[320,768]{1,0:T(8,128)(2,1)S(1)} %get-tuple-element.249, bf16[320,768]{1,0:T(8,128)(2,1)S(1)} %copy-done.111, bf16[320,768]{1,0:T(8,128)(2,1)S(1)} %copy-done.107), kind=kOutput, calls=%fused_computation.16 | convolution fusion | flops 4034396160 | bytes 13500416 | tf_op jit(solution)/shard_map/dot_general | solution.py:991
  552.9 12.6 %collective-permute-done.68 = bf16[128,2048]{1,0:T(8,128)(2,1)S(1)} collective-permute-done((bf16[128,2048]{1,0:T(8,128)(2,1)S(1)}, bf16[128,2048]{1,0:T(8,128)(2,1)S(1)}, u32[]{:S(2)}, u32[]{:S(2)}) %collective-permute-start.68) | collective-permute-done | bytes 524320 | tf_op jit(solution)/shard_map/ppermute | solution.py:130
  566.9 12.1 %collective-permute-done.71 = bf16[128,2048]{1,0:T(8,128)(2,1)S(1)} collective-permute-done((bf16[128,2048]{1,0:T(8,128)(2,1)S(1)}, bf16[128,2048]{1,0:T(8,128)(2,1)S(1)}, u32[]{:S(2)}, u32[]{:S(2)}) %collective-permute-start.71) | collective-permute-done | bytes 524320 | tf_op jit(solution)/shard_map/ppermute | solution.py:130
  607.9 23.1 %shard_map.318 = (bf16[16,64,768]{2,1,0:T(8,128)(2,1)S(1)}, f32[1,128]{1,0:T(1,128)S(1)}, f32[1,128]{1,0:T(1,128)S(1)}) custom-call(s32[16]{0:T(128)S(1)} %copy-done.95, s32[8]{0:T(128)S(1)} %copy-done.89, bf16[128,2048]{1,0:T(8,128)(2,1)S(1)} %get-tuple-element.321.refs_0_, bf16[128,2048]{1,0:T(8,128)(2,1)S(1)} %collective-permute-done.72.refs_1_, ...), custom_call_target="tpu_custom_call" | custom-call | flops 1 | bytes 1 | tf_op jit(solution)/shard_map/pallas_call | solution.py:1109
  670.0 10.0 %collective-permute-done.86 = bf16[512,768]{1,0:T(8,128)(2,1)} collective-permute-done((bf16[512,768]{1,0:T(8,128)(2,1)}, bf16[512,768]{1,0:T(8,128)(2,1)}, u32[]{:S(2)}, u32[]{:S(2)}) %collective-permute-start.86) | collective-permute-done | bytes 786464 | tf_op jit(solution)/shard_map/ppermute | solution.py:130
  689.5 12.5 %collective-permute-done.87 = bf16[512,768]{1,0:T(8,128)(2,1)S(1)} collective-permute-done((bf16[512,768]{1,0:T(8,128)(2,1)S(1)}, bf16[512,768]{1,0:T(8,128)(2,1)S(1)}, u32[]{:S(2)}, u32[]{:S(2)}) %collective-permute-start.87) | collective-permute-done | bytes 786464 | tf_op jit(solution)/shard_map/ppermute | solution.py:130
  720.7 8.4 collective-permute-done.111
  733.7 12.2 %collective-permute-done.88 = bf16[128,2048]{1,0:T(8,128)(2,1)S(1)} collective-permute-done((bf16[128,2048]{1,0:T(8,128)(2,1)S(1)}, bf16[128,2048]{1,0:T(8,128)(2,1)S(1)}, u32[]{:S(2)}, u32[]{:S(2)}) %collective-permute-start.88) | collective-permute-done | bytes 524320 | tf_op jit(solution)/shard_map/ppermute | solution.py:130
  759.8 10.5 %collective-permute-done.89 = bf16[128,2048]{1,0:T(8,128)(2,1)S(1)} collective-permute-done((bf16[128,2048]{1,0:T(8,128)(2,1)S(1)}, bf16[128,2048]{1,0:T(8,128)(2,1)S(1)}, u32[]{:S(2)}, u32[]{:S(2)}) %collective-permute-start.89) | collective-permute-done | bytes 524320 | tf_op jit(solution)/shard_map/ppermute | solution.py:130
  841.8 7.8 shard_map.320
  (869 shorter events, 481.2 us)
Async XLA Ops:
  62.6 30.8 %collective-permute-start.16 = (bf16[512,768]{1,0:T(8,128)(2,1)}, bf16[512,768]{1,0:T(8,128)(2,1)}, u32[]{:S(2)}, u32[]{:S(2)}) collective-permute-start(bf16[512,768]{1,0:T(8,128)(2,1)} %collective-permute-done.10), channel_id=1, source_target_pairs={{0,1},{1,2},{2,3},{3,0},{4,5},{5,6},{6,7},{7,4},{8,9},{9,10},{10,1... | collective-permute-start | bytes 2359304 | tf_op jit(solution)/shard_map/ppermute | solution.py:130
  99.0 30.6 %collective-permute-start.21 = (bf16[512,768]{1,0:T(8,128)(2,1)}, bf16[512,768]{1,0:T(8,128)(2,1)}, u32[]{:S(2)}, u32[]{:S(2)}) collective-permute-start(bf16[512,768]{1,0:T(8,128)(2,1)} %collective-permute-done.16), channel_id=1, source_target_pairs={{0,1},{1,2},{2,3},{3,0},{4,5},{5,6},{6,7},{7,4},{8,9},{9,10},{10,1... | collective-permute-start | bytes 2359304 | tf_op jit(solution)/shard_map/ppermute | solution.py:130
  130.5 30.4 %all-to-all-start = ((bf16[8,64,2048]{2,1,0:T(8,128)(2,1)}), bf16[8,64,2048]{2,1,0:T(8,128)(2,1)S(1)}, u32[]{:S(2)}, u32[]{:S(2)}) async-start(bf16[8,64,2048]{2,1,0:T(8,128)(2,1)} %bitcast.24), calls=%async_computation | async-start | bytes 4194304 | tf_op jit(solution)/shard_map/all_to_all | solution.py:850
  162.4 50.2 %collective-permute-start.44 = (bf16[512,2048]{1,0:T(8,128)(2,1)}, bf16[512,2048]{1,0:T(8,128)(2,1)}, u32[]{:S(2)}, u32[]{:S(2)}) collective-permute-start(bf16[512,2048]{1,0:T(8,128)(2,1)} %constant_dynamic-update-slice_fusion.5.refs_5_), channel_id=1, source_target_pairs={{0,1},{1,2},{2,3},{3,0},{4,5},{5,6},{6,7},{7,4},{8,9},{9,10},{10,1... | collective-permute-start | bytes 6291464 | tf_op jit(solution)/shard_map/ppermute | solution.py:130
  183.1 30.4 %collective-permute-start.30 = (bf16[128,2048]{1,0:T(8,128)(2,1)S(1)}, bf16[128,2048]{1,0:T(8,128)(2,1)S(1)}, u32[]{:S(2)}, u32[]{:S(2)}) collective-permute-start(bf16[128,2048]{1,0:T(8,128)(2,1)S(1)} %pad_maximum_fusion.11), channel_id=1, source_target_pairs={{0,16},{4,20},{8,24},{12,28},{16,0},{20,4},{24,8},{28,12},{1,17},{... | collective-permute-start | bytes 1572872 | tf_op jit(solution)/shard_map/ppermute | solution.py:51
  212.6 93.8 %collective-permute-start.49 = (bf16[512,2048]{1,0:T(8,128)(2,1)}, bf16[512,2048]{1,0:T(8,128)(2,1)}, u32[]{:S(2)}, u32[]{:S(2)}) collective-permute-start(bf16[512,2048]{1,0:T(8,128)(2,1)} %collective-permute-done.44.refs_5_), channel_id=1, source_target_pairs={{0,1},{1,2},{2,3},{3,0},{4,5},{5,6},{6,7},{7,4},{8,9},{9,10},{10,1... | collective-permute-start | bytes 6291464 | tf_op jit(solution)/shard_map/ppermute | solution.py:130
  219.0 54.2 %collective-permute-start.35 = (bf16[128,2048]{1,0:T(8,128)(2,1)S(1)}, bf16[128,2048]{1,0:T(8,128)(2,1)}, u32[]{:S(2)}, u32[]{:S(2)}) collective-permute-start(bf16[128,2048]{1,0:T(8,128)(2,1)S(1)} %multiply_convert_fusion.refs_0_), channel_id=1, source_target_pairs={{0,1},{1,2},{2,3},{3,0},{4,5},{5,6},{6,7},{7,4},{8,9},{9,10},{10,1... | collective-permute-start | bytes 1572872 | tf_op jit(solution)/shard_map/ppermute | solution.py:130
  304.9 30.3 %collective-permute-start.38 = (bf16[320,2048]{1,0:T(8,128)(2,1)}, bf16[320,2048]{1,0:T(8,128)(2,1)}, u32[]{:S(2)}, u32[]{:S(2)}) collective-permute-start(bf16[320,2048]{1,0:T(8,128)(2,1)} %get-tuple-element.184), channel_id=1, source_target_pairs={{0,4},{4,0},{8,12},{12,8},{16,20},{20,16},{24,28},{28,24},{1,5},{5... | collective-permute-start | bytes 3932168 | tf_op jit(solution)/shard_map/ppermute | solution.py:51
  322.5 30.3 %collective-permute-start.43 = (bf16[128,2048]{1,0:T(8,128)(2,1)}, bf16[128,2048]{1,0:T(8,128)(2,1)S(1)}, u32[]{:S(2)}, u32[]{:S(2)}) collective-permute-start(bf16[128,2048]{1,0:T(8,128)(2,1)} %collective-permute-done.41.refs_0_), channel_id=1, source_target_pairs={{0,16},{4,20},{8,24},{12,28},{16,0},{20,4},{24,8},{28,12},{1,17},{... | collective-permute-start | bytes 1572872 | tf_op jit(solution)/shard_map/ppermute | solution.py:51
  322.8 30.0 %collective-permute-start.42 = (bf16[128,2048]{1,0:T(8,128)(2,1)}, bf16[128,2048]{1,0:T(8,128)(2,1)S(1)}, u32[]{:S(2)}, u32[]{:S(2)}) collective-permute-start(bf16[128,2048]{1,0:T(8,128)(2,1)} %collective-permute-done.41.refs_0_), channel_id=1, source_target_pairs={{0,8},{4,12},{8,0},{12,4},{16,24},{20,28},{24,16},{28,20},{1,9},{5... | collective-permute-start | bytes 1572872 | tf_op jit(solution)/shard_map/ppermute | solution.py:51
  324.5 35.8 %collective-permute-start.48 = (bf16[128,2048]{1,0:T(8,128)(2,1)}, bf16[128,2048]{1,0:T(8,128)(2,1)S(1)}, u32[]{:S(2)}, u32[]{:S(2)}) collective-permute-start(bf16[128,2048]{1,0:T(8,128)(2,1)} %collective-permute-done.41.refs_0_), channel_id=1, source_target_pairs={{0,1},{1,2},{2,3},{3,0},{4,5},{5,6},{6,7},{7,4},{8,9},{9,10},{10,1... | collective-permute-start | bytes 1572872 | tf_op jit(solution)/shard_map/ppermute | solution.py:130
  471.9 61.1 %collective-permute-start.63 = (bf16[384,2048]{1,0:T(8,128)(2,1)}, bf16[384,2048]{1,0:T(8,128)(2,1)}, u32[]{:S(2)}, u32[]{:S(2)}) collective-permute-start(bf16[384,2048]{1,0:T(8,128)(2,1)} %pad_maximum_fusion.4), channel_id=1, source_target_pairs={{0,16},{4,20},{8,24},{12,28},{16,0},{20,4},{24,8},{28,12},{1,17},{... | collective-permute-start | bytes 4718600 | tf_op jit(solution)/shard_map/ppermute | solution.py:51
  475.3 57.7 %collective-permute-start.62 = (bf16[384,2048]{1,0:T(8,128)(2,1)}, bf16[384,2048]{1,0:T(8,128)(2,1)}, u32[]{:S(2)}, u32[]{:S(2)}) collective-permute-start(bf16[384,2048]{1,0:T(8,128)(2,1)} %pad_maximum_fusion.3), channel_id=1, source_target_pairs={{0,8},{4,12},{8,0},{12,4},{16,24},{20,28},{24,16},{28,20},{1,9},{5... | collective-permute-start | bytes 4718600 | tf_op jit(solution)/shard_map/ppermute | solution.py:51
  477.7 40.0 %collective-permute-start.66 = (bf16[64,2048]{1,0:T(8,128)(2,1)S(1)}, bf16[64,2048]{1,0:T(8,128)(2,1)S(1)}, u32[]{:S(2)}, u32[]{:S(2)}) collective-permute-start(bf16[64,2048]{1,0:T(8,128)(2,1)S(1)} %get-tuple-element.354), channel_id=1, source_target_pairs={{0,8},{4,12},{8,0},{12,4},{16,24},{20,28},{24,16},{28,20},{1,9},{5... | collective-permute-start | bytes 786440 | tf_op jit(solution)/shard_map/ppermute | solution.py:51
  479.1 38.6 %collective-permute-start.65 = (bf16[64,2048]{1,0:T(8,128)(2,1)S(1)}, bf16[64,2048]{1,0:T(8,128)(2,1)S(1)}, u32[]{:S(2)}, u32[]{:S(2)}) collective-permute-start(bf16[64,2048]{1,0:T(8,128)(2,1)S(1)} %get-tuple-element.355), channel_id=1, source_target_pairs={{0,16},{4,20},{8,24},{12,28},{16,0},{20,4},{24,8},{28,12},{1,17},{... | collective-permute-start | bytes 786440 | tf_op jit(solution)/shard_map/ppermute | solution.py:51
  602.6 39.7 %collective-permute-start.81 = (bf16[256,2048]{1,0:T(8,128)(2,1)}, bf16[256,2048]{1,0:T(8,128)(2,1)}, u32[]{:S(2)}, u32[]{:S(2)}) collective-permute-start(bf16[256,2048]{1,0:T(8,128)(2,1)} %get-tuple-element.268), channel_id=1, source_target_pairs={{0,16},{4,20},{8,24},{12,28},{16,0},{20,4},{24,8},{28,12},{1,17},{... | collective-permute-start | bytes 3145736 | tf_op jit(solution)/shard_map/ppermute | solution.py:51
  602.7 39.5 %collective-permute-start.82 = (bf16[256,2048]{1,0:T(8,128)(2,1)}, bf16[256,2048]{1,0:T(8,128)(2,1)}, u32[]{:S(2)}, u32[]{:S(2)}) collective-permute-start(bf16[256,2048]{1,0:T(8,128)(2,1)} %get-tuple-element.269), channel_id=1, source_target_pairs={{0,8},{4,12},{8,0},{12,4},{16,24},{20,28},{24,16},{28,20},{1,9},{5... | collective-permute-start | bytes 3145736 | tf_op jit(solution)/shard_map/ppermute | solution.py:51
  636.1 32.6 %all-to-all-start.1 = ((bf16[8,64,2048]{2,1,0:T(8,128)(2,1)}), bf16[8,64,2048]{2,1,0:T(8,128)(2,1)}, u32[]{:S(2)}, u32[]{:S(2)}) async-start(bf16[8,64,2048]{2,1,0:T(8,128)(2,1)} %bitcast.228), calls=%async_computation.1 | async-start | bytes 4194304 | tf_op jit(solution)/shard_map/all_to_all | solution.py:1106
  665.1 48.8 %collective-permute-start.84 = (bf16[512,2048]{1,0:T(8,128)(2,1)}, bf16[512,2048]{1,0:T(8,128)(2,1)}, u32[]{:S(2)}, u32[]{:S(2)}) collective-permute-start(bf16[512,2048]{1,0:T(8,128)(2,1)} %pad_maximum_fusion.1), channel_id=1, source_target_pairs={{0,16},{4,20},{8,24},{12,28},{16,0},{20,4},{24,8},{28,12},{1,17},{... | collective-permute-start | bytes 6291464 | tf_op jit(solution)/shard_map/ppermute | solution.py:51
  667.1 48.8 %collective-permute-start.83 = (bf16[512,2048]{1,0:T(8,128)(2,1)}, bf16[512,2048]{1,0:T(8,128)(2,1)}, u32[]{:S(2)}, u32[]{:S(2)}) collective-permute-start(bf16[512,2048]{1,0:T(8,128)(2,1)} %pad_maximum_fusion), channel_id=1, source_target_pairs={{0,8},{4,12},{8,0},{12,4},{16,24},{20,28},{24,16},{28,20},{1,9},{5... | collective-permute-start | bytes 6291464 | tf_op jit(solution)/shard_map/ppermute | solution.py:51
  685.6 69.6 %collective-permute-start.91 = (bf16[512,2048]{1,0:T(8,128)(2,1)}, bf16[512,2048]{1,0:T(8,128)(2,1)}, u32[]{:S(2)}, u32[]{:S(2)}) collective-permute-start(bf16[512,2048]{1,0:T(8,128)(2,1)} %convolution_convert_fusion.1), channel_id=1, source_target_pairs={{0,4},{4,0},{8,12},{12,8},{16,20},{20,16},{24,28},{28,24},{1,5},{5... | collective-permute-start | bytes 6291464 | tf_op jit(solution)/shard_map/ppermute | solution.py:51
  703.3 50.5 %collective-permute-start.106 = (bf16[512,768]{1,0:T(8,128)(2,1)}, bf16[512,768]{1,0:T(8,128)(2,1)}, u32[]{:S(2)}, u32[]{:S(2)}) collective-permute-start(bf16[512,768]{1,0:T(8,128)(2,1)} %get-tuple-element.315), channel_id=1, source_target_pairs={{0,4},{4,0},{8,12},{12,8},{16,20},{20,16},{24,28},{28,24},{1,5},{5... | collective-permute-start | bytes 2359304 | tf_op jit(solution)/shard_map/ppermute | solution.py:51
  752.7 31.7 %collective-permute-start.108 = (bf16[512,768]{1,0:T(8,128)(2,1)S(1)}, bf16[512,768]{1,0:T(8,128)(2,1)S(1)}, u32[]{:S(2)}, u32[]{:S(2)}) collective-permute-start(bf16[512,768]{1,0:T(8,128)(2,1)S(1)} %collective-permute-done.103), channel_id=1, source_target_pairs={{0,4},{4,0},{8,12},{12,8},{16,20},{20,16},{24,28},{28,24},{1,5},{5... | collective-permute-start | bytes 2359304 | tf_op jit(solution)/shard_map/ppermute | solution.py:51
  784.6 45.4 %collective-permute-start.118 = (bf16[128,2048]{1,0:T(8,128)(2,1)}, bf16[128,2048]{1,0:T(8,128)(2,1)}, u32[]{:S(2)}, u32[]{:S(2)}) collective-permute-start(bf16[128,2048]{1,0:T(8,128)(2,1)} %get-tuple-element.313), channel_id=1, source_target_pairs={{0,4},{4,0},{8,12},{12,8},{16,20},{20,16},{24,28},{28,24},{1,5},{5... | collective-permute-start | bytes 1572872 | tf_op jit(solution)/shard_map/ppermute | solution.py:51
  (282 other events, 3629.7 us)

commit v3 on v2

--- a/solution.py
+++ b/solution.py
@@ -16,7 +16,7 @@
 SMEM_SPEC = pl.BlockSpec(memory_space=pltpu.SMEM)
 QUERY_ROWS = 128
 KEY_ROWS = 256
-ATTEND_LIMIT = 40 << 20
+ATTEND_LIMIT = 60 << 20
 COST = pl.CostEstimate(flops=1, bytes_accessed=1, transcendentals=0)
 
 
@@ -36,9 +36,9 @@
     return jax.nn.silu(gate_pre) * up_pre
 
 
-def rope_tables(length, head_width):
+def rope_tables(length, head_width, zero):
     inv_freq = ROPE_BASE ** (-jnp.arange(0, head_width // 2, dtype=F32) * 2.0 / head_width)
-    angle_table = jnp.arange(length, dtype=F32)[:, None] * inv_freq[None, :]
+    angle_table = (jnp.arange(length, dtype=F32) + zero)[:, None] * inv_freq[None, :]
     cosine, sine = jnp.cos(angle_table), jnp.sin(angle_table)
     return jnp.concatenate([cosine, cosine], 1), jnp.concatenate([-sine, sine], 1)
 
@@ -84,45 +84,73 @@
     return mine + [swap(piece, 1) for piece in mine]
 
 
-def diag_sends(diag):
-    half = diag.shape[0] // 2
-    return swap(diag[:half], 4), swap(diag[half:], 2)
+def sum_kernel(*refs):
+    total = refs[0][...].astype(F32)
+    for ref in refs[1:-1]:
+        total = total + ref[...].astype(F32)
+    refs[-1][...] = total.astype(refs[-1].dtype)
+
+
+def sum_of(values, kind, limit=24):
+    return pl.pallas_call(
+        sum_kernel,
+        out_shape=jax.ShapeDtypeStruct(values[0].shape, kind),
+        in_specs=[VMEM_SPEC] * len(values),
+        out_specs=VMEM_SPEC,
+        compiler_params=pltpu.CompilerParams(vmem_limit_bytes=limit << 20),
+        cost_estimate=COST,
+    )(*values)
+
+
+def add_diag_kernel(part_x_ref, part_y_ref, from_y_ref, from_x_ref, out_x_ref, out_y_ref):
+    half = from_y_ref.shape[0]
+    low = lambda a, b: (a.astype(F32) + b.astype(F32)).astype(BF)
+    out_x_ref[:half] = low(part_x_ref[:half], from_y_ref[...])
+    out_x_ref[half:] = part_x_ref[half:].astype(BF)
+    out_y_ref[:half] = part_y_ref[:half].astype(BF)
+    out_y_ref[half:] = low(part_y_ref[half:], from_x_ref[...])
 
 
 def add_diag(part_x, part_y, from_y, from_x):
-    half = from_y.shape[0]
-    part_x, part_y = part_x.astype(F32), part_y.astype(F32)
-    part_x = jnp.concatenate([part_x[:half] + from_y.astype(F32), part_x[half:]], 0).astype(BF)
-    part_y = jnp.concatenate([part_y[:half], part_y[half:] + from_x.astype(F32)], 0).astype(BF)
-    return part_x, part_y
-
-
-def plane_sum(own, part_x, part_y, diag):
-    part_x, part_y = add_diag(part_x, part_y, *diag_sends(diag))
-    return own.astype(F32) + swap(part_x, 2).astype(F32) + swap(part_y, 4).astype(F32)
-
-
-def plane_scatter(multiply, left, fill=None, *others):
+    return pl.pallas_call(
+        add_diag_kernel,
+        out_shape=(jax.ShapeDtypeStruct(part_x.shape, BF),) * 2,
+        in_specs=[VMEM_SPEC] * 4,
+        out_specs=[VMEM_SPEC] * 2,
+        compiler_params=pltpu.CompilerParams(vmem_limit_bytes=24 << 20),
+        cost_estimate=COST,
+    )(part_x, part_y, from_y, from_x)
+
+
+def plane_scatter(multiply, left, fill=None, others=(), last=()):
     count = lax.axis_size("ctx")
     if count != 8:
-        parts = multiply(left).astype(BF)
+        parts = multiply(left, BF)
         return lax.psum_scatter(parts, "ctx", scatter_dimension=0, tiled=True).astype(F32)
     side = left.shape[0] // 2
     rows = side // 4
-    give = multiply(left[side:]).astype(BF)
+    half = rows // 2
+    give = multiply(left[side:], BF)
     got = swap(give, 1)
-    keep = multiply(after(left[:side], give))
-    kept = keep + after(got, keep).astype(F32)
-    if others:
-        kept = after(kept, *others)
-    diag = kept[3 * rows :].astype(BF)
-    half = rows // 2
-    sends = diag[:half], diag[half:]
+    keep = multiply(after(left[:side], give), BF)
+    kept = sum_of(after([keep, got], others), BF)
+    sends = kept[3 * rows : -half], kept[-half:]
     from_y, from_x = swap(sends[0], 4), swap(sends[1], 2)
-    if fill is not None:
-        from_y, from_x = after((from_y, from_x), fill(sends))
+    from_y, from_x = after((from_y, from_x), fill(sends))
     part_x, part_y = add_diag(kept[rows : 2 * rows], kept[2 * rows : 3 * rows], from_y, from_x)
-    return kept[:rows] + swap(part_x, 2).astype(F32) + swap(part_y, 4).astype(F32)
+    got = after((swap(part_x, 2), swap(part_y, 4)), last)
+    return kept[:rows].astype(F32) + got[0].astype(F32) + got[1].astype(F32)
+
+
+class Order:
+    def __init__(self, *values):
+        self.last = values
+
+    def take(self, value):
+        return after(value, *self.last)
+
+    def give(self, *values):
+        self.last = values
 
 
 def ring(value):
@@ -488,11 +516,13 @@
     )(*pieces, *others, target)
 
 
-def spread_kernel(chunks, part, *refs):
+def spread_kernel(chunks, part, grouped, *refs):
     mine_refs, other_refs = refs[:chunks], refs[chunks : 2 * chunks]
-    target_ref, own_ref, x_ref, y_ref, diag_ref = refs[2 * chunks :]
+    target_ref, first_ref, second_ref = refs[2 * chunks : 2 * chunks + 3]
+    outs = refs[2 * chunks + 3 :]
     slots = mine_refs[0].shape[0] // 2
-    rows = own_ref.shape[0] // chunks
+    half = first_ref.shape[0] // chunks
+    rows = 2 * half
     spot = slice(part * slots, (part + 1) * slots)
     for j in range(chunks):
         values = jnp.concatenate([mine_refs[j][spot], other_refs[j][spot]], axis=0)
@@ -500,23 +530,34 @@
         index = lax.broadcasted_iota(jnp.int32, (4 * rows, 2 * slots), 1)
         pick = one_hot((index == target[:, 0:1]) | (index == target[:, 1:2]))
         spread = jnp.dot(pick, values, preferred_element_type=F32).astype(BF)
-        for k, ref in enumerate((own_ref, x_ref, y_ref, diag_ref)):
-            ref[j * rows : (j + 1) * rows] = spread[k * rows : (k + 1) * rows]
-
-
-def spread_rows(mine, other, target, rows, part):
+        for k in range(3):
+            ref, start = (outs[k], j * rows) if grouped else (outs[3 * j + k], 0)
+            ref[start : start + rows] = spread[k * rows : (k + 1) * rows]
+        if grouped:
+            ref = first_ref if 2 * j < chunks else second_ref
+            start = j % (chunks // 2) * rows
+            ref[start : start + rows] = spread[3 * rows :]
+        else:
+            first_ref[j * half : (j + 1) * half] = spread[3 * rows : 3 * rows + half]
+            second_ref[j * half : (j + 1) * half] = spread[3 * rows + half :]
+
+
+def spread_rows(mine, other, target, rows, part, grouped):
     chunks = len(mine)
     slots, width = mine[0].shape
-    return pl.pallas_call(
-        functools.partial(spread_kernel, chunks, part),
-        out_shape=(jax.ShapeDtypeStruct((chunks * rows, width), BF),) * 4,
+    low = lambda count: jax.ShapeDtypeStruct((count, width), BF)
+    blocks = (low(chunks * rows),) * 3 if grouped else (low(rows),) * (3 * chunks)
+    outs = pl.pallas_call(
+        functools.partial(spread_kernel, chunks, part, grouped),
+        out_shape=(low(chunks * rows // 2),) * 2 + blocks,
         in_specs=[VMEM_SPEC] * (2 * chunks + 1),
-        out_specs=[VMEM_SPEC] * 4,
+        out_specs=[VMEM_SPEC] * (2 + len(blocks)),
         compiler_params=pltpu.CompilerParams(
             vmem_limit_bytes=(16 << 20) if chunks == 1 else (36 << 20)
         ),
         cost_estimate=COST,
     )(*mine, *other, target)
+    return outs[:2], outs[2:]
 
 
 def expert_kernel(expert_ref, mine_ref, other_ref, *refs):
@@ -675,7 +716,7 @@
             jax.ShapeDtypeStruct((rows, dim * count // share), F32),
             jax.ShapeDtypeStruct((rows, dim * count // share), F32),
         ),
-        compiler_params=pltpu.CompilerParams(vmem_limit_bytes=20 << 20),
+        compiler_params=pltpu.CompilerParams(vmem_limit_bytes=ATTEND_LIMIT),
         cost_estimate=COST,
     )(order, owner, parts)
 
@@ -697,9 +738,113 @@
             ),
         ),
         out_shape=jax.ShapeDtypeStruct((chunks, count, rows, width), F32),
-        compiler_params=pltpu.CompilerParams(vmem_limit_bytes=20 << 20),
+        compiler_params=pltpu.CompilerParams(vmem_limit_bytes=ATTEND_LIMIT),
         cost_estimate=COST,
     )(owner, parts)
+
+
+def place_pieces_kernel(share, owner_ref, *refs):
+    pieces, (query_ref, key_ref, value_ref) = refs[:-3], refs[-3:]
+    rows, dim = query_ref.shape[0], key_ref.shape[1] * share // 8
+    cols = query_ref.shape[1] // 8
+    for k in range(4):
+        both = [
+            [ref[...].astype(F32) for ref in refs_of]
+            for refs_of in (block_refs(pieces, k), block_refs(pieces, k + 4))
+        ]
+        both = [p[0] if len(p) == 1 else jnp.concatenate(p, axis=0) for p in both]
+        for side in range(2):
+            start = pl.multiple_of(owner_ref[k + 4 * side] * cols, cols)
+            query_ref[:, pl.ds(start, cols)] = both[side][:, :cols]
+        start = pl.multiple_of(owner_ref[k] // share * dim, dim)
+        key_ref[:, pl.ds(start, dim)] = both[0][:, cols : cols + dim] + both[1][:, cols : cols + dim]
+        value_ref[:, pl.ds(start, dim)] = both[0][:, cols + dim :] + both[1][:, cols + dim :]
+
+
+def block_refs(pieces, k):
+    first = k // 4 * 5 + k % 4
+    return pieces[first : first + 2] if k % 4 == 3 else pieces[first : first + 1]
+
+
+def place_weight_pieces(pieces, owner, share, dim):
+    rows, width = pieces[0].shape
+    cols = width - 2 * dim
+    return pl.pallas_call(
+        functools.partial(place_pieces_kernel, share),
+        out_shape=(
+            jax.ShapeDtypeStruct((rows, cols * 8), F32),
+            jax.ShapeDtypeStruct((rows, dim * 8 // share), F32),
+            jax.ShapeDtypeStruct((rows, dim * 8 // share), F32),
+        ),
+        in_specs=[SMEM_SPEC] + [VMEM_SPEC] * len(pieces),
+        out_specs=[VMEM_SPEC] * 3,
+        compiler_params=pltpu.CompilerParams(vmem_limit_bytes=ATTEND_LIMIT),
+        cost_estimate=COST,
+    )(owner, *pieces)
+
+
+def row_pieces_kernel(owner_ref, *refs):
+    pieces, out_ref = refs[:-1], refs[-1]
+    chunks, _, rows, _ = out_ref.shape
+    for k in range(8):
+        parts = [ref[...] for ref in block_refs(pieces, k)]
+        part = parts[0] if len(parts) == 1 else jnp.concatenate(parts, axis=0)
+        for chunk in range(chunks):
+            out_ref[chunk, owner_ref[k]] = part[chunk * rows : (chunk + 1) * rows].astype(F32)
+
+
+def place_row_pieces(pieces, owner, chunks):
+    rows, width = pieces[0].shape
+    return pl.pallas_call(
+        row_pieces_kernel,
+        out_shape=jax.ShapeDtypeStruct((chunks, 8, rows // chunks, width), F32),
+        in_specs=[SMEM_SPEC] + [VMEM_SPEC] * len(pieces),
+        out_specs=VMEM_SPEC,
+        compiler_params=pltpu.CompilerParams(vmem_limit_bytes=ATTEND_LIMIT),
+        cost_estimate=COST,
+    )(owner, *pieces)
+
+
+def product_kernel(dims, rows, left_count, right_count, starts, start_ref, *refs):
+    lefts, rights = refs[:left_count], refs[left_count : left_count + right_count]
+    outs = refs[left_count + right_count :]
+    join = lambda parts: parts[0] if len(parts) == 1 else jnp.concatenate(parts, axis=0)
+    right = join([ref[...] for ref in rights])
+    for k, out_ref in enumerate(outs):
+        if starts:
+            width = out_ref.shape[0]
+            cols = pl.ds(pl.multiple_of(start_ref[k] * width, width), width)
+            left = join([ref[:, cols] for ref in lefts])
+        else:
+            left = join([ref[...] if rows is None else ref[:rows] for ref in lefts])
+        out = lax.dot_general(left, right, (dims, ((), ())), preferred_element_type=F32)
+        out_ref[...] = out.astype(out_ref.dtype)
+
+
+def product(lefts, rights, dims, out_shape, kind=F32, rows=None, starts=None, limit=60, tile=None):
+    count = 1 if starts is None else starts.shape[0]
+    start_arg = jnp.zeros((1,), jnp.int32) if starts is None else starts
+    if tile is None:
+        left_specs, right_specs = [VMEM_SPEC] * len(lefts), [VMEM_SPEC] * len(rights)
+        out_spec = VMEM_SPEC
+    else:
+        left_specs = [
+            pl.BlockSpec((rows or left.shape[0], tile), lambda i: (0, i)) for left in lefts
+        ]
+        right_specs = [pl.BlockSpec(right.shape, lambda i: (0, 0)) for right in rights]
+        out_spec = pl.BlockSpec((tile, out_shape[1]), lambda i: (i, 0))
+    outs = pl.pallas_call(
+        functools.partial(
+            product_kernel, dims, None, len(lefts), len(rights), starts is not None
+        ),
+        grid=() if tile is None else (out_shape[0] // tile,),
+        out_shape=(jax.ShapeDtypeStruct(out_shape, kind),) * count,
+        in_specs=[SMEM_SPEC] + left_specs + right_specs,
+        out_specs=[out_spec] * count,
+        compiler_params=pltpu.CompilerParams(vmem_limit_bytes=limit << 20),
+        cost_estimate=COST,
+    )(start_arg, *lefts, *rights)
+    return outs[0] if starts is None else outs
 
 
 def move_slots(slot_array):
@@ -744,7 +889,7 @@
     group = me // share
     shard_width = model_width // wt_count
     capacity = max(2, half_rows * top_count * 5 // (4 * experts))
-    dense = ctx_count == 8 and w_gate.shape[0] == 1
+    dense = ctx_count == 8 and wt_count == 4 and w_gate.shape[0] == 1
     nt = (((1,), (1,)), ((), ()))
     tn = (((0,), (0,)), ((), ()))
     owners = block_owner(ctx_count, me)
@@ -797,56 +942,66 @@
             counts = jnp.sum((near[None] == indices).astype(F32), axis=(1, 2, 3, 4))
             return own_slot, target, target.transpose(0, 2, 1), near_routes, counts
 
-        near = routes[0].T.astype(BF)
+        block_rows = own_chunks * piece_rows
+        out_piece = out_piece.reshape(block_rows, model_width)
+        ticks = [(out_piece, own_weight), (ring(out_piece), ring(own_weight))]
+        own = after(normed_low, out_piece, own_weight)
+        via_x, via_y = swap(own, 2), swap(own, 4)
+        near = after(routes[0].T.astype(BF), own)
         near_x, near_y = swap(near, 2), swap(near, 4)
+        sent = via_x[:half_rows], via_y[half_rows:]
+        diag_a, diag_b = swap(sent[0], 4), swap(sent[1], 2)
+        near_x, near_y = after((near_x, near_y), sent)
         near = jnp.concatenate([near, near_x, near_y, swap(near_x, 4)], axis=0)
         near = jnp.concatenate([near, swap(near, 1)], axis=0)
-        via_x, via_y = swap(normed_low, 2), swap(normed_low, 4)
-        router_rows = w_router.T.reshape(-1, model_width)
-        block_rows = own_chunks * piece_rows
-        shard = jnp.concatenate([out_piece.reshape(block_rows, model_width), router_rows], axis=0)
-        out_pieces = jnp.zeros((ctx_count * piece_rows, model_width), BF)
-        router = jnp.zeros((wt_count,) + router_rows.shape, BF)
-        weight = jnp.zeros((model_width, own_weight.shape[1]), BF)
-
-        def keep(j, out_pieces, router, weight, shard, own_weight):
-            put = lax.dynamic_update_slice_in_dim
-            return (
-                put(out_pieces, shard[:block_rows], planes[j] * block_rows, 0),
-                put(router, shard[None, block_rows:], planes[j], 0),
-                put(weight, own_weight, planes[j] * shard_width, 0),
-            )
-
-        ticks = [(shard, own_weight), (ring(shard), ring(own_weight))]
-        diag_a, diag_b = swap(via_x[:half_rows], 4), swap(via_y[half_rows:], 2)
-        hidden_pieces = [normed_low, via_x, via_y, diag_a, diag_b]
+        hidden_pieces = [own, via_x, via_y, diag_a, diag_b]
         hidden_pieces = hidden_pieces + [swap(piece, 1) for piece in hidden_pieces]
         ticks[1], near, cot_block = after((ticks[1], near, cot), ticks[1], hidden_pieces, near)
-        nears = [near, ring(near)]
+        near_rows = near.shape[0]
+        tiny = jnp.concatenate([near, w_router.T.reshape(-1, tok_rows)], axis=0)
+        tinies = [tiny, ring(tiny)]
         cot_x, cot_y = swap(cot_block, 2), swap(cot_block, 4)
         ticks.append((ring(ticks[1][0]), ring(ticks[1][1])))
         first_tables = tables(near)
-        ticks[2], cot_x, cot_y, nears[1] = after(
-            (ticks[2], cot_x, cot_y, nears[1]), ticks[2], cot_x, cot_y, nears[1], first_tables
-        )
-        nears.append(ring(nears[1]))
+        zero = ticks[1][0][0, 0].astype(F32) * 0.0
+        tables_done = cosine, sine = rope_tables(seq_len, head_dim, zero)
+        def keep(j, buffers, shards):
+            put = lax.dynamic_update_slice_in_dim
+            return (
+                put(buffers[0], shards[0], planes[j] * block_rows, 0),
+                put(buffers[1], shards[1], planes[j] * shard_width, 0),
+            )
+
         cot_sent = cot_x[:half_rows], cot_y[half_rows:]
+        ticks[2], cot_sent, tinies[1] = after(
+            (ticks[2], cot_sent, tinies[1]), ticks[2], cot_sent, tinies[1], first_tables, tables_done
+        )
+        ticks.append((ring(ticks[2][0]), ring(ticks[2][1])))
+        tinies.append(ring(tinies[1]))
         diag_a, diag_b = swap(cot_sent[0], 4), swap(cot_sent[1], 2)
-        ticks.append((ring(ticks[2][0]), ring(ticks[2][1])))
-        for j in range(wt_count - 1):
-            out_pieces, router, weight = keep(j, out_pieces, router, weight, *ticks[j])
-        cot_all = jnp.concatenate([cot, cot_x, cot_y, diag_a, diag_b], axis=0)
-        ticks[3] = after(ticks[3], cot_all, nears[2], weight, out_pieces)
-        out_pieces, router, weight = keep(3, out_pieces, router, weight, *ticks[3])
-        router = router.reshape(wt_count, experts, shard_width).transpose(1, 0, 2)
-        router = router.reshape(experts, model_width)
-        nears.append(ring(after(nears[2], weight)))
-        cots = [cot_all, ring(after(cot_all, weight))]
+        seed = ticks[2][0][:1, :1] * 0
+        buffers = (
+            jnp.broadcast_to(seed, (ctx_count * piece_rows, model_width)),
+            jnp.broadcast_to(seed, (model_width, own_weight.shape[1])),
+        )
+
+        for j in range(3):
+            buffers = keep(j, buffers, ticks[j])
+        cot_pieces = [cot, cot_x, cot_y, diag_a, diag_b]
+        cot_diag = jnp.concatenate([diag_a, diag_b], axis=0)
+        ticks[3] = after(ticks[3], cot_diag, tinies[2], buffers)
+        out_pieces, weight = keep(3, buffers, ticks[3])
+        tinies.append(ring(after(tinies[2], weight)))
+        cot_next = [ring(after(p, weight)) for p in (cot, cot_x, cot_y, cot_diag)]
+        nears = [tiny[:near_rows] for tiny in tinies]
+        router = jnp.stack([tiny[near_rows:].reshape(experts, shard_width) for tiny in tinies])
+        router = router[planes].transpose(1, 0, 2).reshape(experts, model_width)
     else:
         hidden_pieces = plane_gather(normed_low)
         out_pieces = lax.all_gather(out_piece, "wt", axis=0, tiled=True)
         weight = lax.all_gather(own_weight, "wt", axis=0, tiled=True)
         router = lax.all_gather(w_router, "wt", axis=0, tiled=True).T
+        cosine, sine = rope_tables(seq_len, head_dim, 0.0)
     out_weight = lax.all_to_all(
         out_pieces.reshape(ctx_count, piece_rows, model_width), "ctx", 0, 0, tiled=True
     ).reshape(head_cols, model_width)
@@ -861,7 +1016,6 @@
         (seg[None, :] < seg[::QUERY_ROWS][:, None]).astype(jnp.int32), axis=1
     ).astype(jnp.int32)
     seg_row, seg_col = seg.reshape(1, seq_len), seg.reshape(seq_len, 1)
-    cosine, sine = rope_tables(seq_len, head_dim)
     query_gain_row, key_gain_row = query_gain.reshape(1, -1), key_gain.reshape(1, -1)
 
     width = head_cols + 2 * head_dim
@@ -896,15 +1050,21 @@
     )
     attn_rows = attn_low.reshape(seq_len, head_cols)
     later_tables = []
-
-    def fill(sends):
-        if dense:
+    out_project = lambda rows, kind: low_matmul(rows, out_weight).astype(kind)
+    if dense:
+        attn_rows = after(attn_rows, cot_next[:2])
+        out_project = lambda rows, kind: product(
+            [rows], [out_weight], ((1,), (0,)), (rows.shape[0], model_width), kind
+        )
+
+        def fill(sends):
             later_tables.extend(tables(after(jnp.concatenate(nears[1:], axis=0), sends)))
-        return tuple(later_tables)
-
-    residual = inputs + plane_scatter(
-        lambda rows: low_matmul(rows, out_weight), attn_rows, fill
-    )
+            return tuple(later_tables) + (cot_next[2],)
+
+        attn = plane_scatter(out_project, attn_rows, fill, (), (cot_next[3],))
+    else:
+        attn = plane_scatter(out_project, attn_rows)
+    residual = inputs + attn
     normed_two, ffn_back = jax.vjp(rms_norm, residual, ffn_gain)
     normed_two_low = normed_two.astype(BF)
     grad_out = cotangent[0].astype(F32)
@@ -924,10 +1084,10 @@
         last = wt_count - 1
         mine_backs, other_backs, results = [], [], []
 
-        def compute(j, pieces, others, gates):
+        def compute(j, pieces, others, gates, second=()):
             pieces = after(pieces, *gates)
             mine, other = select_rows(pieces, others, target_rows[j], slots)
-            received = swap(other, 1)
+            received = after(swap(other, 1), second)
             result = expert_rows(
                 expert.reshape(1),
                 mine,
@@ -941,70 +1101,83 @@
             )
             mine_backs.append(result[0])
             other_backs.append(swap(result[1], 1))
-            results.append((mine[:slots], received[:slots]) + tuple(result[2:]))
+            results.append((mine, received) + tuple(result[2:]))
             return result[0]
 
-        chunk, pieces, done = normed_two_low, None, None
+        payload, before, done = normed_two_low, None, None
         for j in range(wt_count):
+            if j == 2:
+                cot_own = cot_next[0]
+                halves = payload[:half_rows], cot_own[:half_rows], payload[half_rows:], cot_own[half_rows:]
+                payload = jnp.concatenate(halves, axis=0)
             if j > 0:
-                chunk = ring(chunk)
-            payload = chunk
-            if j == last:
-                cot_last = ring(cots[j - 1][:tok_rows])
-                halves = chunk[:half_rows], cot_last[:half_rows], chunk[half_rows:], cot_last[half_rows:]
-                payload = jnp.concatenate(halves, axis=0)
-            elif j > 1:
-                cots.append(ring(cots[-1]))
-            if j > 0:
-                payload = after(payload, sent)
-            via_x, via_y = swap(payload, 2), swap(payload, 4)
+                payload = ring(payload)
+            block = payload if j == 0 else after(payload, before[3:])
+            via_x, via_y = swap(block, 2), swap(block, 4)
             if done is not None:
                 via_x, via_y = after((via_x, via_y), done)
             middle = via_x.shape[0] // 2
             sent = via_x[:middle], via_y[middle:]
-            before, pieces = pieces, [payload, via_x, via_y, swap(sent[0], 4), swap(sent[1], 2)]
+            pieces = [block, via_x, via_y, swap(sent[0], 4), swap(sent[1], 2)]
             if before is not None:
-                done = compute(j - 1, before, [cots[j - 1]], (sent,))
-        parts = spread_rows(mine_backs, other_backs, target_cols[:last], tok_rows, 0)
-        half = parts[3].shape[0] // 2
-        group_sent = parts[3][:half], parts[3][half:]
+                done = compute(j - 1, before, [cot_pieces, cot_next, []][j - 1], (sent,), pieces[3:])
+            before = pieces
+        group_sent, blocks = spread_rows(
+            mine_backs, other_backs, target_cols[:last], tok_rows, 0, False
+        )
+        group_sent = after(group_sent, sent)
         group_diag = swap(group_sent[0], 4), swap(group_sent[1], 2)
-        done = compute(last, pieces, [], (group_sent,))
-        group_x, group_y = add_diag(*after((parts[1], parts[2]), done), *after(group_diag, done))
-        got_x, got_y = swap(group_x, 2), swap(group_y, 4)
-        tail = spread_rows(
-            mine_backs[last:], other_backs[last:], after(target_cols[last:], group_x, group_y), tok_rows, 0
-        )
-        tail_sent = tail[3][:half_rows], tail[3][half_rows:]
+        done = compute(last, pieces, [], (done,), group_sent)
+        step = Order(done)
+
+        def add_chunk(own, part_x, part_y, from_y, from_x):
+            part_x, part_y, from_y, from_x = step.take((part_x, part_y, from_y, from_x))
+            part_x, part_y = add_diag(part_x, part_y, from_y, from_x)
+            step.give(part_x, part_y)
+            return own, swap(part_x, 2), swap(part_y, 4)
+
+        def chunk_sum(own, got_x, got_y):
+            return [own] + list(step.take((got_x, got_y)))
+
+        def chunk_diag(j):
+            return [part[j * half_rows : (j + 1) * half_rows] for part in group_diag]
+
+        partial = {j: add_chunk(*blocks[3 * j : 3 * j + 3], *chunk_diag(j)) for j in range(1, last)}
+        tail_sent, tail = spread_rows(
+            step.take(mine_backs[last:]), other_backs[last:], target_cols[last:], tok_rows, 0, False
+        )
+        step.give(tail_sent)
         tail_diag = swap(tail_sent[0], 4), swap(tail_sent[1], 2)
-        rows_all = jnp.concatenate([r for res in results for r in res[:2]], axis=0)
-        hidden_low, gate_low, up_low, routed = (
-            jnp.concatenate([res[k] for res in results], axis=0) for k in range(2, 6)
-        )
-        rows_all = after(rows_all, tail_sent)
-        grad_w_gate = lax.dot_general(rows_all, gate_low, tn, preferred_element_type=F32)[None]
-        tail_x, tail_y = add_diag(
-            *after((tail[1], tail[2]), grad_w_gate), *after(tail_diag, grad_w_gate)
-        )
-        tail_got = swap(tail_x, 2), swap(tail_y, 4)
-        rows_all = after(rows_all, tail_x, tail_y)
-        grad_w_up = lax.dot_general(rows_all, up_low, tn, preferred_element_type=F32)[None]
-        hidden_low = after(hidden_low, grad_w_up)
-        grad_w_down = lax.dot_general(hidden_low, routed, tn, preferred_element_type=F32)[None]
-        got_x, got_y = after((got_x, got_y), grad_w_down)
-        sums = parts[0].astype(F32) + got_x.astype(F32) + got_y.astype(F32)
-        sums = sums.reshape(last, tok_rows, model_width)
-        total = sums[1].astype(BF)
-        backs = after(mine_backs[0], total)
+        rows_all = [r for res in results for r in res[:2]]
+        hidden_low, gate_low, up_low, routed = ([res[k] for res in results] for k in range(2, 6))
+        ff = w_gate.shape[2]
+        grad_w_gate = product(step.take(rows_all), gate_low, ((0,), (0,)), (model_width, ff), F32, slots, tile=512, limit=40)
+        step.give(grad_w_gate)
+        total = sum_of(chunk_sum(*partial[1]), BF)
+        step.give(total)
         total = ring(total)
-        parts = spread_rows([backs] + mine_backs[1:], other_backs, target_cols, tok_rows, 1)
-        total = after(total, parts)
-        tail_got = after(tail_got, parts)
+        grad_w_up = product(step.take(rows_all), up_low, ((0,), (0,)), (model_width, ff), F32, slots, tile=512, limit=40)
+        step.give(grad_w_up)
         for j in range(2, last):
-            total = ring((total.astype(F32) + sums[j]).astype(BF)).astype(F32)
-        tail_sum = tail[0].astype(F32) + tail_got[0].astype(F32) + tail_got[1].astype(F32)
-        total = ring((total.astype(F32) + tail_sum).astype(BF)).astype(F32) + sums[0]
+            total = sum_of([step.take(total)] + chunk_sum(*partial[j]), BF)
+            step.give(total)
+            total = ring(total)
+        partial[last] = add_chunk(*tail, *tail_diag)
+        partial[0] = add_chunk(*blocks[:3], *chunk_diag(0))
+        grad_w_down = product(
+            step.take(hidden_low), routed, ((0,), (0,)), (ff, model_width), F32, tile=256, limit=40
+        )
+        step.give(grad_w_down)
+        total = sum_of([step.take(total)] + chunk_sum(*partial[last]), BF)
+        step.give(total)
+        total = ring(total)
+        out_sent, out_blocks = spread_rows(
+            step.take(mine_backs), other_backs, target_cols, tok_rows, 1, True
+        )
+        step.give(out_sent)
+        total = sum_of([step.take(total)] + chunk_sum(*partial[0]), F32)
         grad_normed_two = total + jnp.dot(logits_grad_low, router, preferred_element_type=F32)
+        grad_w_gate, grad_w_up, grad_w_down = grad_w_gate[None], grad_w_up[None], grad_w_down[None]
         router_grad = sum(res[6] for res in results) + lax.dot_general(
             logits_grad_low, normed_two_low, tn, preferred_element_type=F32
         )
@@ -1095,12 +1268,16 @@
     grad_residual_part, grad_ffn_gain = ffn_back(grad_normed_two)
     grad_residual = grad_out + grad_residual_part
     grad_pieces = plane_gather(grad_residual.astype(BF))
-    out_grad = lax.dot_general(
-        attn_rows, jnp.concatenate(grad_pieces, axis=0), tn, preferred_element_type=F32
-    ).astype(BF)
     if dense:
-        half = parts[3].shape[0] // 2
-        out_sent = after((parts[3][:half], parts[3][half:]), grad_pieces)
+        out_grad = product(
+            [attn_rows], grad_pieces, ((0,), (0,)), (head_cols, model_width), BF, limit=40
+        )
+    else:
+        out_grad = lax.dot_general(
+            attn_rows, jnp.concatenate(grad_pieces, axis=0), tn, preferred_element_type=F32
+        ).astype(BF)
+    if dense:
+        out_sent = after(out_sent, grad_pieces)
         out_diag = swap(out_sent[0], 4), swap(out_sent[1], 2)
         query = after(query, out_sent, out_grad)
     out_grad = lax.all_to_all(
@@ -1122,7 +1299,7 @@
             pltpu.VMEM((seq_len, head_dim), F32),
             pltpu.VMEM((2 * ctx_count, half_rows, head_cols), BF),
         ],
-        compiler_params=pltpu.CompilerParams(vmem_limit_bytes=ATTEND_LIMIT),
+        compiler_params=pltpu.CompilerParams(vmem_limit_bytes=40 << 20),
         cost_estimate=COST,
     )(
         places,
@@ -1141,59 +1318,104 @@
         seg_col,
     )
     head_grads = head_grads.reshape(seq_len, width)
-    hidden_rows = jnp.concatenate(hidden_pieces, axis=0)
-    last_gates = ()
+    heads_back = lambda rows, kind: lax.dot_general(
+        rows, weight, nt, preferred_element_type=F32
+    ).astype(kind)
     if dense:
-        def weight_part(j, grads):
-            cols = lax.dynamic_slice_in_dim(hidden_rows, planes[j] * shard_width, shard_width, 1)
-            return lax.dot_general(cols, grads, tn, preferred_element_type=F32)
-
-        part = weight_part(1, head_grads).astype(BF)
-        total = ring(part)
-        out_x, out_y = add_diag(*after((parts[1], parts[2]), part), *after(out_diag, part))
-        got_x, got_y = swap(out_x, 2), swap(out_y, 4)
-        head_grads = after(head_grads, out_x, out_y)
-        part = weight_part(2, head_grads)
-        more = [weight_part(j, after(head_grads, part)) for j in (3, 0)]
-        total = after(total, more).astype(F32) + part
-        total_low = total.astype(BF)
-        total = ring(total_low)
-        head_grads = after(head_grads, total_low, out_grad)
-        total = total.astype(F32) + more[0]
-        total_low = total.astype(BF)
-        total = ring(total_low)
-        got_x, got_y = after((got_x, got_y), total_low)
-        out_parts = parts[0].astype(F32) + got_x.astype(F32) + got_y.astype(F32)
-        out_parts = out_parts.reshape(wt_count, tok_rows, model_width)
-        weight_grad = (total.astype(F32) + more[1]).astype(BF)
-        out_parts = after([out_parts[j] for j in range(wt_count)], weight_grad)
-        output = (residual + ring_sum(out_parts, BF)).astype(BF)
-        out_grad = after(out_grad, weight_grad)
-        last_gates = (got_x, got_y)
+        step = Order(out_grad)
+
+        def weight_parts(places, kind):
+            return product(
+                hidden_pieces,
+                [step.take(head_grads)],
+                ((0,), (0,)),
+                (shard_width, width),
+                kind,
+                starts=places,
+            )
+
+        def add_send(got, part, kind=BF):
+            total = sum_of([step.take(got), part], kind)
+            step.give(total)
+            return ring(total)
+
+        (first,) = weight_parts(planes[1:2], BF)
+        step.give(first)
+        total = ring(first)
+        out_x, out_y = add_diag(*step.take((out_blocks[1], out_blocks[2])), *step.take(out_diag))
+        step.give(out_x, out_y)
+        out_got = swap(out_x, 2), swap(out_y, 4)
+        more = weight_parts(planes[jnp.asarray([2, 3, 0])], F32)
+        step.give(more)
+        total = add_send(total, more[0])
+        side = seq_len // 2
+        give = product(
+            [step.take(head_grads[side:])], [weight], ((1,), (1,)), (side, model_width), BF
+        )
+        step.give(give)
+        got = swap(give, 1)
+        keep_part = product(
+            [step.take(head_grads[:side])], [weight], ((1,), (1,)), (side, model_width), BF
+        )
+        step.give(keep_part)
+        total = add_send(total, more[1])
+        out_parts = step.take(out_grad).reshape(wt_count, block_rows, model_width)
+        out_parts = [
+            lax.dynamic_index_in_dim(out_parts, planes[j], 0, keepdims=False)
+            for j in range(wt_count)
+        ]
+        step.give(out_parts[1])
+        out_total = ring(out_parts[1])
+        sums = sum_of([out_blocks[0]] + list(step.take(out_got)), F32)
+        step.give(sums)
+        sums = sums.reshape(wt_count, tok_rows, model_width)
+        kept = sum_of([keep_part, step.take(got)], BF)
+        kept_sent = kept[3 * tok_rows : -half_rows], kept[-half_rows:]
+        step.give(kept_sent)
+        kept_diag = swap(kept_sent[0], 4), swap(kept_sent[1], 2)
+        mixed_low = step.take(sums[1]).astype(BF)
+        step.give(mixed_low)
+        mixed_total = ring(mixed_low)
+        weight_grad = sum_of([step.take(total), more[2]], BF)
+        step.give(weight_grad)
+        weight_x, weight_y = swap(weight_grad, 2), swap(weight_grad, 4)
+        half = weight_grad.shape[0] // 2
+        weight_x, weight_y = step.take((weight_x, weight_y))
+        weight_sent = weight_x[:half], weight_y[half:]
+        step.give(weight_sent)
+        weight_pieces = [
+            weight_grad,
+            weight_x,
+            weight_y,
+            swap(weight_sent[0], 4),
+            swap(weight_sent[1], 2),
+        ]
+        weight_pieces = weight_pieces + [swap(piece, 1) for piece in weight_pieces]
+        kept_x, kept_y = add_diag(
+            kept[tok_rows : 2 * tok_rows], kept[2 * tok_rows : 3 * tok_rows], *step.take(kept_diag)
+        )
+        step.give(kept_x, kept_y)
+        kept_got = swap(kept_x, 2), swap(kept_y, 4)
+        out_total = add_send(out_total, out_parts[2])
+        mixed_total = add_send(mixed_total, sums[2])
+        kept_got = step.take(kept_got)
+        grad_normed_one = sum_of([kept[:tok_rows]] + list(kept_got), F32)
     else:
+        hidden_rows = jnp.concatenate(hidden_pieces, axis=0)
         weight_grad = lax.dot_general(hidden_rows, head_grads, tn, preferred_element_type=F32)
         weight_grad = lax.psum_scatter(
             weight_grad.astype(BF), "wt", scatter_dimension=0, tiled=True
         )
-    weight_grads = jnp.concatenate(plane_gather(weight_grad), axis=0)
-    grad_w_query, grad_w_key, grad_w_value = place_weight_grads(
-        weight_grads.reshape(ctx_count, -1, width), owners, share, head_dim
-    )
-    if dense:
-        parts = out_grad.reshape(wt_count, own_chunks * piece_rows, model_width)[planes]
-        out_grad = ring_sum([parts[j] for j in range(wt_count)], BF).astype(BF)
-    else:
+        weight_grads = jnp.concatenate(plane_gather(weight_grad), axis=0)
+        grad_w_query, grad_w_key, grad_w_value = place_weight_grads(
+            weight_grads.reshape(ctx_count, -1, width), owners, share, head_dim
+        )
         out_grad = lax.psum_scatter(out_grad, "wt", scatter_dimension=0, tiled=True)
-    out_grads = jnp.concatenate(plane_gather(out_grad.reshape(-1, model_width)), axis=0)
-    grad_w_output = place_rows(
-        out_grads.reshape(ctx_count, own_chunks, piece_rows, model_width), owners
-    ).reshape(w_output.shape)
-    grad_normed_one = plane_scatter(
-        lambda rows: lax.dot_general(rows, weight, nt, preferred_element_type=F32),
-        head_grads,
-        None,
-        *last_gates,
-    )
+        out_grads = jnp.concatenate(plane_gather(out_grad.reshape(-1, model_width)), axis=0)
+        grad_w_output = place_rows(
+            out_grads.reshape(ctx_count, own_chunks, piece_rows, model_width), owners
+        ).reshape(w_output.shape)
+        grad_normed_one = plane_scatter(heads_back, head_grads)
     grad_inputs_part, grad_attn_gain = attn_back(grad_normed_one)
     grad_inputs = grad_residual + grad_inputs_part
 
@@ -1213,8 +1435,37 @@
     small = jnp.concatenate([router_grad, grad_ffn_gain[None], grad_attn_gain[None]], axis=0)
     small = small.reshape(experts + 2, wt_count, shard_width).transpose(1, 0, 2)
     small = jnp.concatenate([small, gains[:, None]], axis=1)[planes]
-    small = ring_sum([small[j] for j in range(wt_count)], F32)
-    small = axis_sum(small, "ctx")
+    if dense:
+        out_total = add_send(out_total, out_parts[3])
+        mixed_total = add_send(mixed_total, sums[3])
+        small_low = step.take(small[1])
+        small_total = ring(small_low)
+        out_total = sum_of([step.take(out_total), out_parts[0]], BF)
+        step.give(out_total)
+        out_x, out_y = swap(out_total, 2), swap(out_total, 4)
+        small_total = add_send(small_total, small[2], F32)
+        grad_w_query, grad_w_key, grad_w_value = place_weight_pieces(
+            step.take(weight_pieces), owners, share, head_dim
+        )
+        step.give(grad_w_value)
+        out_x, out_y = step.take((out_x, out_y))
+        half = out_total.shape[0] // 2
+        out_sent = out_x[:half], out_y[half:]
+        step.give(out_sent)
+        out_pieces = [out_total, out_x, out_y, swap(out_sent[0], 4), swap(out_sent[1], 2)]
+        out_pieces = out_pieces + [swap(piece, 1) for piece in out_pieces]
+        small_total = add_send(small_total, small[3], F32)
+        output = step.take(mixed_total).astype(F32) + sums[0]
+        output = (residual + output).astype(BF)
+        step.give(output)
+        small = step.take(small_total) + small[0]
+        step.give(small)
+        grad_w_output = place_row_pieces(step.take(out_pieces), owners, own_chunks)
+        grad_w_output = grad_w_output.reshape(w_output.shape)
+        small = axis_sum(small, "ctx")
+    else:
+        small = ring_sum([small[j] for j in range(wt_count)], F32)
+        small = axis_sum(small, "ctx")
     if dense:
         prob_sums = small[experts + 2, 2 * part : 2 * part + wt_count * experts]
         prob_sums = jnp.sum(prob_sums.reshape(wt_count, experts), axis=0)

time: 859 us -> 757 us (0.88)
  waiting for transfers between devices: 358 us -> 257 us
  Pallas kernels: 128 us -> 209 us
  matrix products: 46.8 us -> 4.27 us
  other arithmetic: 60.5 us -> 27 us
  local copies, waits for them, and re-layouts: 137 us -> 127 us
    ppermute x30 -> x31, waiting for transfers between devices: 250 us -> 121 us  [ring(): lax.ppermute(value, 'wt', [(i, (i + 1) % count) for i in range(count)])]
    pallas_call x5 -> x40, Pallas kernels: 24.8 us -> 101 us  [the longest x10 55.8 us: product(): pl.pallas_call(functools.partial(product_kernel, dims, None, len(lefts),...]
    dot_general x12 -> x0, matrix products: 43.6 us -> none  [the longest x1 8.77 us: local(): lax.dot_general(rows_all, up_low, tn, preferred_element_type=F32)[None]]
    ppermute x90 -> x94, waiting for transfers between devices: 102 us -> 133 us  [swap(): return lax.ppermute(value, 'ctx', [(i, i ^ bit) for i in range(count)])]
    another operation x10 -> x1, other arithmetic: 10.9 us -> 0.82 us  [local(): jnp.stack([tiny[near_rows:].reshape(experts, shard_width) for tiny in tin...]
    unnamed x408 -> x521, local copies, waits for them, and re-layouts: 69.4 us -> 64.2 us
    slice x21 -> x27, local copies, waits for them, and re-layouts: 14 us -> 18.5 us  [the longest x2 2.46 us: chunk_diag(): return [part[j * half_rows:(j + 1) * half_rows] for part in group_diag]]
    ppermute x30 -> x31, starting transfers between devices: 20.4 us -> 16.5 us  [ring(): lax.ppermute(value, 'wt', [(i, (i + 1) % count) for i in range(count)])]
  transfers between devices with their start and end apart: 125 -> 130, of which waited for: 59 -> 61; matrix products, arithmetic and copies ran while one was open for 24% -> 11% of each run, Pallas kernels for 13% -> 25%
where the time goes in v3:
time: 757 us; the launch traced here: 746 us
  waiting for transfers between devices  257 us (34%)
  Pallas kernels  209 us (28%)
  local copies, waits for them, and re-layouts  127 us (17%)
  starting transfers between devices  101 us (13%)
  other arithmetic  27 us (4%)
  between operations  19.7 us (3%)
    ppermute x94, waiting for transfers between devices, swap(): return lax.ppermute(value, 'ctx', [(i, i ^ bit) for i in range(count)])  133 us
    ppermute x31, waiting for transfers between devices, ring(): lax.ppermute(value, 'wt', [(i, (i + 1) % count) for i in range(count)])  121 us
    ppermute x94, starting transfers between devices, swap(): return lax.ppermute(value, 'ctx', [(i, i ^ bit) for i in range(count)])  73.5 us
    unnamed x521, local copies, waits for them, and re-layouts  64.2 us
    pallas_call x10, Pallas kernels, product(): pl.pallas_call(functools.partial(product_kernel, dims, None, len(lefts),...  55.8 us
    pallas_call x4, Pallas kernels, expert_rows(): pl.pallas_call(expert_kernel, out_shape=(low(width), low(width), low(ff),...  48.4 us
    pallas_call x1, Pallas kernels, local(): pl.pallas_call(functools.partial(attend_back_kernel, heads, piece_count),...  23.2 us
    pallas_call x4, Pallas kernels, select_rows(): pl.pallas_call(functools.partial(select_kernel, (len(pieces), len(others)...  18.4 us
  transfers between devices with their start and end apart: 130, of which 61 were waited for; matrix products, arithmetic and copies ran while one was open for 11% of the time, Pallas kernels for 25%

profile of v3, /device:TPU:0, one launch (start us, length us, event | category | flops | bytes accessed | tf_op | source)
XLA Modules:
  0.0 745.7 jit_solution(2060923156766923694)
XLA Ops:
  15.2 10.2 %collective-permute-done.1.refs_2_ = bf16[128,2048]{1,0:T(8,128)(2,1)S(1)} collective-permute-done((bf16[128,2048]{1,0:T(8,128)(2,1)S(1)}, bf16[128,2048]{1,0:T(8,128)(2,1)S(1)}, u32[]{:S(2)}, u32[]{:S(2)}) %collective-permute-start.1) | collective-permute-done | bytes 524320 | tf_op jit(solution)/shard_map/ppermute | solution.py:51
  41.8 7.3 collective-permute-done.10
  70.5 13.7 %collective-permute-done.16 = bf16[512,768]{1,0:T(8,128)(2,1)} collective-permute-done((bf16[512,768]{1,0:T(8,128)(2,1)}, bf16[512,768]{1,0:T(8,128)(2,1)}, u32[]{:S(2)}, u32[]{:S(2)}) %collective-permute-start.16) | collective-permute-done | bytes 786464 | tf_op jit(solution)/shard_map/ppermute | solution.py:158
  103.2 12.8 %collective-permute-done.21 = bf16[512,768]{1,0:T(8,128)(2,1)S(1)} collective-permute-done((bf16[512,768]{1,0:T(8,128)(2,1)}, bf16[512,768]{1,0:T(8,128)(2,1)S(1)}, u32[]{:S(2)}, u32[]{:S(2)}) %collective-permute-start.21) | collective-permute-done | bytes 786464 | tf_op jit(solution)/shard_map/ppermute | solution.py:158
  127.4 18.0 %shard_map.306 = (bf16[1024,512]{1,0:T(8,128)(2,1)}, bf16[1024,128]{1,0:T(8,128)(2,1)}, bf16[1024,128]{1,0:T(8,128)(2,1)}, f32[1024,640]{1,0:T(8,128)}, bf16[16,64,512]{2,1,0:T(8,128)(2,1)}) custom-call(s32[16]{0:T(128)} %copy-done.241, s32[16]{0:T(128)} %select_reduce_fusion.place_ref, s32[8]{0:T(128)} %convert_reduce_fusion.2.first_ref, ...), custom_call_target="tpu_custom_call" | custom-call | flops 1 | bytes 1 | tf_op jit(solution)/shard_map/pallas_call | solution.py:1024
  191.0 10.1 %collective-permute-done.32 = bf16[128,2048]{1,0:T(8,128)(2,1)S(1)} collective-permute-done((bf16[128,2048]{1,0:T(8,128)(2,1)S(1)}, bf16[128,2048]{1,0:T(8,128)(2,1)S(1)}, u32[]{:S(2)}, u32[]{:S(2)}) %collective-permute-start.32) | collective-permute-done | bytes 524320 | tf_op jit(solution)/shard_map/ppermute | solution.py:51
  206.2 8.2 %collective-permute-done.36.refs_2_ = bf16[128,2048]{1,0:T(8,128)(2,1)S(1)} collective-permute-done((bf16[128,2048]{1,0:T(8,128)(2,1)S(1)}, bf16[128,2048]{1,0:T(8,128)(2,1)S(1)}, u32[]{:S(2)}, u32[]{:S(2)}) %collective-permute-start.36) | collective-permute-done | bytes 524320 | tf_op jit(solution)/shard_map/ppermute | solution.py:51
  228.4 7.3 collective-permute-done.41.refs_2_
  263.0 11.9 %shard_map.312 = (bf16[320,2048]{1,0:T(8,128)(2,1)S(1)}, bf16[320,2048]{1,0:T(8,128)(2,1)S(1)}, bf16[320,768]{1,0:T(8,128)(2,1)S(1)}, bf16[320,768]{1,0:T(8,128)...) custom-call(s32[1]{0:T(128)} %bitcast.29.expert_ref, ...), custom_call_target="tpu_custom_call" | custom-call | flops 1 | bytes 1 | tf_op jit(solution)/shard_map/pallas_call | solution.py:655
  298.5 12.1 %shard_map.314 = (bf16[320,2048]{1,0:T(8,128)(2,1)S(1)}, bf16[320,2048]{1,0:T(8,128)(2,1)S(1)}, bf16[320,768]{1,0:T(8,128)(2,1)S(1)}, bf16[320,768]{1,0:T(8,128)...) custom-call(s32[1]{0:T(128)} %bitcast.29.expert_ref, ...), custom_call_target="tpu_custom_call" | custom-call | flops 1 | bytes 1 | tf_op jit(solution)/shard_map/pallas_call | solution.py:655
  310.6 6.9 collective-permute-done.53.refs_2_
  330.6 11.5 %collective-permute-done.56.refs_4_ = bf16[128,2048]{1,0:T(8,128)(2,1)} collective-permute-done((bf16[128,2048]{1,0:T(8,128)(2,1)}, bf16[128,2048]{1,0:T(8,128)(2,1)}, u32[]{:S(2)}, u32[]{:S(2)}) %collective-permute-start.56) | collective-permute-done | bytes 524320 | tf_op jit(solution)/shard_map/ppermute | solution.py:51
  344.5 12.3 %shard_map.316 = (bf16[320,2048]{1,0:T(8,128)(2,1)S(1)}, bf16[320,2048]{1,0:T(8,128)(2,1)S(1)}, bf16[320,768]{1,0:T(8,128)(2,1)S(1)}, bf16[320,768]{1,0:T(8,128)...) custom-call(s32[1]{0:T(128)} %bitcast.29.expert_ref, ...), custom_call_target="tpu_custom_call" | custom-call | flops 1 | bytes 1 | tf_op jit(solution)/shard_map/pallas_call | solution.py:655
  380.4 12.1 %shard_map.319 = (bf16[320,2048]{1,0:T(8,128)(2,1)S(1)}, bf16[320,2048]{1,0:T(8,128)(2,1)S(1)}, bf16[320,768]{1,0:T(8,128)(2,1)S(1)}, bf16[320,768]{1,0:T(8,128)...) custom-call(s32[1]{0:T(128)} %bitcast.29.expert_ref, ...), custom_call_target="tpu_custom_call" | custom-call | flops 1 | bytes 1 | tf_op jit(solution)/shard_map/pallas_call | solution.py:655
  408.4 7.9 %shard_map.323 = f32[2048,768]{1,0:T(8,128)} custom-call(s32[1]{0:T(128)} %constant.73.clone.1.start_ref, bf16[320,2048]{1,0:T(8,128)(2,1)S(1)} %copy-done.11, bf16[320,2048]{1,0:T(8,128)(2,1)} %collective-permute-done.42.other_ref.refs_1_, bf16[320,2048]{1,0:T(8,128)(2,1)S(1)} %copy-done.14, bf16[320,2048]{1,0:T(8,128)(2,1)} %collective-permute-done.48.other_ref.refs_3_, ...), custom_call_target="tpu_custom_call" | custom-call | flops 1 | bytes 1 | tf_op jit(solution)/shard_map/pallas_call | solution.py:836
  418.7 8.0 %shard_map.325 = f32[2048,768]{1,0:T(8,128)} custom-call(s32[1]{0:T(128)} %constant.73.clone.1.start_ref, bf16[320,2048]{1,0:T(8,128)(2,1)S(1)} %copy-done.11, bf16[320,2048]{1,0:T(8,128)(2,1)} %collective-permute-done.42.other_ref.refs_1_, bf16[320,2048]{1,0:T(8,128)(2,1)S(1)} %copy-done.14, bf16[320,2048]{1,0:T(8,128)(2,1)} %collective-permute-done.48.other_ref.refs_3_, ...), custom_call_target="tpu_custom_call" | custom-call | flops 1 | bytes 1 | tf_op jit(solution)/shard_map/pallas_call | solution.py:836
  464.5 10.7 %collective-permute-done.78.refs_3_.refs_2_ = bf16[128,2048]{1,0:T(8,128)(2,1)S(1)} collective-permute-done((bf16[128,2048]{1,0:T(8,128)(2,1)S(1)}, bf16[128,2048]{1,0:T(8,128)(2,1)S(1)}, u32[]{:S(2)}, u32[]{:S(2)}) %collective-permute-start.78) | collective-permute-done | bytes 524320 | tf_op jit(solution)/shard_map/ppermute | solution.py:51
  512.1 23.2 %shard_map.334 = (bf16[16,64,768]{2,1,0:T(8,128)(2,1)S(1)}, f32[1,128]{1,0:T(1,128)S(1)}, f32[1,128]{1,0:T(1,128)S(1)}) custom-call(s32[16]{0:T(128)S(1)} %copy-done.162, s32[8]{0:T(128)S(1)} %copy-done.159, bf16[128,2048]{1,0:T(8,128)(2,1)S(1)} %copy-done.44, bf16[128,2048]{1,0:T(8,128)(2,1)S(1)} %copy-done.49, bf16[128,2048]{1,0:T(8,128)(2,1)S(1)} %copy-done.47, ...), custom_call_target="tpu_custom_call" | custom-call | flops 1 | bytes 1 | tf_op jit(solution)/shard_map/pallas_call | solution.py:1286
  556.2 6.6 shard_map.337
  579.0 14.2 %collective-permute-done.91.refs_0_ = bf16[512,768]{1,0:T(8,128)(2,1)} collective-permute-done((bf16[512,768]{1,0:T(8,128)(2,1)S(1)}, bf16[512,768]{1,0:T(8,128)(2,1)}, u32[]{:S(2)}, u32[]{:S(2)}) %collective-permute-start.91) | collective-permute-done | bytes 786464 | tf_op jit(solution)/shard_map/ppermute | solution.py:158
  628.3 11.9 %collective-permute-done.99.refs_2_ = bf16[512,768]{1,0:T(8,128)(2,1)} collective-permute-done((bf16[512,768]{1,0:T(8,128)(2,1)S(1)}, bf16[512,768]{1,0:T(8,128)(2,1)}, u32[]{:S(2)}, u32[]{:S(2)}) %collective-permute-start.99) | collective-permute-done | bytes 786464 | tf_op jit(solution)/shard_map/ppermute | solution.py:51
  653.1 9.9 %collective-permute-done.101.refs_0_ = bf16[128,2048]{1,0:T(8,128)(2,1)S(1)} collective-permute-done((bf16[128,2048]{1,0:T(8,128)(2,1)S(1)}, bf16[128,2048]{1,0:T(8,128)(2,1)S(1)}, u32[]{:S(2)}, u32[]{:S(2)}) %collective-permute-start.101) | collective-permute-done | bytes 524320 | tf_op jit(solution)/shard_map/ppermute | solution.py:158
  672.5 8.6 %collective-permute-done.100.refs_0_ = bf16[128,2048]{1,0:T(8,128)(2,1)S(1)} collective-permute-done((bf16[128,2048]{1,0:T(8,128)(2,1)S(1)}, bf16[128,2048]{1,0:T(8,128)(2,1)S(1)}, u32[]{:S(2)}, u32[]{:S(2)}) %collective-permute-start.100) | collective-permute-done | bytes 524320 | tf_op jit(solution)/shard_map/ppermute | solution.py:158
  698.6 7.7 %shard_map.353 = (f32[512,4096]{1,0:T(8,128)}, f32[512,512]{1,0:T(8,128)}, f32[512,512]{1,0:T(8,128)}) custom-call(s32[8]{0:T(128)} %get-tuple-element.596.owner_ref, bf16[512,768]{1,0:T(8,128)(2,1)} %copy-done.50, bf16[512,768]{1,0:T(8,128)(2,1)} %collective-permute-done.98.refs_1_, bf16[512,768]{1,0:T(8,128)(2,1)} %collective-permute-done.99.refs_2_, ...), custom_call_target="tpu_custom_call" | custom-call | flops 1 | bytes 1 | tf_op jit(solution)/shard_map/pallas_call | solution.py:772
  (974 shorter events, 463.1 us)
Async XLA Ops:
  2.6 33.0 %collective-permute-start.9 = (bf16[128,2048]{1,0:T(8,128)(2,1)}, bf16[128,2048]{1,0:T(8,128)(2,1)}, u32[]{:S(2)}, u32[]{:S(2)}) collective-permute-start(bf16[128,2048]{1,0:T(8,128)(2,1)} %bitcast.5), channel_id=1, source_target_pairs={{0,1},{1,2},{2,3},{3,0},{4,5},{5,6},{6,7},{7,4},{8,9},{9,10},{10,1... | collective-permute-start | bytes 1572872 | tf_op jit(solution)/shard_map/ppermute | solution.py:158
  10.9 29.1 %collective-permute-start.4 = (bf16[128,2048]{1,0:T(8,128)(2,1)S(1)}, bf16[128,2048]{1,0:T(8,128)(2,1)S(1)}, u32[]{:S(2)}, u32[]{:S(2)}) collective-permute-start(bf16[128,2048]{1,0:T(8,128)(2,1)S(1)} %fusion.14.refs_0_), channel_id=1, source_target_pairs={{0,4},{4,0},{8,12},{12,8},{16,20},{20,16},{24,28},{28,24},{1,5},{5... | collective-permute-start | bytes 1572872 | tf_op jit(solution)/shard_map/ppermute | solution.py:51
  56.0 28.1 %collective-permute-start.16 = (bf16[512,768]{1,0:T(8,128)(2,1)}, bf16[512,768]{1,0:T(8,128)(2,1)}, u32[]{:S(2)}, u32[]{:S(2)}) collective-permute-start(bf16[512,768]{1,0:T(8,128)(2,1)} %collective-permute-done.10), channel_id=1, source_target_pairs={{0,1},{1,2},{2,3},{3,0},{4,5},{5,6},{6,7},{7,4},{8,9},{9,10},{10,1... | collective-permute-start | bytes 2359304 | tf_op jit(solution)/shard_map/ppermute | solution.py:158
  87.9 28.1 %collective-permute-start.21 = (bf16[512,768]{1,0:T(8,128)(2,1)}, bf16[512,768]{1,0:T(8,128)(2,1)S(1)}, u32[]{:S(2)}, u32[]{:S(2)}) collective-permute-start(bf16[512,768]{1,0:T(8,128)(2,1)} %collective-permute-done.16), channel_id=1, source_target_pairs={{0,1},{1,2},{2,3},{3,0},{4,5},{5,6},{6,7},{7,4},{8,9},{9,10},{10,1... | collective-permute-start | bytes 2359304 | tf_op jit(solution)/shard_map/ppermute | solution.py:158
  117.6 36.7 %all-to-all-start = ((bf16[8,64,2048]{2,1,0:T(8,128)(2,1)}), bf16[8,64,2048]{2,1,0:T(8,128)(2,1)S(1)}, u32[]{:S(2)}, u32[]{:S(2)}) async-start(bf16[8,64,2048]{2,1,0:T(8,128)(2,1)} %bitcast.176), calls=%async_computation | async-start | bytes 4194304 | tf_op jit(solution)/shard_map/all_to_all | solution.py:1005
  124.7 27.4 %collective-permute-start.26 = (bf16[128,2048]{1,0:T(8,128)(2,1)}, bf16[128,2048]{1,0:T(8,128)(2,1)}, u32[]{:S(2)}, u32[]{:S(2)}) collective-permute-start(bf16[128,2048]{1,0:T(8,128)(2,1)} %copy-done.86), channel_id=1, source_target_pairs={{0,1},{1,2},{2,3},{3,0},{4,5},{5,6},{6,7},{7,4},{8,9},{9,10},{10,1... | collective-permute-start | bytes 1572872 | tf_op jit(solution)/shard_map/ppermute | solution.py:158
  160.7 25.1 %collective-permute-start.31 = (bf16[128,2048]{1,0:T(8,128)(2,1)}, bf16[128,2048]{1,0:T(8,128)(2,1)}, u32[]{:S(2)}, u32[]{:S(2)}) collective-permute-start(bf16[128,2048]{1,0:T(8,128)(2,1)} %collective-permute-done.18.refs_7_), channel_id=1, source_target_pairs={{0,1},{1,2},{2,3},{3,0},{4,5},{5,6},{6,7},{7,4},{8,9},{9,10},{10,1... | collective-permute-start | bytes 1572872 | tf_op jit(solution)/shard_map/ppermute | solution.py:158
  160.7 30.3 %collective-permute-start.34 = (bf16[128,2048]{1,0:T(8,128)(2,1)}, bf16[128,2048]{1,0:T(8,128)(2,1)}, u32[]{:S(2)}, u32[]{:S(2)}) collective-permute-start(bf16[128,2048]{1,0:T(8,128)(2,1)} %constant_dynamic-update-slice_fusion.5), channel_id=1, source_target_pairs={{0,1},{1,2},{2,3},{3,0},{4,5},{5,6},{6,7},{7,4},{8,9},{9,10},{10,1... | collective-permute-start | bytes 1572872 | tf_op jit(solution)/shard_map/ppermute | solution.py:158
  218.5 26.8 %collective-permute-start.45 = (bf16[256,2048]{1,0:T(8,128)(2,1)S(1)}, bf16[256,2048]{1,0:T(8,128)(2,1)}, u32[]{:S(2)}, u32[]{:S(2)}) collective-permute-start(bf16[256,2048]{1,0:T(8,128)(2,1)S(1)} %pad_maximum_fusion), channel_id=1, source_target_pairs={{0,1},{1,2},{2,3},{3,0},{4,5},{5,6},{6,7},{7,4},{8,9},{9,10},{10,1... | collective-permute-start | bytes 3145736 | tf_op jit(solution)/shard_map/ppermute | solution.py:158
  252.7 24.9 %collective-permute-start.47 = (bf16[256,2048]{1,0:T(8,128)(2,1)}, bf16[256,2048]{1,0:T(8,128)(2,1)}, u32[]{:S(2)}, u32[]{:S(2)}) collective-permute-start(bf16[256,2048]{1,0:T(8,128)(2,1)} %collective-permute-done.45.refs_0_), channel_id=1, source_target_pairs={{0,16},{4,20},{8,24},{12,28},{16,0},{20,4},{24,8},{28,12},{1,17},{... | collective-permute-start | bytes 3145736 | tf_op jit(solution)/shard_map/ppermute | solution.py:51
  254.5 24.5 %collective-permute-start.46 = (bf16[256,2048]{1,0:T(8,128)(2,1)}, bf16[256,2048]{1,0:T(8,128)(2,1)}, u32[]{:S(2)}, u32[]{:S(2)}) collective-permute-start(bf16[256,2048]{1,0:T(8,128)(2,1)} %collective-permute-done.45.refs_0_), channel_id=1, source_target_pairs={{0,8},{4,12},{8,0},{12,4},{16,24},{20,28},{24,16},{28,20},{1,9},{5... | collective-permute-start | bytes 3145736 | tf_op jit(solution)/shard_map/ppermute | solution.py:51
  254.7 32.5 %collective-permute-start.51 = (bf16[256,2048]{1,0:T(8,128)(2,1)}, bf16[256,2048]{1,0:T(8,128)(2,1)}, u32[]{:S(2)}, u32[]{:S(2)}) collective-permute-start(bf16[256,2048]{1,0:T(8,128)(2,1)} %collective-permute-done.45.refs_0_), channel_id=1, source_target_pairs={{0,1},{1,2},{2,3},{3,0},{4,5},{5,6},{6,7},{7,4},{8,9},{9,10},{10,1... | collective-permute-start | bytes 3145736 | tf_op jit(solution)/shard_map/ppermute | solution.py:158
  330.1 35.0 %collective-permute-start.58 = (bf16[320,2048]{1,0:T(8,128)(2,1)}, bf16[320,2048]{1,0:T(8,128)(2,1)S(1)}, u32[]{:S(2)}, u32[]{:S(2)}) collective-permute-start(bf16[320,2048]{1,0:T(8,128)(2,1)} %copy-done.163), channel_id=1, source_target_pairs={{0,4},{4,0},{8,12},{12,8},{16,20},{20,16},{24,28},{28,24},{1,5},{5... | collective-permute-start | bytes 3932168 | tf_op jit(solution)/shard_map/ppermute | solution.py:51
  330.1 35.0 %collective-permute-start.59 = (bf16[320,2048]{1,0:T(8,128)(2,1)}, bf16[320,2048]{1,0:T(8,128)(2,1)S(1)}, u32[]{:S(2)}, u32[]{:S(2)}) collective-permute-start(bf16[320,2048]{1,0:T(8,128)(2,1)} %copy-done.164), channel_id=1, source_target_pairs={{0,4},{4,0},{8,12},{12,8},{16,20},{20,16},{24,28},{28,24},{1,5},{5... | collective-permute-start | bytes 3932168 | tf_op jit(solution)/shard_map/ppermute | solution.py:51
  487.6 48.8 %all-to-all-start.1 = ((bf16[8,64,2048]{2,1,0:T(8,128)(2,1)}), bf16[8,64,2048]{2,1,0:T(8,128)(2,1)}, u32[]{:S(2)}, u32[]{:S(2)}) async-start(bf16[8,64,2048]{2,1,0:T(8,128)(2,1)} %bitcast.143), calls=%async_computation.1 | async-start | bytes 4194304 | tf_op jit(solution)/shard_map/all_to_all | solution.py:1283
  492.5 56.6 %collective-permute-start.86 = (bf16[256,2048]{1,0:T(8,128)(2,1)}, bf16[256,2048]{1,0:T(8,128)(2,1)}, u32[]{:S(2)}, u32[]{:S(2)}) collective-permute-start(bf16[256,2048]{1,0:T(8,128)(2,1)} %copy-done.166), channel_id=1, source_target_pairs={{0,16},{4,20},{8,24},{12,28},{16,0},{20,4},{24,8},{28,12},{1,17},{... | collective-permute-start | bytes 3145736 | tf_op jit(solution)/shard_map/ppermute | solution.py:51
  494.5 54.5 %collective-permute-start.87 = (bf16[256,2048]{1,0:T(8,128)(2,1)}, bf16[256,2048]{1,0:T(8,128)(2,1)}, u32[]{:S(2)}, u32[]{:S(2)}) collective-permute-start(bf16[256,2048]{1,0:T(8,128)(2,1)} %copy-done.165), channel_id=1, source_target_pairs={{0,8},{4,12},{8,0},{12,4},{16,24},{20,28},{24,16},{28,20},{1,9},{5... | collective-permute-start | bytes 3145736 | tf_op jit(solution)/shard_map/ppermute | solution.py:51
  555.6 52.5 %collective-permute-start.88 = (bf16[512,2048]{1,0:T(8,128)(2,1)}, bf16[512,2048]{1,0:T(8,128)(2,1)S(1)}, u32[]{:S(2)}, u32[]{:S(2)}) collective-permute-start(bf16[512,2048]{1,0:T(8,128)(2,1)} %get-tuple-element.463), channel_id=1, source_target_pairs={{0,8},{4,12},{8,0},{12,4},{16,24},{20,28},{24,16},{28,20},{1,9},{5... | collective-permute-start | bytes 6291464 | tf_op jit(solution)/shard_map/ppermute | solution.py:51
  556.1 52.0 %collective-permute-start.89 = (bf16[512,2048]{1,0:T(8,128)(2,1)}, bf16[512,2048]{1,0:T(8,128)(2,1)}, u32[]{:S(2)}, u32[]{:S(2)}) collective-permute-start(bf16[512,2048]{1,0:T(8,128)(2,1)} %get-tuple-element.464), channel_id=1, source_target_pairs={{0,16},{4,20},{8,24},{12,28},{16,0},{20,4},{24,8},{28,12},{1,17},{... | collective-permute-start | bytes 6291464 | tf_op jit(solution)/shard_map/ppermute | solution.py:51
  571.3 42.2 %collective-permute-start.92 = (bf16[512,2048]{1,0:T(8,128)(2,1)}, bf16[512,2048]{1,0:T(8,128)(2,1)}, u32[]{:S(2)}, u32[]{:S(2)}) collective-permute-start(bf16[512,2048]{1,0:T(8,128)(2,1)} %shard_map.339), channel_id=1, source_target_pairs={{0,4},{4,0},{8,12},{12,8},{16,20},{20,16},{24,28},{28,24},{1,5},{5... | collective-permute-start | bytes 6291464 | tf_op jit(solution)/shard_map/ppermute | solution.py:51
  622.6 24.1 %collective-permute-start.94 = (bf16[128,2048]{1,0:T(8,128)(2,1)}, bf16[128,2048]{1,0:T(8,128)(2,1)}, u32[]{:S(2)}, u32[]{:S(2)}) collective-permute-start(bf16[128,2048]{1,0:T(8,128)(2,1)} %get-tuple-element.549), channel_id=1, source_target_pairs={{0,1},{1,2},{2,3},{3,0},{4,5},{5,6},{6,7},{7,4},{8,9},{9,10},{10,1... | collective-permute-start | bytes 1572872 | tf_op jit(solution)/shard_map/ppermute | solution.py:158
  641.5 43.7 %collective-permute-start.112 = (bf16[512,768]{1,0:T(8,128)(2,1)S(1)}, bf16[512,768]{1,0:T(8,128)(2,1)}, u32[]{:S(2)}, u32[]{:S(2)}) collective-permute-start(bf16[512,768]{1,0:T(8,128)(2,1)S(1)} %shard_map.344.refs_0_), channel_id=1, source_target_pairs={{0,4},{4,0},{8,12},{12,8},{16,20},{20,16},{24,28},{28,24},{1,5},{5... | collective-permute-start | bytes 2359304 | tf_op jit(solution)/shard_map/ppermute | solution.py:51
  664.7 24.7 %collective-permute-start.106 = (bf16[128,2048]{1,0:T(8,128)(2,1)S(1)}, bf16[128,2048]{1,0:T(8,128)(2,1)S(1)}, u32[]{:S(2)}, u32[]{:S(2)}) collective-permute-start(bf16[128,2048]{1,0:T(8,128)(2,1)S(1)} %shard_map.348), channel_id=1, source_target_pairs={{0,1},{1,2},{2,3},{3,0},{4,5},{5,6},{6,7},{7,4},{8,9},{9,10},{10,1... | collective-permute-start | bytes 1572872 | tf_op jit(solution)/shard_map/ppermute | solution.py:158
  667.0 30.6 %collective-permute-start.113 = (bf16[512,768]{1,0:T(8,128)(2,1)}, bf16[512,768]{1,0:T(8,128)(2,1)}, u32[]{:S(2)}, u32[]{:S(2)}) collective-permute-start(bf16[512,768]{1,0:T(8,128)(2,1)} %collective-permute-done.98.refs_1_), channel_id=1, source_target_pairs={{0,4},{4,0},{8,12},{12,8},{16,20},{20,16},{24,28},{28,24},{1,5},{5... | collective-permute-start | bytes 2359304 | tf_op jit(solution)/shard_map/ppermute | solution.py:51
  (365 other events, 3637.6 us)

commit v4 on v3

--- a/solution.py
+++ b/solution.py
@@ -111,13 +111,13 @@
     out_y_ref[half:] = low(part_y_ref[half:], from_x_ref[...])
 
 
-def add_diag(part_x, part_y, from_y, from_x):
+def add_diag(part_x, part_y, from_y, from_x, limit=24):
     return pl.pallas_call(
         add_diag_kernel,
         out_shape=(jax.ShapeDtypeStruct(part_x.shape, BF),) * 2,
         in_specs=[VMEM_SPEC] * 4,
         out_specs=[VMEM_SPEC] * 2,
-        compiler_params=pltpu.CompilerParams(vmem_limit_bytes=24 << 20),
+        compiler_params=pltpu.CompilerParams(vmem_limit_bytes=limit << 20),
         cost_estimate=COST,
     )(part_x, part_y, from_y, from_x)
 
@@ -127,13 +127,12 @@
     if count != 8:
         parts = multiply(left, BF)
         return lax.psum_scatter(parts, "ctx", scatter_dimension=0, tiled=True).astype(F32)
-    side = left.shape[0] // 2
-    rows = side // 4
+    rows = left.shape[0] // 8
     half = rows // 2
-    give = multiply(left[side:], BF)
+    give = multiply(left, BF, 1)
     got = swap(give, 1)
-    keep = multiply(after(left[:side], give), BF)
-    kept = sum_of(after([keep, got], others), BF)
+    keep = multiply(after(left, give), BF, 0)
+    kept = sum_of(after([keep, got], others), BF, 60)
     sends = kept[3 * rows : -half], kept[-half:]
     from_y, from_x = swap(sends[0], 4), swap(sends[1], 2)
     from_y, from_x = after((from_y, from_x), fill(sends))
@@ -821,10 +820,14 @@
         out_ref[...] = out.astype(out_ref.dtype)
 
 
-def product(lefts, rights, dims, out_shape, kind=F32, rows=None, starts=None, limit=60, tile=None):
+def product(lefts, rights, dims, out_shape, kind=F32, rows=None, starts=None, limit=60, tile=None, block=None):
     count = 1 if starts is None else starts.shape[0]
     start_arg = jnp.zeros((1,), jnp.int32) if starts is None else starts
-    if tile is None:
+    if block is not None:
+        left_specs = [pl.BlockSpec((rows, left.shape[1]), lambda i: (block, 0)) for left in lefts]
+        right_specs = [pl.BlockSpec(right.shape, lambda i: (0, 0)) for right in rights]
+        out_spec = pl.BlockSpec(out_shape, lambda i: (0, 0))
+    elif tile is None:
         left_specs, right_specs = [VMEM_SPEC] * len(lefts), [VMEM_SPEC] * len(rights)
         out_spec = VMEM_SPEC
     else:
@@ -837,7 +840,7 @@
         functools.partial(
             product_kernel, dims, None, len(lefts), len(rights), starts is not None
         ),
-        grid=() if tile is None else (out_shape[0] // tile,),
+        grid=(1,) if block is not None else () if tile is None else (out_shape[0] // tile,),
         out_shape=(jax.ShapeDtypeStruct(out_shape, kind),) * count,
         in_specs=[SMEM_SPEC] + left_specs + right_specs,
         out_specs=[out_spec] * count,
@@ -993,7 +996,7 @@
         out_pieces, weight = keep(3, buffers, ticks[3])
         tinies.append(ring(after(tinies[2], weight)))
         cot_next = [ring(after(p, weight)) for p in (cot, cot_x, cot_y, cot_diag)]
-        nears = [tiny[:near_rows] for tiny in tinies]
+        tinies_later = tinies[1:]
         router = jnp.stack([tiny[near_rows:].reshape(experts, shard_width) for tiny in tinies])
         router = router[planes].transpose(1, 0, 2).reshape(experts, model_width)
     else:
@@ -1052,16 +1055,19 @@
     later_tables = []
     out_project = lambda rows, kind: low_matmul(rows, out_weight).astype(kind)
     if dense:
-        attn_rows = after(attn_rows, cot_next[:2])
-        out_project = lambda rows, kind: product(
-            [rows], [out_weight], ((1,), (0,)), (rows.shape[0], model_width), kind
-        )
+        attn_rows = after(attn_rows, cot_next[0])
+        side = seq_len // 2
+
+        def out_project(rows, kind, block):
+            shape = (side, model_width)
+            return product([rows], [out_weight], ((1,), (0,)), shape, kind, side, block=block)
+
 
         def fill(sends):
-            later_tables.extend(tables(after(jnp.concatenate(nears[1:], axis=0), sends)))
+            later_tables.extend(tables(jnp.concatenate([t[:near_rows] for t in after(tinies_later, sends)], axis=0)))
             return tuple(later_tables) + (cot_next[2],)
 
-        attn = plane_scatter(out_project, attn_rows, fill, (), (cot_next[3],))
+        attn = plane_scatter(out_project, attn_rows, fill, (cot_next[1],), (cot_next[3],))
     else:
         attn = plane_scatter(out_project, attn_rows)
     residual = inputs + attn
@@ -1269,20 +1275,9 @@
     grad_residual = grad_out + grad_residual_part
     grad_pieces = plane_gather(grad_residual.astype(BF))
     if dense:
-        out_grad = product(
-            [attn_rows], grad_pieces, ((0,), (0,)), (head_cols, model_width), BF, limit=40
-        )
-    else:
-        out_grad = lax.dot_general(
-            attn_rows, jnp.concatenate(grad_pieces, axis=0), tn, preferred_element_type=F32
-        ).astype(BF)
-    if dense:
         out_sent = after(out_sent, grad_pieces)
         out_diag = swap(out_sent[0], 4), swap(out_sent[1], 2)
-        query = after(query, out_sent, out_grad)
-    out_grad = lax.all_to_all(
-        out_grad.reshape(ctx_count, piece_rows, model_width), "ctx", 0, 0, tiled=True
-    )
+        query = after(query, out_sent)
     head_grads, grad_query_gain, grad_key_gain = pl.pallas_call(
         functools.partial(attend_back_kernel, heads, piece_count),
         out_shape=(
@@ -1299,7 +1294,7 @@
             pltpu.VMEM((seq_len, head_dim), F32),
             pltpu.VMEM((2 * ctx_count, half_rows, head_cols), BF),
         ],
-        compiler_params=pltpu.CompilerParams(vmem_limit_bytes=40 << 20),
+        compiler_params=pltpu.CompilerParams(vmem_limit_bytes=ATTEND_LIMIT),
         cost_estimate=COST,
     )(
         places,
@@ -1322,7 +1317,7 @@
         rows, weight, nt, preferred_element_type=F32
     ).astype(kind)
     if dense:
-        step = Order(out_grad)
+        step = Order(out_diag)
 
         def weight_parts(places, kind):
             return product(
@@ -1335,30 +1330,49 @@
             )
 
         def add_send(got, part, kind=BF):
-            total = sum_of([step.take(got), part], kind)
+            total = sum_of([step.take(got), part], kind, 60)
             step.give(total)
             return ring(total)
 
         (first,) = weight_parts(planes[1:2], BF)
         step.give(first)
         total = ring(first)
-        out_x, out_y = add_diag(*step.take((out_blocks[1], out_blocks[2])), *step.take(out_diag))
+        out_x, out_y = add_diag(
+            *step.take((out_blocks[1], out_blocks[2])), *step.take(out_diag), 60
+        )
         step.give(out_x, out_y)
         out_got = swap(out_x, 2), swap(out_y, 4)
         more = weight_parts(planes[jnp.asarray([2, 3, 0])], F32)
         step.give(more)
         total = add_send(total, more[0])
-        side = seq_len // 2
+        out_grad = product(
+            [step.take(attn_rows)], grad_pieces, ((0,), (0,)), (head_cols, model_width), BF
+        )
+        step.give(out_grad)
+        out_grad = lax.all_to_all(
+            out_grad.reshape(ctx_count, piece_rows, model_width), "ctx", 0, 0, tiled=True
+        )
+        total = add_send(total, more[1])
+        shape = (side, model_width)
         give = product(
-            [step.take(head_grads[side:])], [weight], ((1,), (1,)), (side, model_width), BF
+            [step.take(head_grads)], [weight], ((1,), (1,)), shape, BF, side, block=1
         )
         step.give(give)
         got = swap(give, 1)
         keep_part = product(
-            [step.take(head_grads[:side])], [weight], ((1,), (1,)), (side, model_width), BF
+            [step.take(head_grads)], [weight], ((1,), (1,)), shape, BF, side, block=0
         )
         step.give(keep_part)
-        total = add_send(total, more[1])
+        sums = sum_of([out_blocks[0]] + list(step.take(out_got)), F32, 60)
+        step.give(sums)
+        sums = sums.reshape(wt_count, tok_rows, model_width)
+        weight_grad = sum_of([step.take(total), more[2]], BF, 60)
+        step.give(weight_grad)
+        weight_x, weight_y = swap(weight_grad, 2), swap(weight_grad, 4)
+        kept = sum_of([keep_part, step.take(got)], BF, 60)
+        kept_sent = kept[3 * tok_rows : -half_rows], kept[-half_rows:]
+        step.give(kept_sent)
+        kept_diag = swap(kept_sent[0], 4), swap(kept_sent[1], 2)
         out_parts = step.take(out_grad).reshape(wt_count, block_rows, model_width)
         out_parts = [
             lax.dynamic_index_in_dim(out_parts, planes[j], 0, keepdims=False)
@@ -1366,19 +1380,9 @@
         ]
         step.give(out_parts[1])
         out_total = ring(out_parts[1])
-        sums = sum_of([out_blocks[0]] + list(step.take(out_got)), F32)
-        step.give(sums)
-        sums = sums.reshape(wt_count, tok_rows, model_width)
-        kept = sum_of([keep_part, step.take(got)], BF)
-        kept_sent = kept[3 * tok_rows : -half_rows], kept[-half_rows:]
-        step.give(kept_sent)
-        kept_diag = swap(kept_sent[0], 4), swap(kept_sent[1], 2)
         mixed_low = step.take(sums[1]).astype(BF)
         step.give(mixed_low)
         mixed_total = ring(mixed_low)
-        weight_grad = sum_of([step.take(total), more[2]], BF)
-        step.give(weight_grad)
-        weight_x, weight_y = swap(weight_grad, 2), swap(weight_grad, 4)
         half = weight_grad.shape[0] // 2
         weight_x, weight_y = step.take((weight_x, weight_y))
         weight_sent = weight_x[:half], weight_y[half:]
@@ -1391,16 +1395,30 @@
             swap(weight_sent[1], 2),
         ]
         weight_pieces = weight_pieces + [swap(piece, 1) for piece in weight_pieces]
+        out_total = add_send(out_total, out_parts[2])
         kept_x, kept_y = add_diag(
-            kept[tok_rows : 2 * tok_rows], kept[2 * tok_rows : 3 * tok_rows], *step.take(kept_diag)
+            kept[tok_rows : 2 * tok_rows],
+            kept[2 * tok_rows : 3 * tok_rows],
+            *step.take(kept_diag),
+            60,
         )
         step.give(kept_x, kept_y)
         kept_got = swap(kept_x, 2), swap(kept_y, 4)
-        out_total = add_send(out_total, out_parts[2])
+        out_total = add_send(out_total, out_parts[3])
         mixed_total = add_send(mixed_total, sums[2])
         kept_got = step.take(kept_got)
-        grad_normed_one = sum_of([kept[:tok_rows]] + list(kept_got), F32)
+        grad_normed_one = sum_of([kept[:tok_rows]] + list(kept_got), F32, 60)
+        step.give(grad_normed_one)
+        out_total = sum_of([step.take(out_total), out_parts[0]], BF, 60)
+        step.give(out_total)
+        out_x, out_y = swap(out_total, 2), swap(out_total, 4)
     else:
+        out_grad = lax.dot_general(
+            attn_rows, jnp.concatenate(grad_pieces, axis=0), tn, preferred_element_type=F32
+        ).astype(BF)
+        out_grad = lax.all_to_all(
+            out_grad.reshape(ctx_count, piece_rows, model_width), "ctx", 0, 0, tiled=True
+        )
         hidden_rows = jnp.concatenate(hidden_pieces, axis=0)
         weight_grad = lax.dot_general(hidden_rows, head_grads, tn, preferred_element_type=F32)
         weight_grad = lax.psum_scatter(
@@ -1436,14 +1454,10 @@
     small = small.reshape(experts + 2, wt_count, shard_width).transpose(1, 0, 2)
     small = jnp.concatenate([small, gains[:, None]], axis=1)[planes]
     if dense:
-        out_total = add_send(out_total, out_parts[3])
+        small_low = step.take(small[1])
+        step.give(small_low)
+        small_total = ring(small_low)
         mixed_total = add_send(mixed_total, sums[3])
-        small_low = step.take(small[1])
-        small_total = ring(small_low)
-        out_total = sum_of([step.take(out_total), out_parts[0]], BF)
-        step.give(out_total)
-        out_x, out_y = swap(out_total, 2), swap(out_total, 4)
-        small_total = add_send(small_total, small[2], F32)
         grad_w_query, grad_w_key, grad_w_value = place_weight_pieces(
             step.take(weight_pieces), owners, share, head_dim
         )
@@ -1454,15 +1468,15 @@
         step.give(out_sent)
         out_pieces = [out_total, out_x, out_y, swap(out_sent[0], 4), swap(out_sent[1], 2)]
         out_pieces = out_pieces + [swap(piece, 1) for piece in out_pieces]
+        small_total = add_send(small_total, small[2], F32)
+        grad_w_output = place_row_pieces(step.take(out_pieces), owners, own_chunks)
+        step.give(grad_w_output)
+        grad_w_output = grad_w_output.reshape(w_output.shape)
         small_total = add_send(small_total, small[3], F32)
         output = step.take(mixed_total).astype(F32) + sums[0]
         output = (residual + output).astype(BF)
         step.give(output)
-        small = step.take(small_total) + small[0]
-        step.give(small)
-        grad_w_output = place_row_pieces(step.take(out_pieces), owners, own_chunks)
-        grad_w_output = grad_w_output.reshape(w_output.shape)
-        small = axis_sum(small, "ctx")
+        small = axis_sum(step.take(small_total) + small[0], "ctx")
     else:
         small = ring_sum([small[j] for j in range(wt_count)], F32)
         small = axis_sum(small, "ctx")

time: 757 us -> 762 us (level)
  Pallas kernels: 209 us -> 252 us
  waiting for transfers between devices: 257 us -> 223 us
  local copies, waits for them, and re-layouts: 127 us -> 114 us
    ppermute x31, waiting for transfers between devices: 121 us -> 90.2 us  [ring(): lax.ppermute(value, 'wt', [(i, (i + 1) % count) for i in range(count)])]
    pallas_call x18, Pallas kernels: 11.8 us -> 40.7 us  [sum_of(): pl.pallas_call(sum_kernel, out_shape=jax.ShapeDtypeStruct(values[0].shape...]
    unnamed x521 -> x435, local copies, waits for them, and re-layouts: 64.2 us -> 40.7 us
    ppermute x94, waiting for transfers between devices: 133 us -> 124 us  [swap(): return lax.ppermute(value, 'ctx', [(i, i ^ bit) for i in range(count)])]
  transfers between devices with their start and end apart: 130 -> 130, of which waited for: 61 -> 60; matrix products, arithmetic and copies ran while one was open for 11% -> 13% of each run, Pallas kernels for 25% -> 31%
where the time goes in v4:
time: 762 us; the launch traced here: 752 us
  Pallas kernels  252 us (33%)
  waiting for transfers between devices  223 us (29%)
  local copies, waits for them, and re-layouts  114 us (15%)
  starting transfers between devices  107 us (14%)
  other arithmetic  31.8 us (4%)
  between operations  19.1 us (3%)
    ppermute x94, waiting for transfers between devices, swap(): return lax.ppermute(value, 'ctx', [(i, i ^ bit) for i in range(count)])  124 us
    ppermute x31, waiting for transfers between devices, ring(): lax.ppermute(value, 'wt', [(i, (i + 1) % count) for i in range(count)])  90.2 us
    ppermute x94, starting transfers between devices, swap(): return lax.ppermute(value, 'ctx', [(i, i ^ bit) for i in range(count)])  78 us
    pallas_call x10, Pallas kernels, product(): pl.pallas_call(functools.partial(product_kernel, dims, None, len(lefts),...  59.5 us
    pallas_call x4, Pallas kernels, expert_rows(): pl.pallas_call(expert_kernel, out_shape=(low(width), low(width), low(ff),...  48.4 us
    pallas_call x18, Pallas kernels, sum_of(): pl.pallas_call(sum_kernel, out_shape=jax.ShapeDtypeStruct(values[0].shape...  40.7 us
    unnamed x435, local copies, waits for them, and re-layouts  40.7 us
    pallas_call x1, Pallas kernels, local(): pl.pallas_call(functools.partial(attend_back_kernel, heads, piece_count),...  30.6 us
  transfers between devices with their start and end apart: 130, of which 60 were waited for; matrix products, arithmetic and copies ran while one was open for 13% of the time, Pallas kernels for 31%

profile of v4, /device:TPU:0, one launch (start us, length us, event | category | flops | bytes accessed | tf_op | source)
XLA Modules:
  0.0 751.5 jit_solution(13965725988203078564)
XLA Ops:
  15.2 10.3 %collective-permute-done.1.refs_2_ = bf16[128,2048]{1,0:T(8,128)(2,1)S(1)} collective-permute-done((bf16[128,2048]{1,0:T(8,128)(2,1)S(1)}, bf16[128,2048]{1,0:T(8,128)(2,1)S(1)}, u32[]{:S(2)}, u32[]{:S(2)}) %collective-permute-start.1) | collective-permute-done | bytes 524320 | tf_op jit(solution)/shard_map/ppermute | solution.py:51
  71.4 14.3 %collective-permute-done.16 = bf16[512,768]{1,0:T(8,128)(2,1)} collective-permute-done((bf16[512,768]{1,0:T(8,128)(2,1)}, bf16[512,768]{1,0:T(8,128)(2,1)}, u32[]{:S(2)}, u32[]{:S(2)}) %collective-permute-start.16) | collective-permute-done | bytes 786464 | tf_op jit(solution)/shard_map/ppermute | solution.py:157
  104.8 13.3 %collective-permute-done.21 = bf16[512,768]{1,0:T(8,128)(2,1)S(1)} collective-permute-done((bf16[512,768]{1,0:T(8,128)(2,1)}, bf16[512,768]{1,0:T(8,128)(2,1)S(1)}, u32[]{:S(2)}, u32[]{:S(2)}) %collective-permute-start.21) | collective-permute-done | bytes 786464 | tf_op jit(solution)/shard_map/ppermute | solution.py:157
  130.3 19.2 %shard_map.306 = (bf16[1024,512]{1,0:T(8,128)(2,1)}, bf16[1024,128]{1,0:T(8,128)(2,1)}, bf16[1024,128]{1,0:T(8,128)(2,1)}, f32[1024,640]{1,0:T(8,128)}, bf16[16,64,512]{2,1,0:T(8,128)(2,1)}) custom-call(s32[16]{0:T(128)} %copy-done.201, s32[16]{0:T(128)} %select_reduce_fusion.place_ref, s32[8]{0:T(128)} %convert_reduce_fusion.2.first_ref, ...), custom_call_target="tpu_custom_call" | custom-call | flops 1 | bytes 1 | tf_op jit(solution)/shard_map/pallas_call | solution.py:1027
  165.7 7.2 collective-permute-done.27.refs_6_
  205.5 8.8 %collective-permute-done.36.refs_2_ = bf16[128,2048]{1,0:T(8,128)(2,1)S(1)} collective-permute-done((bf16[128,2048]{1,0:T(8,128)(2,1)S(1)}, bf16[128,2048]{1,0:T(8,128)(2,1)S(1)}, u32[]{:S(2)}, u32[]{:S(2)}) %collective-permute-start.36) | collective-permute-done | bytes 524320 | tf_op jit(solution)/shard_map/ppermute | solution.py:51
  227.6 7.9 %collective-permute-done.41.refs_2_ = bf16[128,2048]{1,0:T(8,128)(2,1)S(1)} collective-permute-done((bf16[128,2048]{1,0:T(8,128)(2,1)S(1)}, bf16[128,2048]{1,0:T(8,128)(2,1)S(1)}, u32[]{:S(2)}, u32[]{:S(2)}) %collective-permute-start.41) | collective-permute-done | bytes 524320 | tf_op jit(solution)/shard_map/ppermute | solution.py:51
  262.8 11.9 %shard_map.312 = (bf16[320,2048]{1,0:T(8,128)(2,1)S(1)}, bf16[320,2048]{1,0:T(8,128)(2,1)S(1)}, bf16[320,768]{1,0:T(8,128)(2,1)S(1)}, bf16[320,768]{1,0:T(8,128)...) custom-call(s32[1]{0:T(128)} %bitcast.29.expert_ref, ...), custom_call_target="tpu_custom_call" | custom-call | flops 1 | bytes 1 | tf_op jit(solution)/shard_map/pallas_call | solution.py:654
  299.7 12.1 %shard_map.314 = (bf16[320,2048]{1,0:T(8,128)(2,1)S(1)}, bf16[320,2048]{1,0:T(8,128)(2,1)S(1)}, bf16[320,768]{1,0:T(8,128)(2,1)S(1)}, bf16[320,768]{1,0:T(8,128)...) custom-call(s32[1]{0:T(128)} %bitcast.29.expert_ref, ...), custom_call_target="tpu_custom_call" | custom-call | flops 1 | bytes 1 | tf_op jit(solution)/shard_map/pallas_call | solution.py:654
  330.9 11.6 %collective-permute-done.56.refs_4_ = bf16[128,2048]{1,0:T(8,128)(2,1)} collective-permute-done((bf16[128,2048]{1,0:T(8,128)(2,1)}, bf16[128,2048]{1,0:T(8,128)(2,1)}, u32[]{:S(2)}, u32[]{:S(2)}) %collective-permute-start.56) | collective-permute-done | bytes 524320 | tf_op jit(solution)/shard_map/ppermute | solution.py:51
  345.1 12.1 %shard_map.316 = (bf16[320,2048]{1,0:T(8,128)(2,1)S(1)}, bf16[320,2048]{1,0:T(8,128)(2,1)S(1)}, bf16[320,768]{1,0:T(8,128)(2,1)S(1)}, bf16[320,768]{1,0:T(8,128)...) custom-call(s32[1]{0:T(128)} %bitcast.29.expert_ref, ...), custom_call_target="tpu_custom_call" | custom-call | flops 1 | bytes 1 | tf_op jit(solution)/shard_map/pallas_call | solution.py:654
  382.0 12.3 %shard_map.319 = (bf16[320,2048]{1,0:T(8,128)(2,1)S(1)}, bf16[320,2048]{1,0:T(8,128)(2,1)S(1)}, bf16[320,768]{1,0:T(8,128)(2,1)S(1)}, bf16[320,768]{1,0:T(8,128)...) custom-call(s32[1]{0:T(128)} %bitcast.29.expert_ref, ...), custom_call_target="tpu_custom_call" | custom-call | flops 1 | bytes 1 | tf_op jit(solution)/shard_map/pallas_call | solution.py:654
  408.9 7.9 %shard_map.323 = f32[2048,768]{1,0:T(8,128)} custom-call(s32[1]{0:T(128)} %constant.73.clone.1.start_ref, bf16[320,2048]{1,0:T(8,128)(2,1)S(1)} %copy-done.5, bf16[320,2048]{1,0:T(8,128)(2,1)} %collective-permute-done.42.other_ref.refs_1_, bf16[320,2048]{1,0:T(8,128)(2,1)S(1)} %copy-done.8, bf16[320,2048]{1,0:T(8,128)(2,1)} %collective-permute-done.48.other_ref.refs_3_, ...), custom_call_target="tpu_custom_call" | custom-call | flops 1 | bytes 1 | tf_op jit(solution)/shard_map/pallas_call | solution.py:839
  419.8 7.9 %shard_map.325 = f32[2048,768]{1,0:T(8,128)} custom-call(s32[1]{0:T(128)} %constant.73.clone.1.start_ref, bf16[320,2048]{1,0:T(8,128)(2,1)S(1)} %copy-done.5, bf16[320,2048]{1,0:T(8,128)(2,1)} %collective-permute-done.42.other_ref.refs_1_, bf16[320,2048]{1,0:T(8,128)(2,1)S(1)} %copy-done.8, bf16[320,2048]{1,0:T(8,128)(2,1)} %collective-permute-done.48.other_ref.refs_3_, ...), custom_call_target="tpu_custom_call" | custom-call | flops 1 | bytes 1 | tf_op jit(solution)/shard_map/pallas_call | solution.py:839
  451.1 6.3 shard_map.331
  468.0 8.2 %collective-permute-done.78.refs_2_.refs_3_ = bf16[128,2048]{1,0:T(8,128)(2,1)S(1)} collective-permute-done((bf16[128,2048]{1,0:T(8,128)(2,1)S(1)}, bf16[128,2048]{1,0:T(8,128)(2,1)S(1)}, u32[]{:S(2)}, u32[]{:S(2)}) %collective-permute-start.78) | collective-permute-done | bytes 524320 | tf_op jit(solution)/shard_map/ppermute | solution.py:51
  489.8 30.6 %shard_map.333 = (bf16[16,64,768]{2,1,0:T(8,128)(2,1)}, f32[1,128]{1,0:T(1,128)}, f32[1,128]{1,0:T(1,128)}) custom-call(s32[16]{0:T(128)} %select_reduce_fusion.place_ref, s32[8]{0:T(128)} %convert_reduce_fusion.2.first_ref, bf16[128,2048]{1,0:T(8,128)(2,1)} %copy-done.129, bf16[128,2048]{1,0:T(8,128)(2,1)} %copy-done.131, bf16[128,2048]{1,0:T(8,128)(2,1)} %copy-done.130, ...), custom_call_target="tpu_custom_call" | custom-call | flops 1 | bytes 1 | tf_op jit(solution)/shard_map/pallas_call | solution.py:1281
  532.2 6.6 shard_map.336
  538.7 8.1 %collective-permute-done.90.refs_0_ = bf16[512,768]{1,0:T(8,128)(2,1)S(1)} collective-permute-done((bf16[512,768]{1,0:T(8,128)(2,1)}, bf16[512,768]{1,0:T(8,128)(2,1)S(1)}, u32[]{:S(2)}, u32[]{:S(2)}) %collective-permute-start.90) | collective-permute-done | bytes 786464 | tf_op jit(solution)/shard_map/ppermute | solution.py:157
  552.0 6.2 shard_map.338
  558.3 12.3 %collective-permute-done.91.refs_0_ = bf16[512,768]{1,0:T(8,128)(2,1)S(1)} collective-permute-done((bf16[512,768]{1,0:T(8,128)(2,1)}, bf16[512,768]{1,0:T(8,128)(2,1)S(1)}, u32[]{:S(2)}, u32[]{:S(2)}) %collective-permute-start.91) | collective-permute-done | bytes 786464 | tf_op jit(solution)/shard_map/ppermute | solution.py:157
  610.0 6.2 collective-permute-start.96
  628.7 8.1 %collective-permute-done.97.refs_2_ = bf16[512,768]{1,0:T(8,128)(2,1)} collective-permute-done((bf16[512,768]{1,0:T(8,128)(2,1)}, bf16[512,768]{1,0:T(8,128)(2,1)}, u32[]{:S(2)}, u32[]{:S(2)}) %collective-permute-start.97) | collective-permute-done | bytes 786464 | tf_op jit(solution)/shard_map/ppermute | solution.py:51
  695.9 7.6 %shard_map.352 = (f32[512,4096]{1,0:T(8,128)}, f32[512,512]{1,0:T(8,128)}, f32[512,512]{1,0:T(8,128)}) custom-call(s32[8]{0:T(128)} %get-tuple-element.598.owner_ref, bf16[512,768]{1,0:T(8,128)(2,1)} %shard_map.343.refs_0_, bf16[512,768]{1,0:T(8,128)(2,1)} %collective-permute-done.96.refs_1_, bf16[512,768]{1,0:T(8,128)(2,1)} %collective-permute-done.97.refs_2_, ...), custom_call_target="tpu_custom_call" | custom-call | flops 1 | bytes 1 | tf_op jit(solution)/shard_map/pallas_call | solution.py:771
  (884 shorter events, 475.4 us)
Async XLA Ops:
  2.6 33.8 %collective-permute-start.9 = (bf16[128,2048]{1,0:T(8,128)(2,1)}, bf16[128,2048]{1,0:T(8,128)(2,1)}, u32[]{:S(2)}, u32[]{:S(2)}) collective-permute-start(bf16[128,2048]{1,0:T(8,128)(2,1)} %bitcast.5), channel_id=1, source_target_pairs={{0,1},{1,2},{2,3},{3,0},{4,5},{5,6},{6,7},{7,4},{8,9},{9,10},{10,1... | collective-permute-start | bytes 1572872 | tf_op jit(solution)/shard_map/ppermute | solution.py:157
  11.1 31.7 %collective-permute-start.4 = (bf16[128,2048]{1,0:T(8,128)(2,1)S(1)}, bf16[128,2048]{1,0:T(8,128)(2,1)S(1)}, u32[]{:S(2)}, u32[]{:S(2)}) collective-permute-start(bf16[128,2048]{1,0:T(8,128)(2,1)S(1)} %fusion.14.refs_0_), channel_id=1, source_target_pairs={{0,4},{4,0},{8,12},{12,8},{16,20},{20,16},{24,28},{28,24},{1,5},{5... | collective-permute-start | bytes 1572872 | tf_op jit(solution)/shard_map/ppermute | solution.py:51
  60.4 25.3 %collective-permute-start.16 = (bf16[512,768]{1,0:T(8,128)(2,1)}, bf16[512,768]{1,0:T(8,128)(2,1)}, u32[]{:S(2)}, u32[]{:S(2)}) collective-permute-start(bf16[512,768]{1,0:T(8,128)(2,1)} %collective-permute-done.10), channel_id=1, source_target_pairs={{0,1},{1,2},{2,3},{3,0},{4,5},{5,6},{6,7},{7,4},{8,9},{9,10},{10,1... | collective-permute-start | bytes 2359304 | tf_op jit(solution)/shard_map/ppermute | solution.py:157
  90.0 28.2 %collective-permute-start.21 = (bf16[512,768]{1,0:T(8,128)(2,1)}, bf16[512,768]{1,0:T(8,128)(2,1)S(1)}, u32[]{:S(2)}, u32[]{:S(2)}) collective-permute-start(bf16[512,768]{1,0:T(8,128)(2,1)} %collective-permute-done.16), channel_id=1, source_target_pairs={{0,1},{1,2},{2,3},{3,0},{4,5},{5,6},{6,7},{7,4},{8,9},{9,10},{10,1... | collective-permute-start | bytes 2359304 | tf_op jit(solution)/shard_map/ppermute | solution.py:157
  120.4 31.6 %all-to-all-start = ((bf16[8,64,2048]{2,1,0:T(8,128)(2,1)}), bf16[8,64,2048]{2,1,0:T(8,128)(2,1)}, u32[]{:S(2)}, u32[]{:S(2)}) async-start(bf16[8,64,2048]{2,1,0:T(8,128)(2,1)} %bitcast.166), calls=%async_computation | async-start | bytes 4194304 | tf_op jit(solution)/shard_map/all_to_all | solution.py:1008
  156.4 25.2 %collective-permute-start.30 = (bf16[192,128]{1,0:T(8,128)(2,1)S(1)}, bf16[192,128]{1,0:T(8,128)(2,1)S(1)}, u32[]{:S(2)}, u32[]{:S(2)}) collective-permute-start(bf16[192,128]{1,0:T(8,128)(2,1)S(1)} %collective-permute-done.24), channel_id=1, source_target_pairs={{0,1},{1,2},{2,3},{3,0},{4,5},{5,6},{6,7},{7,4},{8,9},{9,10},{10,1... | collective-permute-start | bytes 147464 | tf_op jit(solution)/shard_map/ppermute | solution.py:157
  156.4 29.3 %collective-permute-start.31 = (bf16[128,2048]{1,0:T(8,128)(2,1)S(1)}, bf16[128,2048]{1,0:T(8,128)(2,1)}, u32[]{:S(2)}, u32[]{:S(2)}) collective-permute-start(bf16[128,2048]{1,0:T(8,128)(2,1)S(1)} %collective-permute-done.18.refs_7_), channel_id=1, source_target_pairs={{0,1},{1,2},{2,3},{3,0},{4,5},{5,6},{6,7},{7,4},{8,9},{9,10},{10,1... | collective-permute-start | bytes 1572872 | tf_op jit(solution)/shard_map/ppermute | solution.py:157
  159.2 36.9 %collective-permute-start.34 = (bf16[128,2048]{1,0:T(8,128)(2,1)}, bf16[128,2048]{1,0:T(8,128)(2,1)}, u32[]{:S(2)}, u32[]{:S(2)}) collective-permute-start(bf16[128,2048]{1,0:T(8,128)(2,1)} %constant_dynamic-update-slice_fusion.5), channel_id=1, source_target_pairs={{0,1},{1,2},{2,3},{3,0},{4,5},{5,6},{6,7},{7,4},{8,9},{9,10},{10,1... | collective-permute-start | bytes 1572872 | tf_op jit(solution)/shard_map/ppermute | solution.py:157
  218.0 25.2 %collective-permute-start.45 = (bf16[256,2048]{1,0:T(8,128)(2,1)S(1)}, bf16[256,2048]{1,0:T(8,128)(2,1)}, u32[]{:S(2)}, u32[]{:S(2)}) collective-permute-start(bf16[256,2048]{1,0:T(8,128)(2,1)S(1)} %pad_maximum_fusion), channel_id=1, source_target_pairs={{0,1},{1,2},{2,3},{3,0},{4,5},{5,6},{6,7},{7,4},{8,9},{9,10},{10,1... | collective-permute-start | bytes 3145736 | tf_op jit(solution)/shard_map/ppermute | solution.py:157
  250.6 25.0 %collective-permute-start.47 = (bf16[256,2048]{1,0:T(8,128)(2,1)}, bf16[256,2048]{1,0:T(8,128)(2,1)}, u32[]{:S(2)}, u32[]{:S(2)}) collective-permute-start(bf16[256,2048]{1,0:T(8,128)(2,1)} %collective-permute-done.45.refs_0_), channel_id=1, source_target_pairs={{0,16},{4,20},{8,24},{12,28},{16,0},{20,4},{24,8},{28,12},{1,17},{... | collective-permute-start | bytes 3145736 | tf_op jit(solution)/shard_map/ppermute | solution.py:51
  252.3 24.5 %collective-permute-start.46 = (bf16[256,2048]{1,0:T(8,128)(2,1)}, bf16[256,2048]{1,0:T(8,128)(2,1)}, u32[]{:S(2)}, u32[]{:S(2)}) collective-permute-start(bf16[256,2048]{1,0:T(8,128)(2,1)} %collective-permute-done.45.refs_0_), channel_id=1, source_target_pairs={{0,8},{4,12},{8,0},{12,4},{16,24},{20,28},{24,16},{28,20},{1,9},{5... | collective-permute-start | bytes 3145736 | tf_op jit(solution)/shard_map/ppermute | solution.py:51
  253.1 33.7 %collective-permute-start.51 = (bf16[256,2048]{1,0:T(8,128)(2,1)}, bf16[256,2048]{1,0:T(8,128)(2,1)}, u32[]{:S(2)}, u32[]{:S(2)}) collective-permute-start(bf16[256,2048]{1,0:T(8,128)(2,1)} %collective-permute-done.45.refs_0_), channel_id=1, source_target_pairs={{0,1},{1,2},{2,3},{3,0},{4,5},{5,6},{6,7},{7,4},{8,9},{9,10},{10,1... | collective-permute-start | bytes 3145736 | tf_op jit(solution)/shard_map/ppermute | solution.py:157
  330.3 35.1 %collective-permute-start.58 = (bf16[320,2048]{1,0:T(8,128)(2,1)}, bf16[320,2048]{1,0:T(8,128)(2,1)S(1)}, u32[]{:S(2)}, u32[]{:S(2)}) collective-permute-start(bf16[320,2048]{1,0:T(8,128)(2,1)} %copy-done.111), channel_id=1, source_target_pairs={{0,4},{4,0},{8,12},{12,8},{16,20},{20,16},{24,28},{28,24},{1,5},{5... | collective-permute-start | bytes 3932168 | tf_op jit(solution)/shard_map/ppermute | solution.py:51
  330.4 35.1 %collective-permute-start.59 = (bf16[320,2048]{1,0:T(8,128)(2,1)}, bf16[320,2048]{1,0:T(8,128)(2,1)S(1)}, u32[]{:S(2)}, u32[]{:S(2)}) collective-permute-start(bf16[320,2048]{1,0:T(8,128)(2,1)} %copy-done.112), channel_id=1, source_target_pairs={{0,4},{4,0},{8,12},{12,8},{16,20},{20,16},{24,28},{28,24},{1,5},{5... | collective-permute-start | bytes 3932168 | tf_op jit(solution)/shard_map/ppermute | solution.py:51
  487.1 33.2 %collective-permute-start.86 = (bf16[256,2048]{1,0:T(8,128)(2,1)}, bf16[256,2048]{1,0:T(8,128)(2,1)}, u32[]{:S(2)}, u32[]{:S(2)}) collective-permute-start(bf16[256,2048]{1,0:T(8,128)(2,1)} %get-tuple-element.456), channel_id=1, source_target_pairs={{0,16},{4,20},{8,24},{12,28},{16,0},{20,4},{24,8},{28,12},{1,17},{... | collective-permute-start | bytes 3145736 | tf_op jit(solution)/shard_map/ppermute | solution.py:51
  488.1 32.3 %collective-permute-start.87 = (bf16[256,2048]{1,0:T(8,128)(2,1)}, bf16[256,2048]{1,0:T(8,128)(2,1)}, u32[]{:S(2)}, u32[]{:S(2)}) collective-permute-start(bf16[256,2048]{1,0:T(8,128)(2,1)} %get-tuple-element.457), channel_id=1, source_target_pairs={{0,8},{4,12},{8,0},{12,4},{16,24},{20,28},{24,16},{28,20},{1,9},{5... | collective-permute-start | bytes 3145736 | tf_op jit(solution)/shard_map/ppermute | solution.py:51
  550.5 48.9 %collective-permute-start.88 = (bf16[512,2048]{1,0:T(8,128)(2,1)}, bf16[512,2048]{1,0:T(8,128)(2,1)}, u32[]{:S(2)}, u32[]{:S(2)}) collective-permute-start(bf16[512,2048]{1,0:T(8,128)(2,1)} %get-tuple-element.468), channel_id=1, source_target_pairs={{0,8},{4,12},{8,0},{12,4},{16,24},{20,28},{24,16},{28,20},{1,9},{5... | collective-permute-start | bytes 6291464 | tf_op jit(solution)/shard_map/ppermute | solution.py:51
  551.0 48.9 %collective-permute-start.89 = (bf16[512,2048]{1,0:T(8,128)(2,1)}, bf16[512,2048]{1,0:T(8,128)(2,1)}, u32[]{:S(2)}, u32[]{:S(2)}) collective-permute-start(bf16[512,2048]{1,0:T(8,128)(2,1)} %get-tuple-element.469), channel_id=1, source_target_pairs={{0,16},{4,20},{8,24},{12,28},{16,0},{20,4},{24,8},{28,12},{1,17},{... | collective-permute-start | bytes 6291464 | tf_op jit(solution)/shard_map/ppermute | solution.py:51
  579.4 36.8 %collective-permute-start.92 = (bf16[512,2048]{1,0:T(8,128)(2,1)}, bf16[512,2048]{1,0:T(8,128)(2,1)}, u32[]{:S(2)}, u32[]{:S(2)}) collective-permute-start(bf16[512,2048]{1,0:T(8,128)(2,1)} %shard_map.340), channel_id=1, source_target_pairs={{0,4},{4,0},{8,12},{12,8},{16,20},{20,16},{24,28},{28,24},{1,5},{5... | collective-permute-start | bytes 6291464 | tf_op jit(solution)/shard_map/ppermute | solution.py:51
  579.4 43.0 %all-to-all-start.1 = ((bf16[8,64,2048]{2,1,0:T(8,128)(2,1)}), bf16[8,64,2048]{2,1,0:T(8,128)(2,1)}, u32[]{:S(2)}, u32[]{:S(2)}) async-start(bf16[8,64,2048]{2,1,0:T(8,128)(2,1)} %bitcast.167), calls=%async_computation.1 | async-start | bytes 4194304 | tf_op jit(solution)/shard_map/all_to_all | solution.py:1352
  608.5 28.3 %collective-permute-start.97 = (bf16[512,768]{1,0:T(8,128)(2,1)}, bf16[512,768]{1,0:T(8,128)(2,1)}, u32[]{:S(2)}, u32[]{:S(2)}) collective-permute-start(bf16[512,768]{1,0:T(8,128)(2,1)} %shard_map.343.refs_0_), channel_id=1, source_target_pairs={{0,16},{4,20},{8,24},{12,28},{16,0},{20,4},{24,8},{28,12},{1,17},{... | collective-permute-start | bytes 2359304 | tf_op jit(solution)/shard_map/ppermute | solution.py:51
  610.0 26.7 %collective-permute-start.96 = (bf16[512,768]{1,0:T(8,128)(2,1)}, bf16[512,768]{1,0:T(8,128)(2,1)}, u32[]{:S(2)}, u32[]{:S(2)}) collective-permute-start(bf16[512,768]{1,0:T(8,128)(2,1)} %shard_map.343.refs_0_), channel_id=1, source_target_pairs={{0,8},{4,12},{8,0},{12,4},{16,24},{20,28},{24,16},{28,20},{1,9},{5... | collective-permute-start | bytes 2359304 | tf_op jit(solution)/shard_map/ppermute | solution.py:51
  626.6 36.9 %collective-permute-start.111 = (bf16[512,768]{1,0:T(8,128)(2,1)S(1)}, bf16[512,768]{1,0:T(8,128)(2,1)}, u32[]{:S(2)}, u32[]{:S(2)}) collective-permute-start(bf16[512,768]{1,0:T(8,128)(2,1)S(1)} %copy-done.132), channel_id=1, source_target_pairs={{0,4},{4,0},{8,12},{12,8},{16,20},{20,16},{24,28},{28,24},{1,5},{5... | collective-permute-start | bytes 2359304 | tf_op jit(solution)/shard_map/ppermute | solution.py:51
  644.6 23.5 %collective-permute-start.94 = (bf16[128,2048]{1,0:T(8,128)(2,1)}, bf16[128,2048]{1,0:T(8,128)(2,1)}, u32[]{:S(2)}, u32[]{:S(2)}) collective-permute-start(bf16[128,2048]{1,0:T(8,128)(2,1)} %slice.393), channel_id=1, source_target_pairs={{0,1},{1,2},{2,3},{3,0},{4,5},{5,6},{6,7},{7,4},{8,9},{9,10},{10,1... | collective-permute-start | bytes 1572872 | tf_op jit(solution)/shard_map/ppermute | solution.py:157
  (321 other events, 3446.4 us)

commit v5 on v3

--- a/solution.py
+++ b/solution.py
@@ -993,7 +993,7 @@
         out_pieces, weight = keep(3, buffers, ticks[3])
         tinies.append(ring(after(tinies[2], weight)))
         cot_next = [ring(after(p, weight)) for p in (cot, cot_x, cot_y, cot_diag)]
-        nears = [tiny[:near_rows] for tiny in tinies]
+        tinies_later = tinies[1:]
         router = jnp.stack([tiny[near_rows:].reshape(experts, shard_width) for tiny in tinies])
         router = router[planes].transpose(1, 0, 2).reshape(experts, model_width)
     else:
@@ -1058,7 +1058,9 @@
         )
 
         def fill(sends):
-            later_tables.extend(tables(after(jnp.concatenate(nears[1:], axis=0), sends)))
+            rows = after(tinies_later, sends)
+            rows = jnp.concatenate([t[:near_rows] for t in rows], axis=0)
+            later_tables.extend(tables(rows))
             return tuple(later_tables) + (cot_next[2],)
 
         attn = plane_scatter(out_project, attn_rows, fill, (), (cot_next[3],))
@@ -1270,7 +1272,7 @@
     grad_pieces = plane_gather(grad_residual.astype(BF))
     if dense:
         out_grad = product(
-            [attn_rows], grad_pieces, ((0,), (0,)), (head_cols, model_width), BF, limit=40
+            [attn_rows], grad_pieces, ((0,), (0,)), (head_cols, model_width), BF
         )
     else:
         out_grad = lax.dot_general(
@@ -1299,7 +1301,7 @@
             pltpu.VMEM((seq_len, head_dim), F32),
             pltpu.VMEM((2 * ctx_count, half_rows, head_cols), BF),
         ],
-        compiler_params=pltpu.CompilerParams(vmem_limit_bytes=40 << 20),
+        compiler_params=pltpu.CompilerParams(vmem_limit_bytes=ATTEND_LIMIT),
         cost_estimate=COST,
     )(
         places,

time: 757 us -> 750 us (level)
  waiting for transfers between devices: 257 us -> 234 us
  Pallas kernels: 209 us -> 226 us
  local copies, waits for them, and re-layouts: 127 us -> 119 us
    ppermute x31, waiting for transfers between devices: 121 us -> 106 us  [ring(): lax.ppermute(value, 'wt', [(i, (i + 1) % count) for i in range(count)])]
    unnamed x521 -> x429, local copies, waits for them, and re-layouts: 64.2 us -> 51.5 us
    pallas_call x1, Pallas kernels: 23.2 us -> 33.2 us  [local(): pl.pallas_call(functools.partial(attend_back_kernel, heads, piece_count),...]
    ppermute x94, waiting for transfers between devices: 133 us -> 123 us  [swap(): return lax.ppermute(value, 'ctx', [(i, i ^ bit) for i in range(count)])]
    ppermute x31, starting transfers between devices: 16.5 us -> 24.6 us  [ring(): lax.ppermute(value, 'wt', [(i, (i + 1) % count) for i in range(count)])]
  transfers between devices with their start and end apart: 130 -> 130, of which waited for: 61 -> 63; matrix products, arithmetic and copies ran while one was open for 11% -> 13% of each run, Pallas kernels for 25% -> 27%
where the time goes in v5:
time: 750 us; the launch traced here: 741 us
  waiting for transfers between devices  234 us (31%)
  Pallas kernels  226 us (30%)
  local copies, waits for them, and re-layouts  119 us (16%)
  starting transfers between devices  107 us (14%)
  other arithmetic  30.3 us (4%)
  between operations  19.3 us (3%)
    ppermute x94, waiting for transfers between devices, swap(): return lax.ppermute(value, 'ctx', [(i, i ^ bit) for i in range(count)])  123 us
    ppermute x31, waiting for transfers between devices, ring(): lax.ppermute(value, 'wt', [(i, (i + 1) % count) for i in range(count)])  106 us
    ppermute x94, starting transfers between devices, swap(): return lax.ppermute(value, 'ctx', [(i, i ^ bit) for i in range(count)])  71.1 us
    pallas_call x10, Pallas kernels, product(): pl.pallas_call(functools.partial(product_kernel, dims, None, len(lefts),...  59.4 us
    unnamed x429, local copies, waits for them, and re-layouts  51.5 us
    pallas_call x4, Pallas kernels, expert_rows(): pl.pallas_call(expert_kernel, out_shape=(low(width), low(width), low(ff),...  48.4 us
    pallas_call x1, Pallas kernels, local(): pl.pallas_call(functools.partial(attend_back_kernel, heads, piece_count),...  33.2 us
    ppermute x31, starting transfers between devices, ring(): lax.ppermute(value, 'wt', [(i, (i + 1) % count) for i in range(count)])  24.6 us
  transfers between devices with their start and end apart: 130, of which 63 were waited for; matrix products, arithmetic and copies ran while one was open for 13% of the time, Pallas kernels for 27%

profile of v5, /device:TPU:0, one launch (start us, length us, event | category | flops | bytes accessed | tf_op | source)
XLA Modules:
  0.0 740.9 jit_solution(886479752347969785)
XLA Ops:
  15.1 10.2 %collective-permute-done.1.refs_2_ = bf16[128,2048]{1,0:T(8,128)(2,1)S(1)} collective-permute-done((bf16[128,2048]{1,0:T(8,128)(2,1)S(1)}, bf16[128,2048]{1,0:T(8,128)(2,1)S(1)}, u32[]{:S(2)}, u32[]{:S(2)}) %collective-permute-start.1) | collective-permute-done | bytes 524320 | tf_op jit(solution)/shard_map/ppermute | solution.py:51
  70.5 14.9 %collective-permute-done.16 = bf16[512,768]{1,0:T(8,128)(2,1)} collective-permute-done((bf16[512,768]{1,0:T(8,128)(2,1)}, bf16[512,768]{1,0:T(8,128)(2,1)}, u32[]{:S(2)}, u32[]{:S(2)}) %collective-permute-start.16) | collective-permute-done | bytes 786464 | tf_op jit(solution)/shard_map/ppermute | solution.py:158
  104.6 14.0 %collective-permute-done.21 = bf16[512,768]{1,0:T(8,128)(2,1)S(1)} collective-permute-done((bf16[512,768]{1,0:T(8,128)(2,1)}, bf16[512,768]{1,0:T(8,128)(2,1)S(1)}, u32[]{:S(2)}, u32[]{:S(2)}) %collective-permute-start.21) | collective-permute-done | bytes 786464 | tf_op jit(solution)/shard_map/ppermute | solution.py:158
  129.6 20.5 %shard_map.306 = (bf16[1024,512]{1,0:T(8,128)(2,1)}, bf16[1024,128]{1,0:T(8,128)(2,1)}, bf16[1024,128]{1,0:T(8,128)(2,1)}, f32[1024,640]{1,0:T(8,128)}, bf16[16,64,512]{2,1,0:T(8,128)(2,1)}) custom-call(s32[16]{0:T(128)} %copy-done.198, s32[16]{0:T(128)} %select_reduce_fusion.place_ref, s32[8]{0:T(128)} %convert_reduce_fusion.2.first_ref, ...), custom_call_target="tpu_custom_call" | custom-call | flops 1 | bytes 1 | tf_op jit(solution)/shard_map/pallas_call | solution.py:1024
  189.3 8.1 %collective-permute-done.32 = bf16[128,2048]{1,0:T(8,128)(2,1)S(1)} collective-permute-done((bf16[128,2048]{1,0:T(8,128)(2,1)S(1)}, bf16[128,2048]{1,0:T(8,128)(2,1)S(1)}, u32[]{:S(2)}, u32[]{:S(2)}) %collective-permute-start.32) | collective-permute-done | bytes 524320 | tf_op jit(solution)/shard_map/ppermute | solution.py:51
  239.6 6.6 collective-permute-done.44.refs_4_
  264.2 12.0 %shard_map.312 = (bf16[320,2048]{1,0:T(8,128)(2,1)S(1)}, bf16[320,2048]{1,0:T(8,128)(2,1)S(1)}, bf16[320,768]{1,0:T(8,128)(2,1)S(1)}, bf16[320,768]{1,0:T(8,128)...) custom-call(s32[1]{0:T(128)} %bitcast.29.expert_ref, ...), custom_call_target="tpu_custom_call" | custom-call | flops 1 | bytes 1 | tf_op jit(solution)/shard_map/pallas_call | solution.py:655
  299.5 12.0 %shard_map.314 = (bf16[320,2048]{1,0:T(8,128)(2,1)S(1)}, bf16[320,2048]{1,0:T(8,128)(2,1)S(1)}, bf16[320,768]{1,0:T(8,128)(2,1)S(1)}, bf16[320,768]{1,0:T(8,128)...) custom-call(s32[1]{0:T(128)} %bitcast.29.expert_ref, ...), custom_call_target="tpu_custom_call" | custom-call | flops 1 | bytes 1 | tf_op jit(solution)/shard_map/pallas_call | solution.py:655
  330.7 12.2 %collective-permute-done.56.refs_4_ = bf16[128,2048]{1,0:T(8,128)(2,1)} collective-permute-done((bf16[128,2048]{1,0:T(8,128)(2,1)}, bf16[128,2048]{1,0:T(8,128)(2,1)}, u32[]{:S(2)}, u32[]{:S(2)}) %collective-permute-start.56) | collective-permute-done | bytes 524320 | tf_op jit(solution)/shard_map/ppermute | solution.py:51
  345.1 12.3 %shard_map.316 = (bf16[320,2048]{1,0:T(8,128)(2,1)S(1)}, bf16[320,2048]{1,0:T(8,128)(2,1)S(1)}, bf16[320,768]{1,0:T(8,128)(2,1)S(1)}, bf16[320,768]{1,0:T(8,128)...) custom-call(s32[1]{0:T(128)} %bitcast.29.expert_ref, ...), custom_call_target="tpu_custom_call" | custom-call | flops 1 | bytes 1 | tf_op jit(solution)/shard_map/pallas_call | solution.py:655
  357.6 6.2 shard_map.317
  379.9 12.1 %shard_map.319 = (bf16[320,2048]{1,0:T(8,128)(2,1)S(1)}, bf16[320,2048]{1,0:T(8,128)(2,1)S(1)}, bf16[320,768]{1,0:T(8,128)(2,1)S(1)}, bf16[320,768]{1,0:T(8,128)...) custom-call(s32[1]{0:T(128)} %bitcast.29.expert_ref, ...), custom_call_target="tpu_custom_call" | custom-call | flops 1 | bytes 1 | tf_op jit(solution)/shard_map/pallas_call | solution.py:655
  408.2 7.9 %shard_map.323 = f32[2048,768]{1,0:T(8,128)} custom-call(s32[1]{0:T(128)} %constant.73.clone.1.start_ref, bf16[320,2048]{1,0:T(8,128)(2,1)S(1)} %copy-done.7, bf16[320,2048]{1,0:T(8,128)(2,1)} %collective-permute-done.42.other_ref.refs_1_, bf16[320,2048]{1,0:T(8,128)(2,1)S(1)} %copy-done.10, bf16[320,2048]{1,0:T(8,128)(2,1)} %collective-permute-done.48.other_ref.refs_3_, ...), custom_call_target="tpu_custom_call" | custom-call | flops 1 | bytes 1 | tf_op jit(solution)/shard_map/pallas_call | solution.py:836
  418.1 8.0 %shard_map.325 = f32[2048,768]{1,0:T(8,128)} custom-call(s32[1]{0:T(128)} %constant.73.clone.1.start_ref, bf16[320,2048]{1,0:T(8,128)(2,1)S(1)} %copy-done.7, bf16[320,2048]{1,0:T(8,128)(2,1)} %collective-permute-done.42.other_ref.refs_1_, bf16[320,2048]{1,0:T(8,128)(2,1)S(1)} %copy-done.10, bf16[320,2048]{1,0:T(8,128)(2,1)} %collective-permute-done.48.other_ref.refs_3_, ...), custom_call_target="tpu_custom_call" | custom-call | flops 1 | bytes 1 | tf_op jit(solution)/shard_map/pallas_call | solution.py:836
  435.6 6.2 shard_map.329
  465.9 8.3 %collective-permute-done.78.refs_3_.refs_2_ = bf16[128,2048]{1,0:T(8,128)(2,1)S(1)} collective-permute-done((bf16[128,2048]{1,0:T(8,128)(2,1)S(1)}, bf16[128,2048]{1,0:T(8,128)(2,1)S(1)}, u32[]{:S(2)}, u32[]{:S(2)}) %collective-permute-start.78) | collective-permute-done | bytes 524320 | tf_op jit(solution)/shard_map/ppermute | solution.py:51
  500.5 33.2 %shard_map.334 = (bf16[16,64,768]{2,1,0:T(8,128)(2,1)}, f32[1,128]{1,0:T(1,128)}, f32[1,128]{1,0:T(1,128)}) custom-call(s32[16]{0:T(128)} %select_reduce_fusion.place_ref, s32[8]{0:T(128)} %convert_reduce_fusion.2.first_ref, bf16[128,2048]{1,0:T(8,128)(2,1)} %copy-done.146, bf16[128,2048]{1,0:T(8,128)(2,1)} %copy-done.149, bf16[128,2048]{1,0:T(8,128)(2,1)} %copy-done.148, ...), custom_call_target="tpu_custom_call" | custom-call | flops 1 | bytes 1 | tf_op jit(solution)/shard_map/pallas_call | solution.py:1288
  552.8 6.6 shard_map.337
  573.2 16.6 %collective-permute-done.91.refs_0_ = bf16[512,768]{1,0:T(8,128)(2,1)} collective-permute-done((bf16[512,768]{1,0:T(8,128)(2,1)S(1)}, bf16[512,768]{1,0:T(8,128)(2,1)}, u32[]{:S(2)}, u32[]{:S(2)}) %collective-permute-start.91) | collective-permute-done | bytes 786464 | tf_op jit(solution)/shard_map/ppermute | solution.py:158
  623.9 11.9 %collective-permute-done.99.refs_2_ = bf16[512,768]{1,0:T(8,128)(2,1)} collective-permute-done((bf16[512,768]{1,0:T(8,128)(2,1)S(1)}, bf16[512,768]{1,0:T(8,128)(2,1)}, u32[]{:S(2)}, u32[]{:S(2)}) %collective-permute-start.99) | collective-permute-done | bytes 786464 | tf_op jit(solution)/shard_map/ppermute | solution.py:51
  648.3 10.3 %collective-permute-done.101.refs_0_ = bf16[128,2048]{1,0:T(8,128)(2,1)S(1)} collective-permute-done((bf16[128,2048]{1,0:T(8,128)(2,1)S(1)}, bf16[128,2048]{1,0:T(8,128)(2,1)S(1)}, u32[]{:S(2)}, u32[]{:S(2)}) %collective-permute-start.101) | collective-permute-done | bytes 524320 | tf_op jit(solution)/shard_map/ppermute | solution.py:158
  662.0 6.6 collective-permute-done.110.refs_3_
  668.6 7.4 collective-permute-done.100.refs_0_
  693.7 7.6 %shard_map.353 = (f32[512,4096]{1,0:T(8,128)}, f32[512,512]{1,0:T(8,128)}, f32[512,512]{1,0:T(8,128)}) custom-call(s32[8]{0:T(128)} %get-tuple-element.600.owner_ref, bf16[512,768]{1,0:T(8,128)(2,1)} %copy-done.35, bf16[512,768]{1,0:T(8,128)(2,1)} %collective-permute-done.98.refs_1_, bf16[512,768]{1,0:T(8,128)(2,1)} %collective-permute-done.99.refs_2_, ...), custom_call_target="tpu_custom_call" | custom-call | flops 1 | bytes 1 | tf_op jit(solution)/shard_map/pallas_call | solution.py:772
  (880 shorter events, 449.9 us)
Async XLA Ops:
  2.6 33.7 %collective-permute-start.9 = (bf16[128,2048]{1,0:T(8,128)(2,1)}, bf16[128,2048]{1,0:T(8,128)(2,1)}, u32[]{:S(2)}, u32[]{:S(2)}) collective-permute-start(bf16[128,2048]{1,0:T(8,128)(2,1)} %bitcast.5), channel_id=1, source_target_pairs={{0,1},{1,2},{2,3},{3,0},{4,5},{5,6},{6,7},{7,4},{8,9},{9,10},{10,1... | collective-permute-start | bytes 1572872 | tf_op jit(solution)/shard_map/ppermute | solution.py:158
  11.0 31.8 %collective-permute-start.4 = (bf16[128,2048]{1,0:T(8,128)(2,1)S(1)}, bf16[128,2048]{1,0:T(8,128)(2,1)S(1)}, u32[]{:S(2)}, u32[]{:S(2)}) collective-permute-start(bf16[128,2048]{1,0:T(8,128)(2,1)S(1)} %fusion.14.refs_0_), channel_id=1, source_target_pairs={{0,4},{4,0},{8,12},{12,8},{16,20},{20,16},{24,28},{28,24},{1,5},{5... | collective-permute-start | bytes 1572872 | tf_op jit(solution)/shard_map/ppermute | solution.py:51
  59.5 25.9 %collective-permute-start.16 = (bf16[512,768]{1,0:T(8,128)(2,1)}, bf16[512,768]{1,0:T(8,128)(2,1)}, u32[]{:S(2)}, u32[]{:S(2)}) collective-permute-start(bf16[512,768]{1,0:T(8,128)(2,1)} %collective-permute-done.10), channel_id=1, source_target_pairs={{0,1},{1,2},{2,3},{3,0},{4,5},{5,6},{6,7},{7,4},{8,9},{9,10},{10,1... | collective-permute-start | bytes 2359304 | tf_op jit(solution)/shard_map/ppermute | solution.py:158
  89.2 29.3 %collective-permute-start.21 = (bf16[512,768]{1,0:T(8,128)(2,1)}, bf16[512,768]{1,0:T(8,128)(2,1)S(1)}, u32[]{:S(2)}, u32[]{:S(2)}) collective-permute-start(bf16[512,768]{1,0:T(8,128)(2,1)} %collective-permute-done.16), channel_id=1, source_target_pairs={{0,1},{1,2},{2,3},{3,0},{4,5},{5,6},{6,7},{7,4},{8,9},{9,10},{10,1... | collective-permute-start | bytes 2359304 | tf_op jit(solution)/shard_map/ppermute | solution.py:158
  119.9 36.5 %all-to-all-start = ((bf16[8,64,2048]{2,1,0:T(8,128)(2,1)}), bf16[8,64,2048]{2,1,0:T(8,128)(2,1)}, u32[]{:S(2)}, u32[]{:S(2)}) async-start(bf16[8,64,2048]{2,1,0:T(8,128)(2,1)} %bitcast.163), calls=%async_computation | async-start | bytes 4194304 | tf_op jit(solution)/shard_map/all_to_all | solution.py:1005
  126.8 27.2 %collective-permute-start.26 = (bf16[128,2048]{1,0:T(8,128)(2,1)S(1)}, bf16[128,2048]{1,0:T(8,128)(2,1)S(1)}, u32[]{:S(2)}, u32[]{:S(2)}) collective-permute-start(bf16[128,2048]{1,0:T(8,128)(2,1)S(1)} %collective-permute-done.17.refs_6_), channel_id=1, source_target_pairs={{0,1},{1,2},{2,3},{3,0},{4,5},{5,6},{6,7},{7,4},{8,9},{9,10},{10,1... | collective-permute-start | bytes 1572872 | tf_op jit(solution)/shard_map/ppermute | solution.py:158
  160.9 28.4 %collective-permute-start.34 = (bf16[128,2048]{1,0:T(8,128)(2,1)}, bf16[128,2048]{1,0:T(8,128)(2,1)}, u32[]{:S(2)}, u32[]{:S(2)}) collective-permute-start(bf16[128,2048]{1,0:T(8,128)(2,1)} %constant_dynamic-update-slice_fusion.5), channel_id=1, source_target_pairs={{0,1},{1,2},{2,3},{3,0},{4,5},{5,6},{6,7},{7,4},{8,9},{9,10},{10,1... | collective-permute-start | bytes 1572872 | tf_op jit(solution)/shard_map/ppermute | solution.py:158
  237.4 24.7 %collective-permute-start.42 = (bf16[320,2048]{1,0:T(8,128)(2,1)}, bf16[320,2048]{1,0:T(8,128)(2,1)}, u32[]{:S(2)}, u32[]{:S(2)}) collective-permute-start(bf16[320,2048]{1,0:T(8,128)(2,1)} %get-tuple-element.315), channel_id=1, source_target_pairs={{0,4},{4,0},{8,12},{12,8},{16,20},{20,16},{24,28},{28,24},{1,5},{5... | collective-permute-start | bytes 3932168 | tf_op jit(solution)/shard_map/ppermute | solution.py:51
  248.0 29.4 %collective-permute-start.47 = (bf16[256,2048]{1,0:T(8,128)(2,1)}, bf16[256,2048]{1,0:T(8,128)(2,1)}, u32[]{:S(2)}, u32[]{:S(2)}) collective-permute-start(bf16[256,2048]{1,0:T(8,128)(2,1)} %collective-permute-done.45.refs_0_), channel_id=1, source_target_pairs={{0,16},{4,20},{8,24},{12,28},{16,0},{20,4},{24,8},{28,12},{1,17},{... | collective-permute-start | bytes 3145736 | tf_op jit(solution)/shard_map/ppermute | solution.py:51
  248.7 28.7 %collective-permute-start.46 = (bf16[256,2048]{1,0:T(8,128)(2,1)}, bf16[256,2048]{1,0:T(8,128)(2,1)}, u32[]{:S(2)}, u32[]{:S(2)}) collective-permute-start(bf16[256,2048]{1,0:T(8,128)(2,1)} %collective-permute-done.45.refs_0_), channel_id=1, source_target_pairs={{0,8},{4,12},{8,0},{12,4},{16,24},{20,28},{24,16},{28,20},{1,9},{5... | collective-permute-start | bytes 3145736 | tf_op jit(solution)/shard_map/ppermute | solution.py:51
  249.3 39.1 %collective-permute-start.51 = (bf16[256,2048]{1,0:T(8,128)(2,1)}, bf16[256,2048]{1,0:T(8,128)(2,1)}, u32[]{:S(2)}, u32[]{:S(2)}) collective-permute-start(bf16[256,2048]{1,0:T(8,128)(2,1)} %collective-permute-done.45.refs_0_), channel_id=1, source_target_pairs={{0,1},{1,2},{2,3},{3,0},{4,5},{5,6},{6,7},{7,4},{8,9},{9,10},{10,1... | collective-permute-start | bytes 3145736 | tf_op jit(solution)/shard_map/ppermute | solution.py:158
  330.1 34.9 %collective-permute-start.58 = (bf16[320,2048]{1,0:T(8,128)(2,1)}, bf16[320,2048]{1,0:T(8,128)(2,1)S(1)}, u32[]{:S(2)}, u32[]{:S(2)}) collective-permute-start(bf16[320,2048]{1,0:T(8,128)(2,1)} %copy-done.127), channel_id=1, source_target_pairs={{0,4},{4,0},{8,12},{12,8},{16,20},{20,16},{24,28},{28,24},{1,5},{5... | collective-permute-start | bytes 3932168 | tf_op jit(solution)/shard_map/ppermute | solution.py:51
  330.1 34.9 %collective-permute-start.59 = (bf16[320,2048]{1,0:T(8,128)(2,1)}, bf16[320,2048]{1,0:T(8,128)(2,1)S(1)}, u32[]{:S(2)}, u32[]{:S(2)}) collective-permute-start(bf16[320,2048]{1,0:T(8,128)(2,1)} %copy-done.128), channel_id=1, source_target_pairs={{0,4},{4,0},{8,12},{12,8},{16,20},{20,16},{24,28},{28,24},{1,5},{5... | collective-permute-start | bytes 3932168 | tf_op jit(solution)/shard_map/ppermute | solution.py:51
  492.4 41.3 %all-to-all-start.1 = ((bf16[8,64,2048]{2,1,0:T(8,128)(2,1)}), bf16[8,64,2048]{2,1,0:T(8,128)(2,1)}, u32[]{:S(2)}, u32[]{:S(2)}) async-start(bf16[8,64,2048]{2,1,0:T(8,128)(2,1)} %bitcast.164), calls=%async_computation.1 | async-start | bytes 4194304 | tf_op jit(solution)/shard_map/all_to_all | solution.py:1285
  497.0 48.2 %collective-permute-start.86 = (bf16[256,2048]{1,0:T(8,128)(2,1)}, bf16[256,2048]{1,0:T(8,128)(2,1)}, u32[]{:S(2)}, u32[]{:S(2)}) collective-permute-start(bf16[256,2048]{1,0:T(8,128)(2,1)} %copy-done.130), channel_id=1, source_target_pairs={{0,16},{4,20},{8,24},{12,28},{16,0},{20,4},{24,8},{28,12},{1,17},{... | collective-permute-start | bytes 3145736 | tf_op jit(solution)/shard_map/ppermute | solution.py:51
  499.0 46.2 %collective-permute-start.87 = (bf16[256,2048]{1,0:T(8,128)(2,1)}, bf16[256,2048]{1,0:T(8,128)(2,1)}, u32[]{:S(2)}, u32[]{:S(2)}) collective-permute-start(bf16[256,2048]{1,0:T(8,128)(2,1)} %copy-done.129), channel_id=1, source_target_pairs={{0,8},{4,12},{8,0},{12,4},{16,24},{20,28},{24,16},{28,20},{1,9},{5... | collective-permute-start | bytes 3145736 | tf_op jit(solution)/shard_map/ppermute | solution.py:51
  550.8 52.4 %collective-permute-start.88 = (bf16[512,2048]{1,0:T(8,128)(2,1)}, bf16[512,2048]{1,0:T(8,128)(2,1)}, u32[]{:S(2)}, u32[]{:S(2)}) collective-permute-start(bf16[512,2048]{1,0:T(8,128)(2,1)} %get-tuple-element.467), channel_id=1, source_target_pairs={{0,8},{4,12},{8,0},{12,4},{16,24},{20,28},{24,16},{28,20},{1,9},{5... | collective-permute-start | bytes 6291464 | tf_op jit(solution)/shard_map/ppermute | solution.py:51
  552.2 51.0 %collective-permute-start.89 = (bf16[512,2048]{1,0:T(8,128)(2,1)}, bf16[512,2048]{1,0:T(8,128)(2,1)}, u32[]{:S(2)}, u32[]{:S(2)}) collective-permute-start(bf16[512,2048]{1,0:T(8,128)(2,1)} %get-tuple-element.468), channel_id=1, source_target_pairs={{0,16},{4,20},{8,24},{12,28},{16,0},{20,4},{24,8},{28,12},{1,17},{... | collective-permute-start | bytes 6291464 | tf_op jit(solution)/shard_map/ppermute | solution.py:51
  567.9 41.2 %collective-permute-start.92 = (bf16[512,2048]{1,0:T(8,128)(2,1)}, bf16[512,2048]{1,0:T(8,128)(2,1)}, u32[]{:S(2)}, u32[]{:S(2)}) collective-permute-start(bf16[512,2048]{1,0:T(8,128)(2,1)} %shard_map.339), channel_id=1, source_target_pairs={{0,4},{4,0},{8,12},{12,8},{16,20},{20,16},{24,28},{28,24},{1,5},{5... | collective-permute-start | bytes 6291464 | tf_op jit(solution)/shard_map/ppermute | solution.py:51
  616.8 25.1 %collective-permute-start.94 = (bf16[128,2048]{1,0:T(8,128)(2,1)}, bf16[128,2048]{1,0:T(8,128)(2,1)}, u32[]{:S(2)}, u32[]{:S(2)}) collective-permute-start(bf16[128,2048]{1,0:T(8,128)(2,1)} %get-tuple-element.553), channel_id=1, source_target_pairs={{0,1},{1,2},{2,3},{3,0},{4,5},{5,6},{6,7},{7,4},{8,9},{9,10},{10,1... | collective-permute-start | bytes 1572872 | tf_op jit(solution)/shard_map/ppermute | solution.py:158
  636.5 42.7 %collective-permute-start.112 = (bf16[512,768]{1,0:T(8,128)(2,1)S(1)}, bf16[512,768]{1,0:T(8,128)(2,1)}, u32[]{:S(2)}, u32[]{:S(2)}) collective-permute-start(bf16[512,768]{1,0:T(8,128)(2,1)S(1)} %shard_map.344.refs_0_), channel_id=1, source_target_pairs={{0,4},{4,0},{8,12},{12,8},{16,20},{20,16},{24,28},{28,24},{1,5},{5... | collective-permute-start | bytes 2359304 | tf_op jit(solution)/shard_map/ppermute | solution.py:51
  660.4 24.6 %collective-permute-start.106 = (bf16[128,2048]{1,0:T(8,128)(2,1)}, bf16[128,2048]{1,0:T(8,128)(2,1)S(1)}, u32[]{:S(2)}, u32[]{:S(2)}) collective-permute-start(bf16[128,2048]{1,0:T(8,128)(2,1)} %shard_map.348), channel_id=1, source_target_pairs={{0,1},{1,2},{2,3},{3,0},{4,5},{5,6},{6,7},{7,4},{8,9},{9,10},{10,1... | collective-permute-start | bytes 1572872 | tf_op jit(solution)/shard_map/ppermute | solution.py:158
  662.0 31.6 %collective-permute-start.113 = (bf16[512,768]{1,0:T(8,128)(2,1)}, bf16[512,768]{1,0:T(8,128)(2,1)}, u32[]{:S(2)}, u32[]{:S(2)}) collective-permute-start(bf16[512,768]{1,0:T(8,128)(2,1)} %collective-permute-done.98.refs_1_), channel_id=1, source_target_pairs={{0,4},{4,0},{8,12},{12,8},{16,20},{20,16},{24,28},{28,24},{1,5},{5... | collective-permute-start | bytes 2359304 | tf_op jit(solution)/shard_map/ppermute | solution.py:51
  668.6 24.5 %collective-permute-start.116 = (bf16[256,768]{1,0:T(8,128)(2,1)}, bf16[256,768]{1,0:T(8,128)(2,1)}, u32[]{:S(2)}, u32[]{:S(2)}) collective-permute-start(bf16[256,768]{1,0:T(8,128)(2,1)} %collective-permute-done.111.refs_4_), channel_id=1, source_target_pairs={{0,4},{4,0},{8,12},{12,8},{16,20},{20,16},{24,28},{28,24},{1,5},{5... | collective-permute-start | bytes 1179656 | tf_op jit(solution)/shard_map/ppermute | solution.py:51
  (318 other events, 3298.1 us)

commit v6 on v5

--- a/solution.py
+++ b/solution.py
@@ -1052,7 +1052,7 @@
     later_tables = []
     out_project = lambda rows, kind: low_matmul(rows, out_weight).astype(kind)
     if dense:
-        attn_rows = after(attn_rows, cot_next[:2])
+        attn_rows = after(attn_rows, cot_next[0])
         out_project = lambda rows, kind: product(
             [rows], [out_weight], ((1,), (0,)), (rows.shape[0], model_width), kind
         )
@@ -1063,7 +1063,7 @@
             later_tables.extend(tables(rows))
             return tuple(later_tables) + (cot_next[2],)
 
-        attn = plane_scatter(out_project, attn_rows, fill, (), (cot_next[3],))
+        attn = plane_scatter(out_project, attn_rows, fill, (cot_next[1],), (cot_next[3],))
     else:
         attn = plane_scatter(out_project, attn_rows)
     residual = inputs + attn

time: 750 us -> 753 us (level)
  waiting for transfers between devices: 234 us -> 257 us
    ppermute x31, waiting for transfers between devices: 106 us -> 117 us  [ring(): lax.ppermute(value, 'wt', [(i, (i + 1) % count) for i in range(count)])]
    ppermute x94, waiting for transfers between devices: 123 us -> 134 us  [swap(): return lax.ppermute(value, 'ctx', [(i, i ^ bit) for i in range(count)])]
    unnamed x429 -> x433, local copies, waits for them, and re-layouts: 51.5 us -> 48.1 us
  transfers between devices with their start and end apart: 130 -> 130, of which waited for: 63 -> 62; matrix products, arithmetic and copies ran while one was open for 13% -> 11% of each run, Pallas kernels for 27% -> 27%
where the time goes in v6:
time: 753 us; the launch traced here: 744 us
  waiting for transfers between devices  257 us (34%)
  Pallas kernels  223 us (30%)
  local copies, waits for them, and re-layouts  112 us (15%)
  starting transfers between devices  103 us (14%)
  other arithmetic  25.5 us (3%)
  between operations  19.7 us (3%)
    ppermute x94, waiting for transfers between devices, swap(): return lax.ppermute(value, 'ctx', [(i, i ^ bit) for i in range(count)])  134 us
    ppermute x31, waiting for transfers between devices, ring(): lax.ppermute(value, 'wt', [(i, (i + 1) % count) for i in range(count)])  117 us
    ppermute x94, starting transfers between devices, swap(): return lax.ppermute(value, 'ctx', [(i, i ^ bit) for i in range(count)])  75.3 us
    pallas_call x10, Pallas kernels, product(): pl.pallas_call(functools.partial(product_kernel, dims, None, len(lefts),...  59.4 us
    pallas_call x4, Pallas kernels, expert_rows(): pl.pallas_call(expert_kernel, out_shape=(low(width), low(width), low(ff),...  48.4 us
    unnamed x433, local copies, waits for them, and re-layouts  48.1 us
    pallas_call x1, Pallas kernels, local(): pl.pallas_call(functools.partial(attend_back_kernel, heads, piece_count),...  30.8 us
    pallas_call x1, Pallas kernels, local(): pl.pallas_call(functools.partial(attend_kernel, heads, piece_count), out_...  19.3 us
  transfers between devices with their start and end apart: 130, of which 62 were waited for; matrix products, arithmetic and copies ran while one was open for 11% of the time, Pallas kernels for 27%

profile of v6, /device:TPU:0, one launch (start us, length us, event | category | flops | bytes accessed | tf_op | source)
XLA Modules:
  0.0 744.5 jit_solution(1493985650104722808)
XLA Ops:
  14.6 10.2 %collective-permute-done.1.refs_2_ = bf16[128,2048]{1,0:T(8,128)(2,1)S(1)} collective-permute-done((bf16[128,2048]{1,0:T(8,128)(2,1)S(1)}, bf16[128,2048]{1,0:T(8,128)(2,1)S(1)}, u32[]{:S(2)}, u32[]{:S(2)}) %collective-permute-start.1) | collective-permute-done | bytes 524320 | tf_op jit(solution)/shard_map/ppermute | solution.py:51
  42.0 6.6 collective-permute-done.10
  69.9 13.8 %collective-permute-done.16 = bf16[512,768]{1,0:T(8,128)(2,1)} collective-permute-done((bf16[512,768]{1,0:T(8,128)(2,1)}, bf16[512,768]{1,0:T(8,128)(2,1)}, u32[]{:S(2)}, u32[]{:S(2)}) %collective-permute-start.16) | collective-permute-done | bytes 786464 | tf_op jit(solution)/shard_map/ppermute | solution.py:158
  102.8 12.8 %collective-permute-done.21 = bf16[512,768]{1,0:T(8,128)(2,1)S(1)} collective-permute-done((bf16[512,768]{1,0:T(8,128)(2,1)}, bf16[512,768]{1,0:T(8,128)(2,1)S(1)}, u32[]{:S(2)}, u32[]{:S(2)}) %collective-permute-start.21) | collective-permute-done | bytes 786464 | tf_op jit(solution)/shard_map/ppermute | solution.py:158
  127.4 19.3 %shard_map.306 = (bf16[1024,512]{1,0:T(8,128)(2,1)}, bf16[1024,128]{1,0:T(8,128)(2,1)}, bf16[1024,128]{1,0:T(8,128)(2,1)}, f32[1024,640]{1,0:T(8,128)}, bf16[16,64,512]{2,1,0:T(8,128)(2,1)}) custom-call(s32[16]{0:T(128)} %copy-done.201, s32[16]{0:T(128)} %select_reduce_fusion.place_ref, s32[8]{0:T(128)} %convert_reduce_fusion.2.first_ref, ...), custom_call_target="tpu_custom_call" | custom-call | flops 1 | bytes 1 | tf_op jit(solution)/shard_map/pallas_call | solution.py:1024
  164.1 7.2 collective-permute-done.27.refs_6_
  194.7 9.0 %collective-permute-done.32 = bf16[128,2048]{1,0:T(8,128)(2,1)S(1)} collective-permute-done((bf16[128,2048]{1,0:T(8,128)(2,1)S(1)}, bf16[128,2048]{1,0:T(8,128)(2,1)S(1)}, u32[]{:S(2)}, u32[]{:S(2)}) %collective-permute-start.32) | collective-permute-done | bytes 524320 | tf_op jit(solution)/shard_map/ppermute | solution.py:51
  208.4 9.1 %collective-permute-done.36.refs_2_ = bf16[128,2048]{1,0:T(8,128)(2,1)S(1)} collective-permute-done((bf16[128,2048]{1,0:T(8,128)(2,1)S(1)}, bf16[128,2048]{1,0:T(8,128)(2,1)S(1)}, u32[]{:S(2)}, u32[]{:S(2)}) %collective-permute-start.36) | collective-permute-done | bytes 524320 | tf_op jit(solution)/shard_map/ppermute | solution.py:51
  246.4 6.7 collective-permute-done.44.refs_4_
  266.0 12.0 %shard_map.312 = (bf16[320,2048]{1,0:T(8,128)(2,1)S(1)}, bf16[320,2048]{1,0:T(8,128)(2,1)S(1)}, bf16[320,768]{1,0:T(8,128)(2,1)S(1)}, bf16[320,768]{1,0:T(8,128)...) custom-call(s32[1]{0:T(128)} %bitcast.29.expert_ref, ...), custom_call_target="tpu_custom_call" | custom-call | flops 1 | bytes 1 | tf_op jit(solution)/shard_map/pallas_call | solution.py:655
  301.7 12.0 %shard_map.314 = (bf16[320,2048]{1,0:T(8,128)(2,1)S(1)}, bf16[320,2048]{1,0:T(8,128)(2,1)S(1)}, bf16[320,768]{1,0:T(8,128)(2,1)S(1)}, bf16[320,768]{1,0:T(8,128)...) custom-call(s32[1]{0:T(128)} %bitcast.29.expert_ref, ...), custom_call_target="tpu_custom_call" | custom-call | flops 1 | bytes 1 | tf_op jit(solution)/shard_map/pallas_call | solution.py:655
  332.3 12.9 %collective-permute-done.56.refs_4_ = bf16[128,2048]{1,0:T(8,128)(2,1)} collective-permute-done((bf16[128,2048]{1,0:T(8,128)(2,1)}, bf16[128,2048]{1,0:T(8,128)(2,1)}, u32[]{:S(2)}, u32[]{:S(2)}) %collective-permute-start.56) | collective-permute-done | bytes 524320 | tf_op jit(solution)/shard_map/ppermute | solution.py:51
  346.8 12.3 %shard_map.316 = (bf16[320,2048]{1,0:T(8,128)(2,1)S(1)}, bf16[320,2048]{1,0:T(8,128)(2,1)S(1)}, bf16[320,768]{1,0:T(8,128)(2,1)S(1)}, bf16[320,768]{1,0:T(8,128)...) custom-call(s32[1]{0:T(128)} %bitcast.29.expert_ref, ...), custom_call_target="tpu_custom_call" | custom-call | flops 1 | bytes 1 | tf_op jit(solution)/shard_map/pallas_call | solution.py:655
  382.1 12.1 %shard_map.319 = (bf16[320,2048]{1,0:T(8,128)(2,1)S(1)}, bf16[320,2048]{1,0:T(8,128)(2,1)S(1)}, bf16[320,768]{1,0:T(8,128)(2,1)S(1)}, bf16[320,768]{1,0:T(8,128)...) custom-call(s32[1]{0:T(128)} %bitcast.29.expert_ref, ...), custom_call_target="tpu_custom_call" | custom-call | flops 1 | bytes 1 | tf_op jit(solution)/shard_map/pallas_call | solution.py:655
  410.0 7.9 %shard_map.323 = f32[2048,768]{1,0:T(8,128)} custom-call(s32[1]{0:T(128)} %constant.73.clone.1.start_ref, bf16[320,2048]{1,0:T(8,128)(2,1)S(1)} %copy-done.7, bf16[320,2048]{1,0:T(8,128)(2,1)} %collective-permute-done.42.other_ref.refs_1_, bf16[320,2048]{1,0:T(8,128)(2,1)S(1)} %copy-done.10, bf16[320,2048]{1,0:T(8,128)(2,1)} %collective-permute-done.48.other_ref.refs_3_, ...), custom_call_target="tpu_custom_call" | custom-call | flops 1 | bytes 1 | tf_op jit(solution)/shard_map/pallas_call | solution.py:836
  420.7 8.0 %shard_map.325 = f32[2048,768]{1,0:T(8,128)} custom-call(s32[1]{0:T(128)} %constant.73.clone.1.start_ref, bf16[320,2048]{1,0:T(8,128)(2,1)S(1)} %copy-done.7, bf16[320,2048]{1,0:T(8,128)(2,1)} %collective-permute-done.42.other_ref.refs_1_, bf16[320,2048]{1,0:T(8,128)(2,1)S(1)} %copy-done.10, bf16[320,2048]{1,0:T(8,128)(2,1)} %collective-permute-done.48.other_ref.refs_3_, ...), custom_call_target="tpu_custom_call" | custom-call | flops 1 | bytes 1 | tf_op jit(solution)/shard_map/pallas_call | solution.py:836
  468.2 8.7 %collective-permute-done.78.refs_3_.refs_2_ = bf16[128,2048]{1,0:T(8,128)(2,1)S(1)} collective-permute-done((bf16[128,2048]{1,0:T(8,128)(2,1)S(1)}, bf16[128,2048]{1,0:T(8,128)(2,1)S(1)}, u32[]{:S(2)}, u32[]{:S(2)}) %collective-permute-start.78) | collective-permute-done | bytes 524320 | tf_op jit(solution)/shard_map/ppermute | solution.py:51
  503.1 30.8 %shard_map.334 = (bf16[16,64,768]{2,1,0:T(8,128)(2,1)}, f32[1,128]{1,0:T(1,128)}, f32[1,128]{1,0:T(1,128)}) custom-call(s32[16]{0:T(128)} %select_reduce_fusion.place_ref, s32[8]{0:T(128)} %convert_reduce_fusion.2.first_ref, bf16[128,2048]{1,0:T(8,128)(2,1)} %copy-done.145, bf16[128,2048]{1,0:T(8,128)(2,1)} %copy-done.148, bf16[128,2048]{1,0:T(8,128)(2,1)} %copy-done.147, ...), custom_call_target="tpu_custom_call" | custom-call | flops 1 | bytes 1 | tf_op jit(solution)/shard_map/pallas_call | solution.py:1288
  555.5 6.5 shard_map.337
  575.1 16.6 %collective-permute-done.91.refs_0_ = bf16[512,768]{1,0:T(8,128)(2,1)} collective-permute-done((bf16[512,768]{1,0:T(8,128)(2,1)S(1)}, bf16[512,768]{1,0:T(8,128)(2,1)}, u32[]{:S(2)}, u32[]{:S(2)}) %collective-permute-start.91) | collective-permute-done | bytes 786464 | tf_op jit(solution)/shard_map/ppermute | solution.py:158
  625.8 11.9 %collective-permute-done.99.refs_2_ = bf16[512,768]{1,0:T(8,128)(2,1)} collective-permute-done((bf16[512,768]{1,0:T(8,128)(2,1)S(1)}, bf16[512,768]{1,0:T(8,128)(2,1)}, u32[]{:S(2)}, u32[]{:S(2)}) %collective-permute-start.99) | collective-permute-done | bytes 786464 | tf_op jit(solution)/shard_map/ppermute | solution.py:51
  651.8 8.9 %collective-permute-done.101.refs_0_ = bf16[128,2048]{1,0:T(8,128)(2,1)S(1)} collective-permute-done((bf16[128,2048]{1,0:T(8,128)(2,1)S(1)}, bf16[128,2048]{1,0:T(8,128)(2,1)S(1)}, u32[]{:S(2)}, u32[]{:S(2)}) %collective-permute-start.101) | collective-permute-done | bytes 524320 | tf_op jit(solution)/shard_map/ppermute | solution.py:158
  670.6 8.1 %collective-permute-done.100.refs_0_ = bf16[128,2048]{1,0:T(8,128)(2,1)S(1)} collective-permute-done((bf16[128,2048]{1,0:T(8,128)(2,1)S(1)}, bf16[128,2048]{1,0:T(8,128)(2,1)S(1)}, u32[]{:S(2)}, u32[]{:S(2)}) %collective-permute-start.100) | collective-permute-done | bytes 524320 | tf_op jit(solution)/shard_map/ppermute | solution.py:158
  697.2 7.6 %shard_map.353 = (f32[512,4096]{1,0:T(8,128)}, f32[512,512]{1,0:T(8,128)}, f32[512,512]{1,0:T(8,128)}) custom-call(s32[8]{0:T(128)} %get-tuple-element.600.owner_ref, bf16[512,768]{1,0:T(8,128)(2,1)} %copy-done.35, bf16[512,768]{1,0:T(8,128)(2,1)} %collective-permute-done.98.refs_1_, bf16[512,768]{1,0:T(8,128)(2,1)} %collective-permute-done.99.refs_2_, ...), custom_call_target="tpu_custom_call" | custom-call | flops 1 | bytes 1 | tf_op jit(solution)/shard_map/pallas_call | solution.py:772
  (884 shorter events, 453.8 us)
Async XLA Ops:
  2.6 32.4 %collective-permute-start.9 = (bf16[128,2048]{1,0:T(8,128)(2,1)}, bf16[128,2048]{1,0:T(8,128)(2,1)}, u32[]{:S(2)}, u32[]{:S(2)}) collective-permute-start(bf16[128,2048]{1,0:T(8,128)(2,1)} %bitcast.5), channel_id=1, source_target_pairs={{0,1},{1,2},{2,3},{3,0},{4,5},{5,6},{6,7},{7,4},{8,9},{9,10},{10,1... | collective-permute-start | bytes 1572872 | tf_op jit(solution)/shard_map/ppermute | solution.py:158
  10.4 29.7 %collective-permute-start.4 = (bf16[128,2048]{1,0:T(8,128)(2,1)S(1)}, bf16[128,2048]{1,0:T(8,128)(2,1)}, u32[]{:S(2)}, u32[]{:S(2)}) collective-permute-start(bf16[128,2048]{1,0:T(8,128)(2,1)S(1)} %fusion.14.refs_0_), channel_id=1, source_target_pairs={{0,4},{4,0},{8,12},{12,8},{16,20},{20,16},{24,28},{28,24},{1,5},{5... | collective-permute-start | bytes 1572872 | tf_op jit(solution)/shard_map/ppermute | solution.py:51
  55.6 28.1 %collective-permute-start.16 = (bf16[512,768]{1,0:T(8,128)(2,1)}, bf16[512,768]{1,0:T(8,128)(2,1)}, u32[]{:S(2)}, u32[]{:S(2)}) collective-permute-start(bf16[512,768]{1,0:T(8,128)(2,1)} %collective-permute-done.10), channel_id=1, source_target_pairs={{0,1},{1,2},{2,3},{3,0},{4,5},{5,6},{6,7},{7,4},{8,9},{9,10},{10,1... | collective-permute-start | bytes 2359304 | tf_op jit(solution)/shard_map/ppermute | solution.py:158
  87.5 28.1 %collective-permute-start.21 = (bf16[512,768]{1,0:T(8,128)(2,1)}, bf16[512,768]{1,0:T(8,128)(2,1)S(1)}, u32[]{:S(2)}, u32[]{:S(2)}) collective-permute-start(bf16[512,768]{1,0:T(8,128)(2,1)} %collective-permute-done.16), channel_id=1, source_target_pairs={{0,1},{1,2},{2,3},{3,0},{4,5},{5,6},{6,7},{7,4},{8,9},{9,10},{10,1... | collective-permute-start | bytes 2359304 | tf_op jit(solution)/shard_map/ppermute | solution.py:158
  117.7 31.4 %all-to-all-start = ((bf16[8,64,2048]{2,1,0:T(8,128)(2,1)}), bf16[8,64,2048]{2,1,0:T(8,128)(2,1)}, u32[]{:S(2)}, u32[]{:S(2)}) async-start(bf16[8,64,2048]{2,1,0:T(8,128)(2,1)} %bitcast.163), calls=%async_computation | async-start | bytes 4194304 | tf_op jit(solution)/shard_map/all_to_all | solution.py:1005
  153.8 28.3 %collective-permute-start.30 = (bf16[192,128]{1,0:T(8,128)(2,1)S(1)}, bf16[192,128]{1,0:T(8,128)(2,1)S(1)}, u32[]{:S(2)}, u32[]{:S(2)}) collective-permute-start(bf16[192,128]{1,0:T(8,128)(2,1)S(1)} %copy-done.189), channel_id=1, source_target_pairs={{0,1},{1,2},{2,3},{3,0},{4,5},{5,6},{6,7},{7,4},{8,9},{9,10},{10,1... | collective-permute-start | bytes 147464 | tf_op jit(solution)/shard_map/ppermute | solution.py:158
  155.5 32.8 %collective-permute-start.31 = (bf16[128,2048]{1,0:T(8,128)(2,1)}, bf16[128,2048]{1,0:T(8,128)(2,1)}, u32[]{:S(2)}, u32[]{:S(2)}) collective-permute-start(bf16[128,2048]{1,0:T(8,128)(2,1)} %collective-permute-done.18.refs_7_), channel_id=1, source_target_pairs={{0,1},{1,2},{2,3},{3,0},{4,5},{5,6},{6,7},{7,4},{8,9},{9,10},{10,1... | collective-permute-start | bytes 1572872 | tf_op jit(solution)/shard_map/ppermute | solution.py:158
  159.7 35.0 %collective-permute-start.34 = (bf16[128,2048]{1,0:T(8,128)(2,1)}, bf16[128,2048]{1,0:T(8,128)(2,1)}, u32[]{:S(2)}, u32[]{:S(2)}) collective-permute-start(bf16[128,2048]{1,0:T(8,128)(2,1)} %copy-done.174), channel_id=1, source_target_pairs={{0,1},{1,2},{2,3},{3,0},{4,5},{5,6},{6,7},{7,4},{8,9},{9,10},{10,1... | collective-permute-start | bytes 1572872 | tf_op jit(solution)/shard_map/ppermute | solution.py:158
  221.4 25.0 %collective-permute-start.45 = (bf16[256,2048]{1,0:T(8,128)(2,1)S(1)}, bf16[256,2048]{1,0:T(8,128)(2,1)}, u32[]{:S(2)}, u32[]{:S(2)}) collective-permute-start(bf16[256,2048]{1,0:T(8,128)(2,1)S(1)} %pad_maximum_fusion), channel_id=1, source_target_pairs={{0,1},{1,2},{2,3},{3,0},{4,5},{5,6},{6,7},{7,4},{8,9},{9,10},{10,1... | collective-permute-start | bytes 3145736 | tf_op jit(solution)/shard_map/ppermute | solution.py:158
  254.8 24.8 %collective-permute-start.47 = (bf16[256,2048]{1,0:T(8,128)(2,1)}, bf16[256,2048]{1,0:T(8,128)(2,1)}, u32[]{:S(2)}, u32[]{:S(2)}) collective-permute-start(bf16[256,2048]{1,0:T(8,128)(2,1)} %collective-permute-done.45.refs_0_), channel_id=1, source_target_pairs={{0,16},{4,20},{8,24},{12,28},{16,0},{20,4},{24,8},{28,12},{1,17},{... | collective-permute-start | bytes 3145736 | tf_op jit(solution)/shard_map/ppermute | solution.py:51
  256.3 34.8 %collective-permute-start.51 = (bf16[256,2048]{1,0:T(8,128)(2,1)}, bf16[256,2048]{1,0:T(8,128)(2,1)}, u32[]{:S(2)}, u32[]{:S(2)}) collective-permute-start(bf16[256,2048]{1,0:T(8,128)(2,1)} %collective-permute-done.45.refs_0_), channel_id=1, source_target_pairs={{0,1},{1,2},{2,3},{3,0},{4,5},{5,6},{6,7},{7,4},{8,9},{9,10},{10,1... | collective-permute-start | bytes 3145736 | tf_op jit(solution)/shard_map/ppermute | solution.py:158
  331.8 35.0 %collective-permute-start.58 = (bf16[320,2048]{1,0:T(8,128)(2,1)}, bf16[320,2048]{1,0:T(8,128)(2,1)S(1)}, u32[]{:S(2)}, u32[]{:S(2)}) collective-permute-start(bf16[320,2048]{1,0:T(8,128)(2,1)} %copy-done.127), channel_id=1, source_target_pairs={{0,4},{4,0},{8,12},{12,8},{16,20},{20,16},{24,28},{28,24},{1,5},{5... | collective-permute-start | bytes 3932168 | tf_op jit(solution)/shard_map/ppermute | solution.py:51
  331.8 35.0 %collective-permute-start.59 = (bf16[320,2048]{1,0:T(8,128)(2,1)}, bf16[320,2048]{1,0:T(8,128)(2,1)S(1)}, u32[]{:S(2)}, u32[]{:S(2)}) collective-permute-start(bf16[320,2048]{1,0:T(8,128)(2,1)} %copy-done.128), channel_id=1, source_target_pairs={{0,4},{4,0},{8,12},{12,8},{16,20},{20,16},{24,28},{28,24},{1,5},{5... | collective-permute-start | bytes 3932168 | tf_op jit(solution)/shard_map/ppermute | solution.py:51
  495.0 38.8 %all-to-all-start.1 = ((bf16[8,64,2048]{2,1,0:T(8,128)(2,1)}), bf16[8,64,2048]{2,1,0:T(8,128)(2,1)}, u32[]{:S(2)}, u32[]{:S(2)}) async-start(bf16[8,64,2048]{2,1,0:T(8,128)(2,1)} %bitcast.164), calls=%async_computation.1 | async-start | bytes 4194304 | tf_op jit(solution)/shard_map/all_to_all | solution.py:1285
  499.6 48.2 %collective-permute-start.86 = (bf16[256,2048]{1,0:T(8,128)(2,1)}, bf16[256,2048]{1,0:T(8,128)(2,1)}, u32[]{:S(2)}, u32[]{:S(2)}) collective-permute-start(bf16[256,2048]{1,0:T(8,128)(2,1)} %copy-done.130), channel_id=1, source_target_pairs={{0,16},{4,20},{8,24},{12,28},{16,0},{20,4},{24,8},{28,12},{1,17},{... | collective-permute-start | bytes 3145736 | tf_op jit(solution)/shard_map/ppermute | solution.py:51
  501.6 46.2 %collective-permute-start.87 = (bf16[256,2048]{1,0:T(8,128)(2,1)}, bf16[256,2048]{1,0:T(8,128)(2,1)}, u32[]{:S(2)}, u32[]{:S(2)}) collective-permute-start(bf16[256,2048]{1,0:T(8,128)(2,1)} %copy-done.129), channel_id=1, source_target_pairs={{0,8},{4,12},{8,0},{12,4},{16,24},{20,28},{24,16},{28,20},{1,9},{5... | collective-permute-start | bytes 3145736 | tf_op jit(solution)/shard_map/ppermute | solution.py:51
  553.5 51.8 %collective-permute-start.88 = (bf16[512,2048]{1,0:T(8,128)(2,1)}, bf16[512,2048]{1,0:T(8,128)(2,1)}, u32[]{:S(2)}, u32[]{:S(2)}) collective-permute-start(bf16[512,2048]{1,0:T(8,128)(2,1)} %get-tuple-element.467), channel_id=1, source_target_pairs={{0,8},{4,12},{8,0},{12,4},{16,24},{20,28},{24,16},{28,20},{1,9},{5... | collective-permute-start | bytes 6291464 | tf_op jit(solution)/shard_map/ppermute | solution.py:51
  554.8 50.4 %collective-permute-start.89 = (bf16[512,2048]{1,0:T(8,128)(2,1)}, bf16[512,2048]{1,0:T(8,128)(2,1)}, u32[]{:S(2)}, u32[]{:S(2)}) collective-permute-start(bf16[512,2048]{1,0:T(8,128)(2,1)} %get-tuple-element.468), channel_id=1, source_target_pairs={{0,16},{4,20},{8,24},{12,28},{16,0},{20,4},{24,8},{28,12},{1,17},{... | collective-permute-start | bytes 6291464 | tf_op jit(solution)/shard_map/ppermute | solution.py:51
  569.8 41.4 %collective-permute-start.92 = (bf16[512,2048]{1,0:T(8,128)(2,1)}, bf16[512,2048]{1,0:T(8,128)(2,1)}, u32[]{:S(2)}, u32[]{:S(2)}) collective-permute-start(bf16[512,2048]{1,0:T(8,128)(2,1)} %shard_map.339), channel_id=1, source_target_pairs={{0,4},{4,0},{8,12},{12,8},{16,20},{20,16},{24,28},{28,24},{1,5},{5... | collective-permute-start | bytes 6291464 | tf_op jit(solution)/shard_map/ppermute | solution.py:51
  619.5 25.1 %collective-permute-start.94 = (bf16[128,2048]{1,0:T(8,128)(2,1)}, bf16[128,2048]{1,0:T(8,128)(2,1)}, u32[]{:S(2)}, u32[]{:S(2)}) collective-permute-start(bf16[128,2048]{1,0:T(8,128)(2,1)} %get-tuple-element.553), channel_id=1, source_target_pairs={{0,1},{1,2},{2,3},{3,0},{4,5},{5,6},{6,7},{7,4},{8,9},{9,10},{10,1... | collective-permute-start | bytes 1572872 | tf_op jit(solution)/shard_map/ppermute | solution.py:158
  639.1 42.9 %collective-permute-start.112 = (bf16[512,768]{1,0:T(8,128)(2,1)S(1)}, bf16[512,768]{1,0:T(8,128)(2,1)}, u32[]{:S(2)}, u32[]{:S(2)}) collective-permute-start(bf16[512,768]{1,0:T(8,128)(2,1)S(1)} %shard_map.344.refs_0_), channel_id=1, source_target_pairs={{0,4},{4,0},{8,12},{12,8},{16,20},{20,16},{24,28},{28,24},{1,5},{5... | collective-permute-start | bytes 2359304 | tf_op jit(solution)/shard_map/ppermute | solution.py:51
  663.1 24.7 %collective-permute-start.106 = (bf16[128,2048]{1,0:T(8,128)(2,1)}, bf16[128,2048]{1,0:T(8,128)(2,1)S(1)}, u32[]{:S(2)}, u32[]{:S(2)}) collective-permute-start(bf16[128,2048]{1,0:T(8,128)(2,1)} %shard_map.348), channel_id=1, source_target_pairs={{0,1},{1,2},{2,3},{3,0},{4,5},{5,6},{6,7},{7,4},{8,9},{9,10},{10,1... | collective-permute-start | bytes 1572872 | tf_op jit(solution)/shard_map/ppermute | solution.py:158
  664.6 32.5 %collective-permute-start.113 = (bf16[512,768]{1,0:T(8,128)(2,1)}, bf16[512,768]{1,0:T(8,128)(2,1)}, u32[]{:S(2)}, u32[]{:S(2)}) collective-permute-start(bf16[512,768]{1,0:T(8,128)(2,1)} %collective-permute-done.98.refs_1_), channel_id=1, source_target_pairs={{0,4},{4,0},{8,12},{12,8},{16,20},{20,16},{24,28},{28,24},{1,5},{5... | collective-permute-start | bytes 2359304 | tf_op jit(solution)/shard_map/ppermute | solution.py:51
  670.6 24.5 %collective-permute-start.116 = (bf16[256,768]{1,0:T(8,128)(2,1)}, bf16[256,768]{1,0:T(8,128)(2,1)}, u32[]{:S(2)}, u32[]{:S(2)}) collective-permute-start(bf16[256,768]{1,0:T(8,128)(2,1)} %collective-permute-done.111.refs_4_), channel_id=1, source_target_pairs={{0,4},{4,0},{8,12},{12,8},{16,20},{20,16},{24,28},{28,24},{1,5},{5... | collective-permute-start | bytes 1179656 | tf_op jit(solution)/shard_map/ppermute | solution.py:51
  (320 other events, 3459.2 us)
